TPU v7x, 32 devices: a whole 2x2x4 slice. The times are simulated.
32 devices in a mesh: energy: 4 (over z), wire: 8 (over y, x, core).
Axes of the slice: x: 2, y: 2, z: 4, core: 2. Of those that a mesh axis runs over, the one named last changes fastest.
Arguments:
- g_prev: bfloat16 [2, 8, 8, 512, 512], P(None, 'energy', 'wire'), may hold values from -0.25 to 0.25
- local_green: bfloat16 [2, 8, 8, 512, 512], P(None, 'energy', 'wire'), may hold values from -0.09375 to 0.09375
- prop: bfloat16 [2, 8, 8, 512, 512], P(None, 'energy', 'wire'), may hold values from -1.5 to 1.5
- incoming: bfloat16 [2, 8, 8, 64, 512], P(None, 'energy', 'wire'), may hold values from -3 to 3
- plus_partner: int32 [8], replicated, may hold values from -1 to 7
- minus_partner: int32 [8], replicated, may hold values from -1 to 7
- counts: int32 [4], P('energy'), may hold values from 1 to 2
- pot_index: int32 [8], P('wire'), may hold values from 0 to 15
- levels: float32 [16], replicated, may hold values from -1 to 1
- coupling: float32 [2], replicated, may hold values from 0.5 to 2
Outputs:
- scattered: bfloat16 [2, 8, 8, 64, 512], P(None, 'energy', 'wire')
- green_next: bfloat16 [2, 8, 8, 512, 512], P(None, 'energy', 'wire')
Inputs may be any that keep to these rules, and one draw needn't show every extreme that they name: `plus_partner`: -1 means that the partner energy lies outside the window. `minus_partner`: -1 means that the partner energy lies outside the window. The first counts[g] of the 2 slots of group g are live.
All inputs are finite; a program needn't handle non-finite values.
Results may differ from a plain program's by a relative error of at most 0.035.
Values may be sent and summed in bfloat16 or wider, within the bound.
No kernel may reach another device: no remote copies, remote signals or barrier semaphores. Data moves between devices by JAX's collectives and lax.ppermute only.
A program may use at most 192 MiB of HBM per device.

v0:
```python
import jax
import jax.numpy as jnp
from jax import lax
from jax.sharding import PartitionSpec as P


def entering(value, axis, join, neutral):
    count, mine = (lax.axis_size(axis), lax.axis_index(axis))
    pieces = jax.tree.map(lambda part: lax.all_gather(part, axis), value)
    subtotal = jax.tree.map(
        lambda part, zero: jnp.full_like(part, 0) + jnp.asarray(zero, part.dtype), value, neutral
    )

    def step(position, subtotal):
        longer = join(subtotal, jax.tree.map(lambda part: part[position], pieces))
        return jax.tree.map(lambda new, old: jnp.where(position < mine, new, old), longer, subtotal)

    return lax.fori_loop(0, count - 1, step, subtotal)


def complex_product(first_op, second_op):

    def multiply(lhs_part, rhs_part):
        return jnp.einsum("sij,sjk->sik", lhs_part, rhs_part, preferred_element_type=jnp.float32)

    real_part = multiply(first_op[0], second_op[0]) - multiply(first_op[1], second_op[1])
    imag_part = multiply(first_op[0], second_op[1]) + multiply(first_op[1], second_op[0])
    return jnp.stack([real_part, imag_part])


def intersection(first_op, second_op):
    return jnp.einsum("smi,smj->sij", first_op, second_op, preferred_element_type=jnp.float32)


def shards(
    g_prev,
    local_green,
    prop,
    incoming,
    plus_partner,
    minus_partner,
    counts,
    pot_index,
    levels,
    coupling,
):
    slot_count = g_prev.shape[1]
    orbitals = g_prev.shape[3]
    mode_count = incoming.shape[3]
    group_index = lax.axis_index("energy")
    plus_own = lax.dynamic_slice_in_dim(plus_partner, group_index * slot_count, slot_count)
    minus_own = lax.dynamic_slice_in_dim(minus_partner, group_index * slot_count, slot_count)
    incident = incoming[:, :, 0]
    green_here = local_green[:, :, 0]
    steps_here = prop[:, :, 0]
    shard_piece = lax.all_gather(g_prev, "energy", axis=1, tiled=True)
    global_index = jnp.arange(shard_piece.shape[1], dtype=jnp.int32)
    slab_piece = shard_piece[:, :, 0]
    plus_select = (plus_own[:, None] == global_index[None, :]).astype(jnp.bfloat16)
    minus_select = (minus_own[:, None] == global_index[None, :]).astype(jnp.bfloat16)

    def select_rows(selector):
        return jnp.einsum(
            "sk,rkab->rsab", selector, slab_piece, preferred_element_type=jnp.float32
        ).astype(jnp.bfloat16)

    upper_block = select_rows(plus_select)
    lower_block = select_rows(minus_select)
    shifted = coupling[0] * complex_product(incident, upper_block) + coupling[1] * complex_product(
        incident, lower_block
    )
    level_hit = pot_index[0] == jnp.arange(levels.shape[0], dtype=jnp.int32)
    potential = jnp.sum(jnp.where(level_hit, levels, jnp.float32(0.0)))
    source_term = (shifted + potential * incident.astype(jnp.float32)).astype(jnp.bfloat16)
    source = complex_product(source_term, green_here)
    identity = jnp.broadcast_to(
        jnp.eye(orbitals, dtype=jnp.bfloat16), (slot_count, orbitals, orbitals)
    )
    identity_map = jnp.stack([identity, jnp.zeros_like(identity)])
    zero_wave = jnp.zeros((2, slot_count, mode_count, orbitals), jnp.bfloat16)

    def compose(earlier, later):
        step_block = complex_product(earlier[0], later[0]).astype(jnp.bfloat16)
        offset_wave = (complex_product(earlier[1], later[0]) + later[1].astype(jnp.float32)).astype(
            jnp.bfloat16
        )
        return (step_block, offset_wave)

    preceding = entering(
        (steps_here, source.astype(jnp.bfloat16)), "wire", compose, (identity_map, zero_wave)
    )
    chained = (complex_product(preceding[1], steps_here) + source).astype(jnp.bfloat16)
    combined = (incident.astype(jnp.float32) + chained.astype(jnp.float32)).astype(jnp.bfloat16)
    green_real = (
        intersection(combined[1], combined[0]) - intersection(combined[0], combined[1])
    ) / mode_count
    green_imag = (
        intersection(combined[0], combined[0]) + intersection(combined[1], combined[1])
    ) / mode_count
    live_mask = (jnp.arange(slot_count, dtype=jnp.int32) < counts[0])[None, :, None, None]
    scattered = jnp.where(live_mask, chained, jnp.zeros_like(chained))[:, :, None]
    green_block = jnp.stack([green_real, green_imag])
    green_next = jnp.where(live_mask, green_block, jnp.zeros_like(green_block)).astype(
        jnp.bfloat16
    )[:, :, None]
    return (scattered, green_next)


def solution(mesh):
    placed = (
        P(None, "energy", "wire", None, None),
        P(None, "energy", "wire", None, None),
        P(None, "energy", "wire", None, None),
        P(None, "energy", "wire", None, None),
        P(),
        P(),
        P("energy"),
        P("wire"),
        P(),
        P(),
    )
    return jax.shard_map(
        shards,
        mesh=mesh,
        in_specs=placed,
        out_specs=(P(None, "energy", "wire", None, None), P(None, "energy", "wire", None, None)),
        check_vma=False,
    )
```

profile of v0, /device:TPU:1, one launch (start us, length us, event | category | flops | bytes accessed | tf_op | source)
XLA Modules:
  0.0 369.5 jit_solution(1472527370898223248)
XLA Ops:
  7.2 3.0 copy.30
  10.3 0.6 copy-done.8
  11.7 0.6 fusion.77
  12.3 0.7 fusion.74
  13.0 149.4 %all-gather.5.cloned.1.call-done = bf16[2,8,1,512,512]{4,3,2,0,1:T(8,128)(2,1)} async-done(((bf16[2,2,1,512,512]{4,3,2,0,1:T(8,128)(2,1)}), bf16[2,8,1,512,512]{4,3,2,0,1:T(8,128)(2,1)}) %all-gather.5.cloned.1.call-update) | async-done | bytes 8388624 | tf_op jit(solution)/shard_map/all_gather | solution.py:56
  162.4 9.0 %fusion.23 = bf16[2,2,512,512]{3,1,2,0:T(2,128)(2,1)S(1)} fusion(bf16[2,8,1,512,512]{4,3,2,0,1:T(8,128)(2,1)} %all-gather.5.cloned.1.call-done, s32[2]{0:T(128)S(1)} %dynamic_slice.21), kind=kOutput, calls=%fused_computation.28 | convolution fusion | flops 17825808 | bytes 10485768 | tf_op jit(solution)/shard_map/sk,rkab->rsab/dot_general | solution.py:63
  171.4 1.7 slice_bitcast_fusion.11
  173.7 0.3 fusion.31
  174.0 0.3 fusion.30
  174.4 5.2 %fusion.26 = bf16[2,2,512,512]{3,1,2,0:T(2,128)(2,1)S(1)} fusion(bf16[2,8,1,512,512]{4,3,2,0,1:T(8,128)(2,1)S(1)} %bitcast.196, s32[2]{0:T(128)S(1)} %dynamic_slice.20), kind=kOutput, calls=%fused_computation.29 | convolution fusion | flops 17825808 | bytes 10485768 | tf_op jit(solution)/shard_map/sk,rkab->rsab/dot_general | solution.py:63
  179.5 1.5 slice_bitcast_fusion.13
  181.0 0.3 fusion.47
  181.3 0.3 fusion.45
  181.7 0.3 fusion.33
  182.0 0.3 fusion.32
  182.3 2.1 fusion.51
  185.6 0.4 copy-done.3
  186.1 0.7 copy-done.5
  186.7 0.7 pad_maximum_fusion
  187.5 0.7 all-gather.9.cloned.1.call-update
  188.9 25.1 %all-gather.7.cloned.1.call-done = bf16[8,2,2,64,512]{4,3,2,1,0:T(8,128)(2,1)} async-done(((bf16[1,2,2,64,512]{4,3,2,1,0:T(8,128)(2,1)}), bf16[8,2,2,64,512]{4,3,2,1,0:T(8,128)(2,1)}) %all-gather.7.cloned.1.call-update) | async-done | bytes 2097168 | tf_op jit(solution)/shard_map/all_gather | solution.py:9
  214.0 91.8 %all-gather.9.cloned.1.call-done = bf16[16,2,1,512,512]{4,3,2,1,0:T(8,128)(2,1)} async-done(((bf16[2,2,1,512,512]{4,3,2,1,0:T(8,128)(2,1)}), bf16[16,2,1,512,512]{4,3,2,1,0:T(8,128)(2,1)}) %all-gather.9.cloned.1.call-update) | async-done | bytes 16777232 | tf_op jit(solution)/shard_map/all_gather | solution.py:9
  305.8 51.0 %while.14 = (s32[]{:T(128)}, bf16[2,2,64,512]{3,2,1,0:T(8,128)(2,1)S(1)}, s32[]{:T(128)}, bf16[8,2,2,512,512]{4,3,2,1,0:T(8,128)(2,1)}, bf16[8,2,2,64,512]{4,3,2,1,0:T(8,128)(2,1)}, /*index=5*/s32[]{:T(128)}, s32[]{:T(128)}, s32[]{}) while((s32[]{:T(128)}, bf16[2,2,64,512]{3,2,1,0:T(8,128)(2,1)S(1)}, s32[]{:T(128)}, ...), condition=%wide.region_2.3_spmd.clone, body=%wide.region_1.2_spmd.clone.sunk | while | flops 269484032 | bytes 8128642 | solution.py:18
  305.8 1.7 fusion.85
  307.5 1.5 fusion.86
  309.0 1.5 fusion.83
  310.5 1.5 fusion.84
  312.1 1.1 fusion.87
  313.2 1.5 fusion.85
  314.7 1.5 fusion.86
  316.3 1.5 fusion.83
  317.8 1.5 fusion.84
  319.3 1.1 fusion.87
  320.5 1.5 fusion.85
  322.0 1.5 fusion.86
  323.5 1.5 fusion.83
  325.1 1.5 fusion.84
  326.6 1.1 fusion.87
  327.7 1.5 fusion.85
  329.3 1.5 fusion.86
  330.8 1.5 fusion.83
  332.3 1.5 fusion.84
  333.9 1.1 fusion.87
  335.0 1.5 fusion.85
  336.5 1.5 fusion.86
  338.1 1.5 fusion.83
  339.6 1.5 fusion.84
  341.1 1.1 fusion.87
  342.3 1.5 fusion.85
  343.8 1.5 fusion.86
  345.3 1.5 fusion.83
  346.8 1.5 fusion.84
  348.4 1.1 fusion.87
  349.5 1.5 fusion.85
  351.0 1.5 fusion.86
  352.6 1.5 fusion.83
  354.1 1.5 fusion.84
  355.6 1.1 fusion.87
  358.2 0.5 fusion.66
  358.7 0.5 fusion.67
  359.2 0.5 multiply_bitcast_fusion.1
  359.7 0.5 multiply_bitcast_fusion
  360.2 2.0 fusion.29
  362.1 0.8 fusion.57
  (52 shorter events, 3.8 us)
Async XLA Ops:
  7.2 155.2 %all-gather.5.cloned.1.call-start = ((), (), s32[]{:S(2)}) async-start(), calls=%async_computation | async-start | bytes 10485760 | tf_op jit(solution)/shard_map/all_gather | solution.py:56
  10.3 0.7 copy-start.8
  10.3 0.7 copy-start.9
  10.3 1.5 copy-start.7
  10.3 2.1 copy-start.10
  10.3 203.7 %all-gather.7.cloned.1.call-start = ((), (), s32[]{:S(2)}) async-start(), calls=%async_computation.1 | async-start | bytes 2359296 | tf_op jit(solution)/shard_map/all_gather | solution.py:9
  162.4 10.7 %copy-start.1 = (bf16[2,2,1,64,512]{4,3,2,1,0:T(8,128)(2,1)S(1)}, bf16[2,2,1,64,512]{4,3,2,1,0:T(8,128)(2,1)}, u32[]{:S(2)}) copy-start(bf16[2,2,1,64,512]{4,3,2,1,0:T(8,128)(2,1)} %param.15) | copy-start | bytes 786436
  162.4 12.0 %slice-start = ((s8[8388608]{0:T(1024)(128)(4,1)}), s8[4194304]{0:T(1024)(128)(4,1)S(1)}, s32[]{:S(2)}) async-start(s8[8388608]{0:T(1024)(128)(4,1)} %bitcast.195), calls=%async_computation.3 | async-start | bytes 8388608
  171.4 2.9 slice-start.1
  181.7 2.8 copy-start.2
  185.3 0.7 copy-start.3
  186.0 0.7 copy-start.5
  187.5 118.3 %all-gather.9.cloned.1.call-start = ((), (), s32[]{:S(2)}) async-start(), calls=%async_computation.2 | async-start | bytes 18874368 | tf_op jit(solution)/shard_map/all_gather | solution.py:9
  305.8 51.0 %copy-start = (bf16[2,2,1,512,512]{4,3,2,1,0:T(8,128)(2,1)S(1)}, bf16[2,2,1,512,512]{4,3,2,1,0:T(8,128)(2,1)}, u32[]{:S(2)}) copy-start(bf16[2,2,1,512,512]{4,3,2,1,0:T(8,128)(2,1)} %param.14) | copy-start | bytes 6291460
  357.1 1.0 copy-start.4
  357.1 1.0 copy-start.6
Sparse Core Ops, SparseCore 0:
  10.4 151.9 all-gather.4
  187.6 26.3 all-gather.6
  215.9 89.8 all-gather.8
where the time goes:
time: 371 us; the launch traced here: 369 us
  waiting for transfers between devices  267 us (72%)
  matrix products  63.7 us (17%)
  between operations  15.3 us (4%)
  other arithmetic  14.3 us (4%)
  local copies, waits for them, and re-layouts  8.73 us (2%)
    all_gather x1, waiting for transfers between devices, shards(): shard_piece = lax.all_gather(g_prev, 'energy', axis=1, tiled=True)  149 us
    all_gather x2, waiting for transfers between devices, entering(): pieces = jax.tree.map(lambda part: lax.all_gather(part, axis), value)  117 us
    dot_general x44, matrix products, multiply(): jnp.einsum('sij,sjk->sik', lhs_part, rhs_part, preferred_element_type=jnp...  47.6 us
    dot_general x2, matrix products, select_rows(): jnp.einsum('sk,rkab->rsab', selector, slab_piece, preferred_element_type=...  14.2 us
    select_n x7, other arithmetic, step(): jnp.where(position < mine, new, old)  7.62 us
  transfers between devices with their start and end apart: 3, of which 3 were waited for; matrix products, arithmetic and copies ran while one was open for 0% of the time, Pallas kernels for 0%

commit v1 on v0

v1 whole, which is shorter than its diff:
```python
import functools

import jax
import jax.numpy as jnp
from jax import lax
from jax.experimental import pallas as pl
from jax.experimental.pallas import tpu as pltpu
from jax.sharding import PartitionSpec as P

VMEM = pl.BlockSpec(memory_space=pltpu.VMEM)
SMEM = pl.BlockSpec(memory_space=pltpu.SMEM)
F32, BF16 = jnp.float32, jnp.bfloat16


def params():
    return pltpu.CompilerParams(vmem_limit_bytes=40 << 20)


def dot(lhs, rhs):
    return jnp.dot(lhs, rhs, preferred_element_type=F32)


def times(lhs, rhs):
    return (
        dot(lhs[0], rhs[0]) - dot(lhs[1], rhs[1]),
        dot(lhs[0], rhs[1]) + dot(lhs[1], rhs[0]),
    )


def partner_kernel(shifts, groups, place, plus, minus, coupling, g_ref, *refs):
    count = len(shifts)
    waves, outs = refs[:count], refs[count:]
    group, core = place[0], place[1]
    slots = g_ref.shape[1]
    for n, shift in enumerate(shifts):
        owner = lax.rem(group + groups - shift, groups)
        for turn in range(slots):
            slot = core if turn == 0 else 1 - core
            target = owner * slots + slot
            wave = (waves[n][0, slot], waves[n][1, slot])
            real, imag = None, None
            for block in range(slots):
                name = group * slots + block
                weight = jnp.where(plus[target] == name, coupling[0], 0.0)
                weight += jnp.where(minus[target] == name, coupling[1], 0.0)
                part = times(wave, (g_ref[0, block], g_ref[1, block]))
                real = part[0] * weight if real is None else real + part[0] * weight
                imag = part[1] * weight if imag is None else imag + part[1] * weight
            out = outs[2 * n + turn]
            out[0] = real.astype(out.dtype)
            out[1] = imag.astype(out.dtype)


def partner_products(shifts, groups, place, plus, minus, coupling, g_here, waves):
    _, _, modes, orbitals = waves[0].shape
    return pl.pallas_call(
        functools.partial(partner_kernel, shifts, groups),
        out_shape=[jax.ShapeDtypeStruct((2, modes, orbitals), BF16)] * (2 * len(shifts)),
        in_specs=[SMEM] * 4 + [VMEM] * (1 + len(shifts)),
        out_specs=[VMEM] * (2 * len(shifts)),
        compiler_params=params(),
        name="partner_products",
    )(place, plus, minus, coupling, g_here, *waves)


def source_kernel(count, place, potential, incident, green, step, *refs):
    here, there = refs[:count], refs[count : 2 * count]
    first_ref, chip_ref, send_ref, term_ref = refs[2 * count :]
    core = place[1]
    for turn, parts in enumerate((here, there)):
        segment = core if turn == 0 else 1 - core
        for c in range(2):
            total = parts[0][c].astype(F32)
            for part in parts[1:]:
                total = total + part[c].astype(F32)
            total = total + potential[segment] * incident[segment, c].astype(F32)
            term_ref[segment, c] = total.astype(BF16)
    first = times((term_ref[0, 0], term_ref[0, 1]), (green[0, 0], green[0, 1]))
    first_ref[0], first_ref[1] = first
    rounded = (first[0].astype(BF16), first[1].astype(BF16))
    passed = times(rounded, (step[0], step[1]))
    added = times((term_ref[1, 0], term_ref[1, 1]), (green[1, 0], green[1, 1]))
    for c in range(2):
        chip = passed[c] + added[c]
        chip_ref[c] = chip
        send_ref[c] = chip.astype(BF16)


def chip_sources(place, potential, incident, green, step, here, there):
    _, _, modes, orbitals = incident.shape
    wave = (2, modes, orbitals)
    return pl.pallas_call(
        functools.partial(source_kernel, len(here)),
        out_shape=[
            jax.ShapeDtypeStruct(wave, F32),
            jax.ShapeDtypeStruct(wave, F32),
            jax.ShapeDtypeStruct(wave, BF16),
        ],
        in_specs=[SMEM] * 2 + [VMEM] * (3 + len(here) + len(there)),
        out_specs=[VMEM] * 3,
        scratch_shapes=[pltpu.VMEM((2, 2, modes, orbitals), BF16)],
        compiler_params=params(),
        name="chip_sources",
    )(place, potential, incident, green, step, *here, *there)


def chain_kernel(count, place, step, chip_map, first, chip, *refs):
    waves, maps = refs[:count], refs[count : 2 * count - 1]
    own_ref, other_ref, keep_ref = refs[2 * count - 1 :]
    core = place[1]
    entering = (waves[-1][0], waves[-1][1])
    for n in range(count - 2, -1, -1):
        moved = times(entering, (maps[n][0], maps[n][1]))
        entering = tuple((moved[c] + waves[n][c].astype(F32)).astype(BF16) for c in range(2))
    at_first = times(entering, (step[0], step[1]))
    at_second = times(entering, (chip_map[0], chip_map[1]))
    for c in range(2):
        keep_ref[0, c] = (at_first[c] + first[c]).astype(BF16)
        keep_ref[1, c] = (at_second[c] + chip[c]).astype(BF16)
    own_ref[...] = keep_ref[core]
    other_ref[...] = keep_ref[1 - core]


def chain(place, step, chip_map, first, chip, waves, maps):
    wave = first.shape
    return pl.pallas_call(
        functools.partial(chain_kernel, len(waves)),
        out_shape=[jax.ShapeDtypeStruct(wave, BF16)] * 2,
        in_specs=[SMEM] + [VMEM] * (4 + len(waves) + len(maps)),
        out_specs=[VMEM] * 2,
        scratch_shapes=[pltpu.VMEM((2,) + wave, BF16)],
        compiler_params=params(),
        name="chain",
    )(place, step, chip_map, first, chip, *waves, *maps)


def across(lhs, rhs):
    return lax.dot_general(lhs, rhs, (((0,), (0,)), ((), ())), preferred_element_type=F32)


def block_kernel(place, counts, incident, own, other, scattered, green_next, both):
    core = place[1]
    modes = own.shape[1]
    for turn, chained in enumerate((own, other)):
        slot = core if turn == 0 else 1 - core
        live = slot < counts[0]
        for c in range(2):
            wave = chained[c].astype(F32)
            scattered[c, slot] = jnp.where(live, wave, 0.0).astype(BF16)
            combined = (incident[c, slot].astype(F32) + wave).astype(BF16)
            both[0, c * modes : (c + 1) * modes] = combined
            both[1, (1 - c) * modes : (2 - c) * modes] = -combined if c == 0 else combined
        stacked = both[0]
        real = across(both[1], stacked) / modes
        imag = across(stacked, stacked) / modes
        green_next[0, slot] = jnp.where(live, real, 0.0).astype(BF16)
        green_next[1, slot] = jnp.where(live, imag, 0.0).astype(BF16)


def green_blocks(place, counts, incident, own, other):
    _, slots, modes, orbitals = incident.shape
    return pl.pallas_call(
        block_kernel,
        out_shape=[
            jax.ShapeDtypeStruct((2, slots, modes, orbitals), BF16),
            jax.ShapeDtypeStruct((2, slots, orbitals, orbitals), BF16),
        ],
        in_specs=[SMEM] * 2 + [VMEM] * 3,
        out_specs=[VMEM] * 2,
        scratch_shapes=[pltpu.VMEM((2, 2 * modes, orbitals), BF16)],
        compiler_params=params(),
        name="green_blocks",
    )(place, counts, incident, own, other)


def complex_matrix(lhs, rhs):
    real = dot(lhs[0], rhs[0]) - dot(lhs[1], rhs[1])
    imag = dot(lhs[0], rhs[1]) + dot(lhs[1], rhs[0])
    return jnp.stack([real, imag])


def shards(groups, segments, g_prev, local_green, prop, incoming, plus_partner, minus_partner, counts, pot_index, levels, coupling):
    chips = segments // 2
    group, segment = lax.axis_index("energy"), lax.axis_index("wire")
    core = lax.rem(segment, 2)
    place = jnp.stack([group, core]).astype(jnp.int32)
    g_here, green_here = g_prev[:, :, 0], local_green[:, :, 0]
    prop_here, incident = prop[:, :, 0], incoming[:, :, 0]

    def turned(shift, swap):
        pairs = []
        for e in range(groups):
            for w in range(segments):
                pairs.append((e * segments + w, (e + shift) % groups * segments + (w ^ swap)))
        return pairs

    def send(value, shift, swap):
        return lax.ppermute(value, ("energy", "wire"), turned(shift, swap))

    def later(value, hops, least=0):
        pairs = []
        for chip in range(least, chips - hops):
            pairs += [(2 * chip + b, 2 * (chip + hops) + b) for b in range(2)]
        return lax.ppermute(value, "wire", pairs)

    waves = [incident] + [send(incident, shift, 0) for shift in range(1, groups)]

    def by_segment(value, axis):
        mine = lax.dynamic_index_in_dim(value, core, axis, False)
        passed = lax.dynamic_index_in_dim(value, 1 - core, axis, False)
        received = send(passed, 0, 1)
        first = jnp.where(core == 0, mine, received)
        second = jnp.where(core == 0, received, mine)
        return first, second

    level_hit = pot_index[0] == jnp.arange(levels.shape[0], dtype=jnp.int32)
    potential = jnp.sum(jnp.where(level_hit, levels, F32(0.0)))[None]
    potential_there = send(potential, 0, 1)
    potentials = jnp.where(
        core == 0,
        jnp.concatenate([potential, potential_there]),
        jnp.concatenate([potential_there, potential]),
    )
    steps = by_segment(prop_here, 1)
    chip_map = complex_matrix(*steps).astype(BF16)
    greens = jnp.stack(by_segment(green_here, 1))
    incidents = jnp.stack(by_segment(incident, 1))

    shifts = tuple(range(groups))
    local = partner_products((0,), groups, place, plus_partner, minus_partner, coupling, g_here, waves[:1])
    far = partner_products(shifts[1:], groups, place, plus_partner, minus_partner, coupling, g_here, waves[1:])
    here, there = [local[0]], [send(local[1], 0, 1)]
    for n, shift in enumerate(shifts[1:]):
        here.append(send(far[2 * n], groups - shift, 0))
        there.append(send(far[2 * n + 1], groups - shift, 1))

    first, chip, chip_send = chip_sources(place, potentials, incidents, greens, steps[1], here, there)
    if chips <= 4:
        maps = [later(chip_map, hops, 1) for hops in range(1, chips - 1)]
        arrived = [later(chip_send, hops) for hops in range(1, chips)]
    else:
        maps = []
        entering = jnp.zeros_like(chip_send)
        for at in range(chips - 1):
            leaving = (complex_matrix(entering, chip_map) + chip).astype(BF16)
            pairs = [(2 * at + b, 2 * at + 2 + b) for b in range(2)]
            entering = entering + lax.ppermute(leaving, "wire", pairs)
        arrived = [entering]
    own, other = chain(place, steps[0], chip_map, first, chip, arrived, maps)

    other = send(other, 0, 1)
    scattered, green_next = green_blocks(place, counts, incident, own, other)
    return scattered[:, :, None], green_next[:, :, None]


def solution(mesh):
    placed = P(None, "energy", "wire", None, None)
    return jax.shard_map(
        functools.partial(shards, mesh.shape["energy"], mesh.shape["wire"]),
        mesh=mesh,
        in_specs=(placed,) * 4 + (P(), P(), P("energy"), P("wire"), P(), P()),
        out_specs=(placed, placed),
        check_vma=False,
    )
```

time: 371 us -> 81.9 us (0.22)
  waiting for transfers between devices: 267 us -> 26.5 us
  matrix products: 63.7 us -> 1.74 us
  starting transfers between devices: 0.12 us -> 27 us
  Pallas kernels: 0 us -> 13.9 us
  between operations: 15.3 us -> 2.2 us
  other arithmetic: 14.3 us -> 5.11 us
  local copies, waits for them, and re-layouts: 8.73 us -> 4.73 us
    all_gather x3 -> x0, waiting for transfers between devices: 266 us -> none  [the longest x1 149 us: shards(): shard_piece = lax.all_gather(g_prev, 'energy', axis=1, tiled=True)]
    dot_general x50 -> x4, matrix products: 63.7 us -> 1.74 us  [dot(): return jnp.dot(lhs, rhs, preferred_element_type=F32)]
    ppermute x0 -> x20, starting transfers between devices: none -> 27 us  [the longest x15 18 us: send(): return lax.ppermute(value, ('energy', 'wire'), turned(shift, swap))]
    ppermute x0 -> x20, waiting for transfers between devices: none -> 26.5 us  [the longest x15 24.6 us: send(): return lax.ppermute(value, ('energy', 'wire'), turned(shift, swap))]
    pallas_call x0 -> x5, Pallas kernels: none -> 13.9 us  [the longest x2 7.14 us: partner_products(): pl.pallas_call(functools.partial(partner_kernel, shifts, groups), out_sha...]
    select_n x7 -> x2, other arithmetic: 7.62 us -> 2.72 us  [the longest x1 1.36 us: by_segment(): second = jnp.where(core == 0, received, mine)]
    unnamed x27 -> x16, local copies, waits for them, and re-layouts: 4.82 us -> 0.04 us
  transfers between devices with their start and end apart: 3 -> 20, of which waited for: 3 -> 8; matrix products, arithmetic and copies ran while one was open for 0% -> 11% of each run, Pallas kernels for 0% -> 11%
where the time goes in v1:
time: 81.9 us; the launch traced here: 81.2 us
  starting transfers between devices  27 us (33%)
  waiting for transfers between devices  26.5 us (32%)
  Pallas kernels  13.9 us (17%)
  other arithmetic  5.11 us (6%)
  local copies, waits for them, and re-layouts  4.73 us (6%)
  between operations  2.2 us (3%)
  matrix products  1.74 us (2%)
    ppermute x15, waiting for transfers between devices, send(): return lax.ppermute(value, ('energy', 'wire'), turned(shift, swap))  24.6 us
    ppermute x15, starting transfers between devices, send(): return lax.ppermute(value, ('energy', 'wire'), turned(shift, swap))  18 us
    ppermute x5, starting transfers between devices, later(): return lax.ppermute(value, 'wire', pairs)  9.03 us
    pallas_call x2, Pallas kernels, partner_products(): pl.pallas_call(functools.partial(partner_kernel, shifts, groups), out_sha...  7.14 us
    squeeze x3, local copies, waits for them, and re-layouts, by_segment(): passed = lax.dynamic_index_in_dim(value, 1 - core, axis, False)  4.7 us
    pallas_call x1, Pallas kernels, green_blocks(): pl.pallas_call(block_kernel, out_shape=[jax.ShapeDtypeStruct((2, slots, m...  2.61 us
    pallas_call x1, Pallas kernels, chain(): pl.pallas_call(functools.partial(chain_kernel, len(waves)), out_shape=[ja...  2.15 us
    pallas_call x1, Pallas kernels, chip_sources(): pl.pallas_call(functools.partial(source_kernel, len(here)), out_shape=[ja...  1.95 us
  transfers between devices with their start and end apart: 20, of which 8 were waited for; matrix products, arithmetic and copies ran while one was open for 11% of the time, Pallas kernels for 11%

profile of v1, /device:TPU:1, one launch (start us, length us, event | category | flops | bytes accessed | tf_op | source)
XLA Modules:
  0.0 81.2 jit_solution(4089770766067929434)
XLA Ops:
  0.6 0.0 copy-start.1
  0.7 2.4 %dynamic-slice_bitcast_fusion.1 = bf16[2,512,512]{2,1,0:T(8,128)(2,1)} fusion(bf16[2,2,1,512,512]{4,3,2,1,0:T(8,128)(2,1)} %param.12, s32[]{:T(128)S(6)} %select_n.58), kind=kLoop, calls=%fused_computation.15 | loop fusion | bytes 2097156 | tf_op jit(solution)/shard_map/jit(dynamic_index_in_dim)/squeeze | solution.py:210
  3.1 0.1 collective-permute-start
  3.2 0.0 copy-done.1
  3.2 2.7 %collective-permute-start.4 = (bf16[2,2,64,512]{3,2,1,0:T(8,128)(2,1)S(1)}, bf16[2,2,64,512]{3,2,1,0:T(8,128)(2,1)S(1)}, u32[]{:S(2)}, u32[]{:S(2)}) collective-permute-start(bf16[2,2,64,512]{3,2,1,0:T(8,128)(2,1)S(1)} %bitcast.66), channel_id=1, source_target_pairs={{0,8},{1,9},{2,10},{3,11},{4,12},{5,13},{6,14},{7,15},{8,16},{9,17... | collective-permute-start | bytes 786440 | tf_op jit(solution)/shard_map/ppermute | solution.py:198
  5.9 2.3 %collective-permute-start.5 = (bf16[2,2,64,512]{3,2,1,0:T(8,128)(2,1)S(1)}, bf16[2,2,64,512]{3,2,1,0:T(8,128)(2,1)S(1)}, u32[]{:S(2)}, u32[]{:S(2)}) collective-permute-start(bf16[2,2,64,512]{3,2,1,0:T(8,128)(2,1)S(1)} %bitcast.67), channel_id=1, source_target_pairs={{0,16},{1,17},{2,18},{3,19},{4,20},{5,21},{6,22},{7,23},{8,24},{9,... | collective-permute-start | bytes 786440 | tf_op jit(solution)/shard_map/ppermute | solution.py:198
  8.2 2.3 %dynamic-slice_bitcast_fusion = bf16[2,512,512]{2,1,0:T(8,128)(2,1)} fusion(bf16[2,2,1,512,512]{4,3,2,1,0:T(8,128)(2,1)} %param.11, s32[]{:T(128)S(6)} %select_n.58), kind=kLoop, calls=%fused_computation.14 | loop fusion | bytes 2097156 | tf_op jit(solution)/shard_map/jit(dynamic_index_in_dim)/squeeze | solution.py:210
  10.5 0.6 collective-permute-start.3
  11.1 0.1 collective-permute-start.2
  11.9 0.0 copy-start.5
  11.9 0.1 pad_add_fusion.place
  12.0 0.0 copy-done
  12.0 2.1 %partner_products.2 = (bf16[2,64,512]{2,1,0:T(8,128)(2,1)S(1)}, bf16[2,64,512]{2,1,0:T(8,128)(2,1)S(1)}) custom-call(s32[2]{0:T(128)S(1)} %pad_add_fusion.place, s32[8]{0:T(128)S(1)} %copy-done.2, s32[8]{0:T(128)S(1)} %copy-done.3, f32[2]{0:T(128)S(1)} %copy-done.4, bf16[2,2,512,512]{3,2,1,0:T(8,128)(2,1)S(1)} %bitcast.64, bf16[2,2,64,512]{3,2,1,0:T(8,128)(2,1)S(1)} %bitcast.68), custom_call_target="tpu_custom_call" | custom-call | tf_op jit(solution)/shard_map/partner_products/pallas_call | solution.py:56
  14.1 0.0 copy-done.7
  14.1 0.6 fusion.10
  14.7 0.0 collective-permute-done
  14.7 0.5 collective-permute-start.1
  15.2 1.4 %bitcast_select_fusion.2 = (bf16[2,512,512]{2,1,0:T(8,128)(2,1)S(1)}, bf16[2,512,512]{2,1,0:T(8,128)(2,1)S(1)}) fusion(bf16[2,512,512]{2,1,0:T(8,128)(2,1)} %collective-permute-done, pred[]{:T(512)S(6)} %eq.6, bf16[2,2,1,512,512]{4,3,2,1,0:T(8,128)(2,1)S(1)} %copy-done.5, s32[]{:T(128)S(6)} %select_n.57), kind=kLoop, calls=%fused_computation.12 | loop fusion | flops 1048576 | bytes 4194309 | tf_op jit(solution)/shard_map/jit(_where)/select_n | solution.py:213
  16.6 0.4 fusion.7
  17.0 0.4 fusion.6
  17.4 0.4 fusion.3
  17.9 0.4 fusion.2
  18.3 0.1 pad_maximum_fusion.1.chip_map
  18.4 0.0 copy-start.6
  18.4 0.0 collective-permute-done.1
  18.5 0.9 %collective-permute-start.17 = (bf16[2,512,512]{2,1,0:T(8,128)(2,1)S(1)}, bf16[2,512,512]{2,1,0:T(8,128)(2,1)S(1)}, u32[]{:S(2)}, u32[]{:S(2)}) collective-permute-start(bf16[2,512,512]{2,1,0:T(8,128)(2,1)S(1)} %pad_maximum_fusion.1.chip_map), channel_id=1, source_target_pairs={{2,4},{3,5},{4,6},{5,7},{10,12},{11,13},{12,14},{13,15},{18,20},{1... | collective-permute-start | bytes 3145736 | tf_op jit(solution)/shard_map/ppermute | solution.py:204
  19.3 0.0 collective-permute-done.2
  19.3 0.7 collective-permute-start.18
  20.1 1.4 %broadcast_select_fusion.potential = f32[2]{0:T(128)S(1)} fusion(pred[]{:T(512)S(6)} %eq.6, f32[1]{0:T(128)} %collective-permute-done.1, f32[1]{0:T(128)} %bitcast.12), kind=kLoop, calls=%fused_computation.29 | loop fusion | flops 6 | bytes 17 | tf_op jit(solution)/shard_map/jit(_where)/select_n | solution.py:219
  21.4 0.0 collective-permute-done.4.refs_0_
  21.4 1.1 %collective-permute-start.6 = (bf16[2,2,64,512]{3,2,1,0:T(8,128)(2,1)S(1)}, bf16[2,2,64,512]{3,2,1,0:T(8,128)(2,1)S(1)}, u32[]{:S(2)}, u32[]{:S(2)}) collective-permute-start(bf16[2,2,64,512]{3,2,1,0:T(8,128)(2,1)S(1)} %bitcast.69), channel_id=1, source_target_pairs={{0,24},{1,25},{2,26},{3,27},{4,28},{5,29},{6,30},{7,31},{8,0},{9,1... | collective-permute-start | bytes 786440 | tf_op jit(solution)/shard_map/ppermute | solution.py:198
  22.5 3.5 %collective-permute-done.5.refs_1_ = bf16[2,2,64,512]{3,2,1,0:T(8,128)(2,1)S(1)} collective-permute-done((bf16[2,2,64,512]{3,2,1,0:T(8,128)(2,1)S(1)}, bf16[2,2,64,512]{3,2,1,0:T(8,128)(2,1)S(1)}, u32[]{:S(2)}, u32[]{:S(2)}) %collective-permute-start.5) | collective-permute-done | bytes 262176 | tf_op jit(solution)/shard_map/ppermute | solution.py:198
  26.0 0.5 collective-permute-start.10
  26.6 5.0 %collective-permute-done.6.refs_2_ = bf16[2,2,64,512]{3,2,1,0:T(8,128)(2,1)S(1)} collective-permute-done((bf16[2,2,64,512]{3,2,1,0:T(8,128)(2,1)S(1)}, bf16[2,2,64,512]{3,2,1,0:T(8,128)(2,1)S(1)}, u32[]{:S(2)}, u32[]{:S(2)}) %collective-permute-start.6) | collective-permute-done | bytes 262176 | tf_op jit(solution)/shard_map/ppermute | solution.py:198
  31.6 5.0 %partner_products.3 = (bf16[2,64,512]{2,1,0:T(8,128)(2,1)S(1)}, bf16[2,64,512]{2,1,0:T(8,128)(2,1)S(1)}, bf16[2,64,512]{2,1,0:T(8,128)(2,1)S(1)}, bf16[2,64,512]...) custom-call(s32[2]{0:T(128)S(1)} %pad_add_fusion.place, s32[8]{0:T(128)S(1)} %copy-done.2, ...), custom_call_target="tpu_custom_call" | custom-call | tf_op jit(solution)/shard_map/partner_products/pallas_call | solution.py:56
  36.6 1.8 %collective-permute-start.11 = (bf16[2,64,512]{2,1,0:T(8,128)(2,1)S(1)}, bf16[2,64,512]{2,1,0:T(8,128)(2,1)S(1)}, u32[]{:S(2)}, u32[]{:S(2)}) collective-permute-start(bf16[2,64,512]{2,1,0:T(8,128)(2,1)S(1)} %get-tuple-element.22), channel_id=1, source_target_pairs={{0,25},{1,24},{2,27},{3,26},{4,29},{5,28},{6,31},{7,30},{8,1},{9,0... | collective-permute-start | bytes 393224 | tf_op jit(solution)/shard_map/ppermute | solution.py:198
  38.4 0.0 collective-permute-done.10.refs_4_
  38.4 0.0 collective-permute-start.12
  38.5 0.0 collective-permute-done.3
  38.5 0.8 collective-permute-start.13
  39.2 1.4 %fusion.4 = (bf16[1,2,512,512]{3,2,1,0:T(8,128)(2,1)S(1)}, bf16[1,2,512,512]{3,2,1,0:T(8,128)(2,1)S(1)}) fusion(bf16[2,512,512]{2,1,0:T(8,128)(2,1)} %collective-permute-done.3, pred[]{:T(512)S(6)} %eq.6, bf16[2,2,1,512,512]{4,3,2,1,0:T(8,128)(2,1)S(1)} %copy-done.6, s32[]{:T(128)S(6)} %select_n.57), kind=kLoop, calls=%fused_computation.10 | loop fusion | flops 1048576 | bytes 4194309 | tf_op jit(solution)/shard_map/stack | solution.py:226
  40.6 1.7 %collective-permute-done.11.refs_5_ = bf16[2,64,512]{2,1,0:T(8,128)(2,1)S(1)} collective-permute-done((bf16[2,64,512]{2,1,0:T(8,128)(2,1)S(1)}, bf16[2,64,512]{2,1,0:T(8,128)(2,1)S(1)}, u32[]{:S(2)}, u32[]{:S(2)}) %collective-permute-start.11) | collective-permute-done | bytes 131104 | tf_op jit(solution)/shard_map/ppermute | solution.py:198
  42.3 3.9 %collective-permute-start.7 = (bf16[2,64,512]{2,1,0:T(8,128)(2,1)S(1)}, bf16[2,64,512]{2,1,0:T(8,128)(2,1)S(1)}, u32[]{:S(2)}, u32[]{:S(2)}) collective-permute-start(bf16[2,64,512]{2,1,0:T(8,128)(2,1)S(1)} %get-tuple-element.18), channel_id=1, source_target_pairs={{0,24},{1,25},{2,26},{3,27},{4,28},{5,29},{6,30},{7,31},{8,0},{9,1... | collective-permute-start | bytes 393224 | tf_op jit(solution)/shard_map/ppermute | solution.py:198
  46.2 4.8 %collective-permute-done.12.refs_6_ = bf16[2,64,512]{2,1,0:T(8,128)(2,1)S(1)} collective-permute-done((bf16[2,64,512]{2,1,0:T(8,128)(2,1)S(1)}, bf16[2,64,512]{2,1,0:T(8,128)(2,1)S(1)}, u32[]{:S(2)}, u32[]{:S(2)}) %collective-permute-start.12) | collective-permute-done | bytes 131104 | tf_op jit(solution)/shard_map/ppermute | solution.py:198
  51.0 0.0 collective-permute-start.8
  51.0 0.0 collective-permute-done.13.refs_7_
  51.0 1.7 %collective-permute-start.9 = (bf16[2,64,512]{2,1,0:T(8,128)(2,1)S(1)}, bf16[2,64,512]{2,1,0:T(8,128)(2,1)S(1)}, u32[]{:S(2)}, u32[]{:S(2)}) collective-permute-start(bf16[2,64,512]{2,1,0:T(8,128)(2,1)S(1)} %get-tuple-element.20), channel_id=1, source_target_pairs={{0,8},{1,9},{2,10},{3,11},{4,12},{5,13},{6,14},{7,15},{8,16},{9,17... | collective-permute-start | bytes 393224 | tf_op jit(solution)/shard_map/ppermute | solution.py:198
  52.7 0.2 pad_maximum_fusion.green
  52.9 0.0 collective-permute-done.7.refs_1_
  52.9 9.3 %collective-permute-done.8.refs_2_ = bf16[2,64,512]{2,1,0:T(8,128)(2,1)S(1)} collective-permute-done((bf16[2,64,512]{2,1,0:T(8,128)(2,1)S(1)}, bf16[2,64,512]{2,1,0:T(8,128)(2,1)S(1)}, u32[]{:S(2)}, u32[]{:S(2)}) %collective-permute-start.8) | collective-permute-done | bytes 131104 | tf_op jit(solution)/shard_map/ppermute | solution.py:198
  62.2 0.0 collective-permute-done.9.refs_3_
  62.2 1.9 %chip_sources.1 = (f32[2,64,512]{2,1,0:T(8,128)S(1)}, f32[2,64,512]{2,1,0:T(8,128)S(1)}, bf16[2,64,512]{2,1,0:T(8,128)(2,1)S(1)}) custom-call(s32[2]{0:T(128)S(1)} %pad_add_fusion.place, f32[2]{0:T(128)S(1)} %broadcast_select_fusion.potential, bf16[2,2,64,512]{3,2,1,0:T(8,128)(2,1)S(1)} %pad_maximum_fusion.2.incident, ...), custom_call_target="tpu_custom_call" | custom-call | tf_op jit(solution)/shard_map/chip_sources/pallas_call | solution.py:92
  64.2 3.3 %collective-permute-start.14 = (bf16[2,64,512]{2,1,0:T(8,128)(2,1)S(1)}, bf16[2,64,512]{2,1,0:T(8,128)(2,1)S(1)}, u32[]{:S(2)}, u32[]{:S(2)}) collective-permute-start(bf16[2,64,512]{2,1,0:T(8,128)(2,1)S(1)} %get-tuple-element.27), channel_id=1, source_target_pairs={{0,2},{1,3},{2,4},{3,5},{4,6},{5,7},{8,10},{9,11},{10,12},{11,13},... | collective-permute-start | bytes 393224 | tf_op jit(solution)/shard_map/ppermute | solution.py:204
  67.5 2.8 %collective-permute-start.15 = (bf16[2,64,512]{2,1,0:T(8,128)(2,1)S(1)}, bf16[2,64,512]{2,1,0:T(8,128)(2,1)S(1)}, u32[]{:S(2)}, u32[]{:S(2)}) collective-permute-start(bf16[2,64,512]{2,1,0:T(8,128)(2,1)S(1)} %get-tuple-element.27), channel_id=1, source_target_pairs={{0,4},{1,5},{2,6},{3,7},{8,12},{9,13},{10,14},{11,15},{16,20},{17,... | collective-permute-start | bytes 393224 | tf_op jit(solution)/shard_map/ppermute | solution.py:204
  70.3 1.3 %collective-permute-start.16 = (bf16[2,64,512]{2,1,0:T(8,128)(2,1)S(1)}, bf16[2,64,512]{2,1,0:T(8,128)(2,1)S(1)}, u32[]{:S(2)}, u32[]{:S(2)}) collective-permute-start(bf16[2,64,512]{2,1,0:T(8,128)(2,1)S(1)} %get-tuple-element.27), channel_id=1, source_target_pairs={{0,6},{1,7},{8,14},{9,15},{16,22},{17,23},{24,30},{25,31}} | collective-permute-start | bytes 393224 | tf_op jit(solution)/shard_map/ppermute | solution.py:204
  71.6 0.0 collective-permute-done.14.refs_0_
  71.6 1.3 %collective-permute-done.15.refs_1_ = bf16[2,64,512]{2,1,0:T(8,128)(2,1)S(1)} collective-permute-done((bf16[2,64,512]{2,1,0:T(8,128)(2,1)S(1)}, bf16[2,64,512]{2,1,0:T(8,128)(2,1)S(1)}, u32[]{:S(2)}, u32[]{:S(2)}) %collective-permute-start.15) | collective-permute-done | bytes 131104 | tf_op jit(solution)/shard_map/ppermute | solution.py:204
  73.0 0.6 collective-permute-done.16.refs_2_
  73.6 0.0 collective-permute-done.17.refs_3_
  73.6 0.0 collective-permute-done.18.refs_4_
  73.6 2.2 %chain.1 = (bf16[2,64,512]{2,1,0:T(8,128)(2,1)S(1)}, bf16[2,64,512]{2,1,0:T(8,128)(2,1)S(1)}) custom-call(s32[2]{0:T(128)S(1)} %pad_add_fusion.place, bf16[2,512,512]{2,1,0:T(8,128)(2,1)S(1)} %get-tuple-element.37.step, bf16[2,512,512]{2,1,0:T(8,128)(2,1)S(1)} %pad_maximum_fusion.1.chip_map, f32[2,64,512]{2,1,0:T(8,128)S(1)} %get-tuple-element.25.first, ...), custom_call_target="tpu_custom_call" | custom-call | tf_op jit(solution)/shard_map/chain/pallas_call | solution.py:126
  75.7 1.8 %collective-permute-start.19 = (bf16[2,64,512]{2,1,0:T(8,128)(2,1)S(1)}, bf16[2,64,512]{2,1,0:T(8,128)(2,1)S(1)}, u32[]{:S(2)}, u32[]{:S(2)}) collective-permute-start(bf16[2,64,512]{2,1,0:T(8,128)(2,1)S(1)} %get-tuple-element.29), channel_id=1, source_target_pairs={{0,1},{1,0},{2,3},{3,2},{4,5},{5,4},{6,7},{7,6},{8,9},{9,8},{10,11... | collective-permute-start | bytes 393224 | tf_op jit(solution)/shard_map/ppermute | solution.py:198
  78.2 0.3 collective-permute-done.19.other
  78.5 2.6 %green_blocks.1 = (bf16[2,2,64,512]{3,2,1,0:T(8,128)(2,1)}, bf16[2,2,512,512]{3,2,1,0:T(8,128)(2,1)}) custom-call(s32[2]{0:T(128)S(1)} %pad_add_fusion.place, s32[1]{0:T(128)S(6)} %copy.14.counts, bf16[2,2,64,512]{3,2,1,0:T(8,128)(2,1)S(1)} %bitcast.70, bf16[2,64,512]{2,1,0:T(8,128)(2,1)S(1)} %get-tuple-element.28.own, ...), custom_call_target="tpu_custom_call" | custom-call | tf_op jit(solution)/shard_map/green_blocks/pallas_call | solution.py:162
  (13 shorter events, 0.1 us)
Async XLA Ops:
  0.6 2.5 %copy-start.1 = (bf16[2,2,1,64,512]{4,3,2,1,0:T(8,128)(2,1)S(1)}, bf16[2,2,1,64,512]{4,3,2,1,0:T(8,128)(2,1)}, u32[]{:S(2)}) copy-start(bf16[2,2,1,64,512]{4,3,2,1,0:T(8,128)(2,1)} %param.13) | copy-start | bytes 786436
  0.6 11.3 %copy-start = (bf16[2,2,1,512,512]{4,3,2,1,0:T(8,128)(2,1)S(1)}, bf16[2,2,1,512,512]{4,3,2,1,0:T(8,128)(2,1)}, u32[]{:S(2)}) copy-start(bf16[2,2,1,512,512]{4,3,2,1,0:T(8,128)(2,1)} %param.10) | copy-start | bytes 6291460
  0.7 11.3 %copy-start.2 = (s32[8]{0:T(128)S(1)}, s32[8]{0:T(128)}, u32[]{:S(2)}) copy-start(s32[8]{0:T(128)} %plus.3) | copy-start | bytes 100
  0.7 11.3 %copy-start.3 = (s32[8]{0:T(128)S(1)}, s32[8]{0:T(128)}, u32[]{:S(2)}) copy-start(s32[8]{0:T(128)} %minus.3) | copy-start | bytes 100
  0.7 11.3 %copy-start.4 = (f32[2]{0:T(128)S(1)}, f32[2]{0:T(128)}, u32[]{:S(2)}) copy-start(f32[2]{0:T(128)} %coupling.3) | copy-start | bytes 28
  3.1 11.6 %collective-permute-start = (bf16[2,512,512]{2,1,0:T(8,128)(2,1)}, bf16[2,512,512]{2,1,0:T(8,128)(2,1)}, u32[]{:S(2)}, u32[]{:S(2)}) collective-permute-start(bf16[2,512,512]{2,1,0:T(8,128)(2,1)} %dynamic-slice_bitcast_fusion.1), channel_id=1, source_target_pairs={{0,1},{1,0},{2,3},{3,2},{4,5},{5,4},{6,7},{7,6},{8,9},{9,8},{10,11... | collective-permute-start | bytes 3145736 | tf_op jit(solution)/shard_map/ppermute | solution.py:198
  3.2 10.9 %copy-start.7 = (f32[16]{0:T(128)S(1)}, f32[16]{0:T(128)}, u32[]{:S(2)}) copy-start(f32[16]{0:T(128)} %param.18) | copy-start | bytes 196
  3.2 18.3 %collective-permute-start.4 = (bf16[2,2,64,512]{3,2,1,0:T(8,128)(2,1)S(1)}, bf16[2,2,64,512]{3,2,1,0:T(8,128)(2,1)S(1)}, u32[]{:S(2)}, u32[]{:S(2)}) collective-permute-start(bf16[2,2,64,512]{3,2,1,0:T(8,128)(2,1)S(1)} %bitcast.66), channel_id=1, source_target_pairs={{0,8},{1,9},{2,10},{3,11},{4,12},{5,13},{6,14},{7,15},{8,16},{9,17... | collective-permute-start | bytes 786440 | tf_op jit(solution)/shard_map/ppermute | solution.py:198
  5.9 20.1 %collective-permute-start.5 = (bf16[2,2,64,512]{3,2,1,0:T(8,128)(2,1)S(1)}, bf16[2,2,64,512]{3,2,1,0:T(8,128)(2,1)S(1)}, u32[]{:S(2)}, u32[]{:S(2)}) collective-permute-start(bf16[2,2,64,512]{3,2,1,0:T(8,128)(2,1)S(1)} %bitcast.67), channel_id=1, source_target_pairs={{0,16},{1,17},{2,18},{3,19},{4,20},{5,21},{6,22},{7,23},{8,24},{9,... | collective-permute-start | bytes 786440 | tf_op jit(solution)/shard_map/ppermute | solution.py:198
  10.5 28.0 %collective-permute-start.3 = (bf16[2,512,512]{2,1,0:T(8,128)(2,1)}, bf16[2,512,512]{2,1,0:T(8,128)(2,1)}, u32[]{:S(2)}, u32[]{:S(2)}) collective-permute-start(bf16[2,512,512]{2,1,0:T(8,128)(2,1)} %dynamic-slice_bitcast_fusion), channel_id=1, source_target_pairs={{0,1},{1,0},{2,3},{3,2},{4,5},{5,4},{6,7},{7,6},{8,9},{9,8},{10,11... | collective-permute-start | bytes 3145736 | tf_op jit(solution)/shard_map/ppermute | solution.py:198
  11.1 8.2 %collective-permute-start.2 = (bf16[2,64,512]{2,1,0:T(8,128)(2,1)S(1)}, bf16[2,64,512]{2,1,0:T(8,128)(2,1)S(1)}, u32[]{:S(2)}, u32[]{:S(2)}) collective-permute-start(bf16[2,64,512]{2,1,0:T(8,128)(2,1)S(1)} %dynamic-slice_bitcast_fusion.2), channel_id=1, source_target_pairs={{0,1},{1,0},{2,3},{3,2},{4,5},{5,4},{6,7},{7,6},{8,9},{9,8},{10,11... | collective-permute-start | bytes 393224 | tf_op jit(solution)/shard_map/ppermute | solution.py:198
  11.9 3.3 %copy-start.5 = (bf16[2,2,1,512,512]{4,3,2,1,0:T(8,128)(2,1)S(1)}, bf16[2,2,1,512,512]{4,3,2,1,0:T(8,128)(2,1)}, u32[]{:S(2)}) copy-start(bf16[2,2,1,512,512]{4,3,2,1,0:T(8,128)(2,1)} %param.12) | copy-start | bytes 6291460
  14.7 3.7 %collective-permute-start.1 = (f32[1]{0:T(128)}, f32[1]{0:T(128)}, u32[]{:S(2)}, u32[]{:S(2)}) collective-permute-start(f32[1]{0:T(128)} %bitcast.12), channel_id=1, source_target_pairs={{0,1},{1,0},{2,3},{3,2},{4,5},{5,4},{6,7},{7,6},{8,9},{9,8},{10,11... | collective-permute-start | bytes 20 | tf_op jit(solution)/shard_map/ppermute | solution.py:198
  18.4 20.8 %copy-start.6 = (bf16[2,2,1,512,512]{4,3,2,1,0:T(8,128)(2,1)S(1)}, bf16[2,2,1,512,512]{4,3,2,1,0:T(8,128)(2,1)}, u32[]{:S(2)}) copy-start(bf16[2,2,1,512,512]{4,3,2,1,0:T(8,128)(2,1)} %param.11) | copy-start | bytes 6291460
  18.5 55.1 %collective-permute-start.17 = (bf16[2,512,512]{2,1,0:T(8,128)(2,1)S(1)}, bf16[2,512,512]{2,1,0:T(8,128)(2,1)S(1)}, u32[]{:S(2)}, u32[]{:S(2)}) collective-permute-start(bf16[2,512,512]{2,1,0:T(8,128)(2,1)S(1)} %pad_maximum_fusion.1.chip_map), channel_id=1, source_target_pairs={{2,4},{3,5},{4,6},{5,7},{10,12},{11,13},{12,14},{13,15},{18,20},{1... | collective-permute-start | bytes 3145736 | tf_op jit(solution)/shard_map/ppermute | solution.py:204
  19.3 54.2 %collective-permute-start.18 = (bf16[2,512,512]{2,1,0:T(8,128)(2,1)S(1)}, bf16[2,512,512]{2,1,0:T(8,128)(2,1)S(1)}, u32[]{:S(2)}, u32[]{:S(2)}) collective-permute-start(bf16[2,512,512]{2,1,0:T(8,128)(2,1)S(1)} %pad_maximum_fusion.1.chip_map), channel_id=1, source_target_pairs={{2,6},{3,7},{10,14},{11,15},{18,22},{19,23},{26,30},{27,31}} | collective-permute-start | bytes 3145736 | tf_op jit(solution)/shard_map/ppermute | solution.py:204
  21.4 10.2 %collective-permute-start.6 = (bf16[2,2,64,512]{3,2,1,0:T(8,128)(2,1)S(1)}, bf16[2,2,64,512]{3,2,1,0:T(8,128)(2,1)S(1)}, u32[]{:S(2)}, u32[]{:S(2)}) collective-permute-start(bf16[2,2,64,512]{3,2,1,0:T(8,128)(2,1)S(1)} %bitcast.69), channel_id=1, source_target_pairs={{0,24},{1,25},{2,26},{3,27},{4,28},{5,29},{6,30},{7,31},{8,0},{9,1... | collective-permute-start | bytes 786440 | tf_op jit(solution)/shard_map/ppermute | solution.py:198
  26.0 12.4 %collective-permute-start.10 = (bf16[2,64,512]{2,1,0:T(8,128)(2,1)S(1)}, bf16[2,64,512]{2,1,0:T(8,128)(2,1)S(1)}, u32[]{:S(2)}, u32[]{:S(2)}) collective-permute-start(bf16[2,64,512]{2,1,0:T(8,128)(2,1)S(1)} %get-tuple-element.21), channel_id=1, source_target_pairs={{0,1},{1,0},{2,3},{3,2},{4,5},{5,4},{6,7},{7,6},{8,9},{9,8},{10,11... | collective-permute-start | bytes 393224 | tf_op jit(solution)/shard_map/ppermute | solution.py:198
  36.6 5.6 %collective-permute-start.11 = (bf16[2,64,512]{2,1,0:T(8,128)(2,1)S(1)}, bf16[2,64,512]{2,1,0:T(8,128)(2,1)S(1)}, u32[]{:S(2)}, u32[]{:S(2)}) collective-permute-start(bf16[2,64,512]{2,1,0:T(8,128)(2,1)S(1)} %get-tuple-element.22), channel_id=1, source_target_pairs={{0,25},{1,24},{2,27},{3,26},{4,29},{5,28},{6,31},{7,30},{8,1},{9,0... | collective-permute-start | bytes 393224 | tf_op jit(solution)/shard_map/ppermute | solution.py:198
  38.4 12.5 %collective-permute-start.12 = (bf16[2,64,512]{2,1,0:T(8,128)(2,1)S(1)}, bf16[2,64,512]{2,1,0:T(8,128)(2,1)S(1)}, u32[]{:S(2)}, u32[]{:S(2)}) collective-permute-start(bf16[2,64,512]{2,1,0:T(8,128)(2,1)S(1)} %get-tuple-element.23), channel_id=1, source_target_pairs={{0,17},{1,16},{2,19},{3,18},{4,21},{5,20},{6,23},{7,22},{8,25},{9,... | collective-permute-start | bytes 393224 | tf_op jit(solution)/shard_map/ppermute | solution.py:198
  38.5 12.5 %collective-permute-start.13 = (bf16[2,64,512]{2,1,0:T(8,128)(2,1)S(1)}, bf16[2,64,512]{2,1,0:T(8,128)(2,1)S(1)}, u32[]{:S(2)}, u32[]{:S(2)}) collective-permute-start(bf16[2,64,512]{2,1,0:T(8,128)(2,1)S(1)} %get-tuple-element.24), channel_id=1, source_target_pairs={{0,9},{1,8},{2,11},{3,10},{4,13},{5,12},{6,15},{7,14},{8,17},{9,16... | collective-permute-start | bytes 393224 | tf_op jit(solution)/shard_map/ppermute | solution.py:198
  42.3 10.7 %collective-permute-start.7 = (bf16[2,64,512]{2,1,0:T(8,128)(2,1)S(1)}, bf16[2,64,512]{2,1,0:T(8,128)(2,1)S(1)}, u32[]{:S(2)}, u32[]{:S(2)}) collective-permute-start(bf16[2,64,512]{2,1,0:T(8,128)(2,1)S(1)} %get-tuple-element.18), channel_id=1, source_target_pairs={{0,24},{1,25},{2,26},{3,27},{4,28},{5,29},{6,30},{7,31},{8,0},{9,1... | collective-permute-start | bytes 393224 | tf_op jit(solution)/shard_map/ppermute | solution.py:198
  51.0 11.2 %collective-permute-start.8 = (bf16[2,64,512]{2,1,0:T(8,128)(2,1)S(1)}, bf16[2,64,512]{2,1,0:T(8,128)(2,1)S(1)}, u32[]{:S(2)}, u32[]{:S(2)}) collective-permute-start(bf16[2,64,512]{2,1,0:T(8,128)(2,1)S(1)} %get-tuple-element.19), channel_id=1, source_target_pairs={{0,16},{1,17},{2,18},{3,19},{4,20},{5,21},{6,22},{7,23},{8,24},{9,... | collective-permute-start | bytes 393224 | tf_op jit(solution)/shard_map/ppermute | solution.py:198
  51.0 11.2 %collective-permute-start.9 = (bf16[2,64,512]{2,1,0:T(8,128)(2,1)S(1)}, bf16[2,64,512]{2,1,0:T(8,128)(2,1)S(1)}, u32[]{:S(2)}, u32[]{:S(2)}) collective-permute-start(bf16[2,64,512]{2,1,0:T(8,128)(2,1)S(1)} %get-tuple-element.20), channel_id=1, source_target_pairs={{0,8},{1,9},{2,10},{3,11},{4,12},{5,13},{6,14},{7,15},{8,16},{9,17... | collective-permute-start | bytes 393224 | tf_op jit(solution)/shard_map/ppermute | solution.py:198
  64.2 7.5 %collective-permute-start.14 = (bf16[2,64,512]{2,1,0:T(8,128)(2,1)S(1)}, bf16[2,64,512]{2,1,0:T(8,128)(2,1)S(1)}, u32[]{:S(2)}, u32[]{:S(2)}) collective-permute-start(bf16[2,64,512]{2,1,0:T(8,128)(2,1)S(1)} %get-tuple-element.27), channel_id=1, source_target_pairs={{0,2},{1,3},{2,4},{3,5},{4,6},{5,7},{8,10},{9,11},{10,12},{11,13},... | collective-permute-start | bytes 393224 | tf_op jit(solution)/shard_map/ppermute | solution.py:204
  67.5 5.5 %collective-permute-start.15 = (bf16[2,64,512]{2,1,0:T(8,128)(2,1)S(1)}, bf16[2,64,512]{2,1,0:T(8,128)(2,1)S(1)}, u32[]{:S(2)}, u32[]{:S(2)}) collective-permute-start(bf16[2,64,512]{2,1,0:T(8,128)(2,1)S(1)} %get-tuple-element.27), channel_id=1, source_target_pairs={{0,4},{1,5},{2,6},{3,7},{8,12},{9,13},{10,14},{11,15},{16,20},{17,... | collective-permute-start | bytes 393224 | tf_op jit(solution)/shard_map/ppermute | solution.py:204
  70.3 3.2 %collective-permute-start.16 = (bf16[2,64,512]{2,1,0:T(8,128)(2,1)S(1)}, bf16[2,64,512]{2,1,0:T(8,128)(2,1)S(1)}, u32[]{:S(2)}, u32[]{:S(2)}) collective-permute-start(bf16[2,64,512]{2,1,0:T(8,128)(2,1)S(1)} %get-tuple-element.27), channel_id=1, source_target_pairs={{0,6},{1,7},{8,14},{9,15},{16,22},{17,23},{24,30},{25,31}} | collective-permute-start | bytes 393224 | tf_op jit(solution)/shard_map/ppermute | solution.py:204
  75.7 2.8 %collective-permute-start.19 = (bf16[2,64,512]{2,1,0:T(8,128)(2,1)S(1)}, bf16[2,64,512]{2,1,0:T(8,128)(2,1)S(1)}, u32[]{:S(2)}, u32[]{:S(2)}) collective-permute-start(bf16[2,64,512]{2,1,0:T(8,128)(2,1)S(1)} %get-tuple-element.29), channel_id=1, source_target_pairs={{0,1},{1,0},{2,3},{3,2},{4,5},{5,4},{6,7},{7,6},{8,9},{9,8},{10,11... | collective-permute-start | bytes 393224 | tf_op jit(solution)/shard_map/ppermute | solution.py:198

commit v2 on v1

v2 whole, which is shorter than its diff:
```python
import functools

import jax
import jax.numpy as jnp
from jax import lax
from jax.experimental import pallas as pl
from jax.experimental.pallas import tpu as pltpu
from jax.sharding import PartitionSpec as P

VMEM = pl.BlockSpec(memory_space=pltpu.VMEM)
SMEM = pl.BlockSpec(memory_space=pltpu.SMEM)
COST = 1000000000
F32, BF16 = jnp.float32, jnp.bfloat16


def call(kernel, name, outs, scalars, arrays, scratch=()):
    shapes = [jax.ShapeDtypeStruct(shape, kind) for shape, kind in outs]
    moved = sum(x.size * x.dtype.itemsize for x in list(arrays) + shapes)
    return pl.pallas_call(
        kernel,
        out_shape=shapes,
        in_specs=[SMEM] * len(scalars) + [VMEM] * len(arrays),
        out_specs=[VMEM] * len(outs),
        scratch_shapes=[pltpu.VMEM(shape, kind) for shape, kind in scratch],
        compiler_params=pltpu.CompilerParams(vmem_limit_bytes=16 << 20),
        cost_estimate=pl.CostEstimate(flops=COST, bytes_accessed=1, transcendentals=0),
        name=name,
    )(*scalars, *arrays)


def this_core():
    return lax.rem(lax.axis_index("wire"), 2)


def dot(lhs, rhs):
    return jnp.dot(lhs, rhs, preferred_element_type=F32)


def times(lhs, rhs):
    return (
        dot(lhs[0], rhs[0]) - dot(lhs[1], rhs[1]),
        dot(lhs[0], rhs[1]) + dot(lhs[1], rhs[0]),
    )


def pair(ref, *index):
    return ref[(0,) + index], ref[(1,) + index]


def weighted(slot, owner, whole, real_valued, wave_ref, g_ref, total):
    slots = g_ref.shape[1]
    energies = whole.shape[0] // 2
    group, target = lax.axis_index("energy"), owner * slots + slot
    total[...] = jnp.zeros_like(total)
    for block in range(slots):
        name = group * slots + block
        weight = jnp.where(whole[target] == name, real_valued[0], 0.0)
        weight += jnp.where(whole[energies + target] == name, real_valued[1], 0.0)

        @pl.when(weight != 0.0)
        def _():
            real, imag = times(pair(wave_ref, slot), pair(g_ref, block))
            total[0] += real * weight
            total[1] += imag * weight


def product_kernel(offset, whole, real_valued, wave_ref, g_ref, out_ref, total):
    group = lax.axis_index("energy")
    for slot in range(g_ref.shape[1]):
        weighted(slot, group ^ offset, whole, real_valued, wave_ref, g_ref, total)
        for c in range(2):
            out_ref[c, slot] = total[c].astype(BF16)


def own_kernel(whole, real_valued, wave_ref, g_ref, out_ref, total):
    group = lax.axis_index("energy")
    potential = real_valued[2 + whole[whole.shape[0] - 1]]
    for slot in range(g_ref.shape[1]):
        weighted(slot, group, whole, real_valued, wave_ref, g_ref, total)
        for c in range(2):
            out_ref[c, slot] = total[c] + potential * wave_ref[c, slot].astype(F32)


def term_kernel(base, *refs):
    parts, outs = refs[:-2], refs[-2:]
    core = this_core()
    for out_ref, slot in zip(outs, (core, 1 - core)):
        for c in range(2):
            total = base[c, slot]
            for part in parts:
                total = total + part[c, slot].astype(F32)
            out_ref[c] = total.astype(BF16)


def prepare_kernel(prop, prop_other, green, green_other, steps, greens, chip_map, arrived):
    core = this_core()
    copies = []
    for n, (source, target) in enumerate(((prop, steps), (prop_other, steps), (green, greens), (green_other, greens))):
        segment = core if n % 2 == 0 else 1 - core
        copies += [
            pltpu.make_async_copy(source.at[c, core], target.at[segment, c], arrived.at[n, c])
            for c in range(2)
        ]
    for copy in copies:
        copy.start()
    for copy in copies[:4]:
        copy.wait()
    second = (steps[1, 0], steps[1, 1])
    half = steps.shape[2] // 2
    for rows in (slice(0, half), slice(half, None)):
        moved = times((steps[0, 0, rows], steps[0, 1, rows]), second)
        for c in range(2):
            chip_map[c, rows] = moved[c].astype(BF16)
    for copy in copies[4:]:
        copy.wait()


def source_kernel(own, other, steps, greens, first_ref, chip_ref, send_ref, term):
    core = this_core()
    term[core], term[1 - core] = own[...], other[...]
    first = times((term[0, 0], term[0, 1]), (greens[0, 0], greens[0, 1]))
    first_ref[0], first_ref[1] = first
    rounded = (first[0].astype(BF16), first[1].astype(BF16))
    passed = times(rounded, (steps[1, 0], steps[1, 1]))
    added = times((term[1, 0], term[1, 1]), (greens[1, 0], greens[1, 1]))
    for c in range(2):
        chip = passed[c] + added[c]
        chip_ref[c] = chip
        send_ref[c] = chip.astype(BF16)


def chain_kernel(count, steps, chip_map, first, chip, *refs):
    waves, maps = refs[:count], refs[count : 2 * count - 1]
    own_ref, other_ref, keep = refs[2 * count - 1 :]
    core = this_core()
    entering = (waves[-1][0], waves[-1][1])
    for n in range(count - 2, -1, -1):
        moved = times(entering, (maps[n][0], maps[n][1]))
        entering = tuple((moved[c] + waves[n][c].astype(F32)).astype(BF16) for c in range(2))
    at_first = times(entering, (steps[0, 0], steps[0, 1]))
    at_second = times(entering, (chip_map[0], chip_map[1]))
    for c in range(2):
        keep[0, c] = (at_first[c] + first[c]).astype(BF16)
        keep[1, c] = (at_second[c] + chip[c]).astype(BF16)
    own_ref[...] = keep[core]
    other_ref[...] = keep[1 - core]


def across(lhs, rhs):
    return lax.dot_general(lhs, rhs, (((0,), (0,)), ((), ())), preferred_element_type=F32)


def block_kernel(counts, incident, own, other, scattered, green_next, both):
    core = this_core()
    modes = own.shape[1]
    for turn, chained in enumerate((own, other)):
        slot = core if turn == 0 else 1 - core
        live = slot < counts[0]
        for c in range(2):
            wave = chained[c].astype(F32)
            scattered[c, slot] = jnp.where(live, wave, 0.0).astype(BF16)
            combined = (incident[c, slot].astype(F32) + wave).astype(BF16)
            both[0, c * modes : (c + 1) * modes] = combined
            both[1, (1 - c) * modes : (2 - c) * modes] = -combined if c == 0 else combined
        stacked = both[0]
        real = across(both[1], stacked) / modes
        imag = across(stacked, stacked) / modes
        green_next[0, slot] = jnp.where(live, real, 0.0).astype(BF16)
        green_next[1, slot] = jnp.where(live, imag, 0.0).astype(BF16)


def complex_matrix(lhs, rhs):
    return jnp.stack(times(lhs, rhs))


def shards(groups, segments, g_prev, local_green, prop, incoming, plus_partner, minus_partner, counts, pot_index, levels, coupling):
    chips = segments // 2
    g_here, green_here = g_prev[:, :, 0], local_green[:, :, 0]
    prop_here, incident = prop[:, :, 0], incoming[:, :, 0]
    _, slots, modes, orbitals = incident.shape
    wave, block = (2, modes, orbitals), (2, orbitals, orbitals)

    def hbm(value):
        return pltpu.with_memory_space_constraint(value, pltpu.MemorySpace.HBM)

    def swap(value, offset, turn=0):
        pairs = [
            (e * segments + w, (e ^ offset) * segments + (w ^ turn))
            for e in range(groups)
            for w in range(segments)
        ]
        return lax.ppermute(value, ("energy", "wire"), pairs)

    def later(value, hops, least=0):
        pairs = []
        for chip in range(least, chips - hops):
            pairs += [(2 * chip + b, 2 * (chip + hops) + b) for b in range(2)]
        return lax.ppermute(value, "wire", pairs)

    scalars = [
        jnp.concatenate([plus_partner, minus_partner, pot_index]),
        jnp.concatenate([coupling, levels]),
    ]
    total = [(wave, F32)]
    every = (2, slots, modes, orbitals)

    waves = [incident] + [None] * (groups - 1)
    if True:
        for offset in range(1, groups):
            if offset == 1 or offset % 2 == 0:
                waves[offset] = swap(incident, offset)
        prop_other, green_other = swap(prop_here, 0, 1), swap(green_here, 0, 1)
        base = call(own_kernel, "own", [(every, F32)], scalars, [incident, g_here], total)[0]
        steps, greens, chip_map = pl.pallas_call(
            prepare_kernel,
            out_shape=[
                jax.ShapeDtypeStruct((2,) + block, BF16),
                jax.ShapeDtypeStruct((2,) + block, BF16),
                jax.ShapeDtypeStruct(block, BF16),
            ],
            in_specs=[pl.BlockSpec(memory_space=pltpu.MemorySpace.HBM), pl.BlockSpec(memory_space=pl.ANY)] * 2,
            out_specs=[VMEM] * 3,
            scratch_shapes=[pltpu.SemaphoreType.DMA((4, 2))],
            compiler_params=pltpu.CompilerParams(vmem_limit_bytes=16 << 20),
            cost_estimate=pl.CostEstimate(flops=COST, bytes_accessed=1, transcendentals=0),
            name="prepare",
        )(hbm(prop_here), prop_other, hbm(green_here), green_other)
    waves[1], waves[2], chip_map, base = lax.optimization_barrier((waves[1], waves[2], chip_map, base))
    for offset in range(3, groups, 2):
        waves[offset] = swap(waves[offset - 1], 1)

    back = []
    for offset in range(1, groups):
        part = call(
            functools.partial(product_kernel, offset), "product", [(every, BF16)], scalars, [waves[offset], g_here], total
        )[0]
        if offset == 1:
            part, waves[-1] = lax.optimization_barrier((part, waves[-1]))
        if offset == 2:
            part, chip_map = lax.optimization_barrier((part, chip_map))
        back.append(swap(part, offset))
    own, other = call(term_kernel, "term", [(wave, BF16)] * 2, [], [base] + back)
    other = swap(other, 0, 1)

    first, chip, chip_send = call(
        source_kernel,
        "source",
        [(wave, F32), (wave, F32), (wave, BF16)],
        [],
        [own, other, steps, greens],
        [((2,) + wave, BF16)])
    if chips <= 4:
        maps = [later(chip_map, hops, 1) for hops in range(1, chips - 1)]
        arrived = [later(chip_send, hops) for hops in range(1, chips)]
    else:
        maps = []
        entering = jnp.zeros_like(chip_send)
        for at in range(chips - 1):
            leaving = (complex_matrix(entering, chip_map) + chip).astype(BF16)
            pairs = [(2 * at + b, 2 * at + 2 + b) for b in range(2)]
            entering = entering + lax.ppermute(leaving, "wire", pairs)
        arrived = [entering]
    own, other = call(
        functools.partial(chain_kernel, len(arrived)),
        "chain",
        [(wave, BF16)] * 2,
        [],
        [steps, chip_map, first, chip] + arrived + maps,
        [((2,) + wave, BF16)])

    other = swap(other, 0, 1)
    scattered, green_next = call(
        block_kernel,
        "green_blocks",
        [((2, slots, modes, orbitals), BF16), ((2, slots, orbitals, orbitals), BF16)],
        [counts],
        [incident, own, other],
        [((2, 2 * modes, orbitals), BF16)])
    return scattered[:, :, None], green_next[:, :, None]


def solution(mesh):
    placed = P(None, "energy", "wire", None, None)
    return jax.shard_map(
        functools.partial(shards, mesh.shape["energy"], mesh.shape["wire"]),
        mesh=mesh,
        in_specs=(placed,) * 4 + (P(), P(), P("energy"), P("wire"), P(), P()),
        out_specs=(placed, placed),
        check_vma=False,
    )
```

time: 81.9 us -> 66.5 us (0.81)
  the two profiles are of different devices: /device:TPU:1 before, /device:TPU:15 now
where the time goes in v2:
time: 66.5 us; the launch traced here: 66.3 us
  waiting for transfers between devices  30.6 us (46%)
  starting transfers between devices  17.8 us (27%)
  Pallas kernels  11.7 us (18%)
  local copies, waits for them, and re-layouts  2.55 us (4%)
  between operations  2.07 us (3%)
  other arithmetic  1.49 us (2%)
    ppermute x10, waiting for transfers between devices, swap(): return lax.ppermute(value, ('energy', 'wire'), pairs)  23.6 us
    ppermute x10, starting transfers between devices, swap(): return lax.ppermute(value, ('energy', 'wire'), pairs)  11.4 us
    pallas_call x8, Pallas kernels, call(): pl.pallas_call(kernel, out_shape=shapes, in_specs=[SMEM] * len(scalars) +...  9 us
    ppermute x5, waiting for transfers between devices, later(): return lax.ppermute(value, 'wire', pairs)  7.09 us
    ppermute x5, starting transfers between devices, later(): return lax.ppermute(value, 'wire', pairs)  6.46 us
    pallas_call x1, Pallas kernels, shards(): pl.pallas_call(prepare_kernel, out_shape=[jax.ShapeDtypeStruct((2,) + blo...  2.69 us
    unnamed x8, local copies, waits for them, and re-layouts  2.55 us
  transfers between devices with their start and end apart: 15, of which 10 were waited for; matrix products, arithmetic and copies ran while one was open for 2% of the time, Pallas kernels for 12%

profile of v2, /device:TPU:15, one launch (start us, length us, event | category | flops | bytes accessed | tf_op | source)
XLA Modules:
  0.0 66.3 jit_solution(16707462941451535157)
XLA Ops:
  0.6 0.7 %collective-permute-start = (bf16[2,2,512,512]{3,2,1,0:T(8,128)(2,1)}, bf16[2,2,512,512]{3,2,1,0:T(8,128)(2,1)S(1)}, u32[]{:S(2)}, u32[]{:S(2)}) collective-permute-start(bf16[2,2,512,512]{3,2,1,0:T(8,128)(2,1)} %bitcast.18), channel_id=1, source_target_pairs={{0,1},{1,0},{2,3},{3,2},{4,5},{5,4},{6,7},{7,6},{8,9},{9,8},{10,11... | collective-permute-start | bytes 6291464 | tf_op jit(solution)/shard_map/ppermute | solution.py:192
  1.4 0.1 collective-permute-start.1
  1.5 0.2 collective-permute-start.2
  1.6 2.3 %collective-permute-start.3 = (bf16[2,2,64,512]{3,2,1,0:T(8,128)(2,1)}, bf16[2,2,64,512]{3,2,1,0:T(8,128)(2,1)S(1)}, u32[]{:S(2)}, u32[]{:S(2)}) collective-permute-start(bf16[2,2,64,512]{3,2,1,0:T(8,128)(2,1)} %bitcast.15), channel_id=1, source_target_pairs={{0,16},{1,17},{2,18},{3,19},{4,20},{5,21},{6,22},{7,23},{8,24},{9,... | collective-permute-start | bytes 786440 | tf_op jit(solution)/shard_map/ppermute | solution.py:192
  4.6 0.7 %pad_maximum_fusion.real_valued = f32[18]{0:T(128)S(1)} fusion(f32[16]{0:T(128)} %param.18, f32[2]{0:T(128)} %param.19), kind=kLoop, calls=%fused_computation.1 | loop fusion | flops 18 | bytes 144 | tf_op jit(solution)/shard_map/concatenate | solution.py:202
  5.3 0.7 %pad_add_fusion.whole = s32[17]{0:T(128)S(1)} fusion(s32[1]{0:T(128)S(6)} %copy.15, s32[8]{0:T(128)} %param.15, s32[8]{0:T(128)} %param.14), kind=kLoop, calls=%fused_computation | loop fusion | flops 34 | bytes 136 | tf_op jit(solution)/shard_map/concatenate | solution.py:201
  6.1 0.0 copy-start
  6.1 1.6 %copy-done = bf16[2,2,1,512,512]{4,3,2,1,0:T(8,128)(2,1)S(1)} copy-done((bf16[2,2,1,512,512]{4,3,2,1,0:T(8,128)(2,1)S(1)}, bf16[2,2,1,512,512]{4,3,2,1,0:T(8,128)(2,1)}, u32[]{:S(2)}) %copy-start) | copy-done | bytes 2097176
  7.7 0.0 copy-start.2
  7.7 0.9 %copy-done.2 = bf16[2,2,1,64,512]{4,3,2,1,0:T(8,128)(2,1)S(1)} copy-done((bf16[2,2,1,64,512]{4,3,2,1,0:T(8,128)(2,1)S(1)}, bf16[2,2,1,64,512]{4,3,2,1,0:T(8,128)(2,1)}, u32[]{:S(2)}) %copy-start.2) | copy-done | bytes 262168
  8.6 1.1 %own.1.base = f32[2,2,64,512]{3,2,1,0:T(8,128)S(1)} custom-call(s32[17]{0:T(128)S(1)} %pad_add_fusion.whole, f32[18]{0:T(128)S(1)} %pad_maximum_fusion.real_valued, bf16[2,2,64,512]{3,2,1,0:T(8,128)(2,1)S(1)} %bitcast.16, bf16[2,2,512,512]{3,2,1,0:T(8,128)(2,1)S(1)} %bitcast.10), custom_call_target="tpu_custom_call" | custom-call | flops 1000000000 | bytes 1 | tf_op jit(solution)/shard_map/own/pallas_call | solution.py:19
  9.8 0.0 copy-start.1
  9.8 0.0 collective-permute-done.prop_other
  9.8 0.0 collective-permute-done.1.green_other
  9.8 2.7 %prepare.1 = (bf16[2,2,512,512]{3,2,1,0:T(8,128)(2,1)S(1)}, bf16[2,2,512,512]{3,2,1,0:T(8,128)(2,1)S(1)}, bf16[2,512,512]{2,1,0:T(8,128)(2,1)S(1)}) custom-call(bf16[2,2,512,512]{3,2,1,0:T(8,128)(2,1)} %bitcast.19, bf16[2,2,512,512]{3,2,1,0:T(8,128)(2,1)S(1)} %collective-permute-done.prop_other, bf16[2,2,512,512]{3,2,1,0:T(8,128)(2,1)} %bitcast.21, ...), custom_call_target="tpu_custom_call" | custom-call | flops 1000000000 | bytes 1 | tf_op jit(solution)/shard_map/prepare/pallas_call | solution.py:214
  12.5 0.2 collective-permute-done.2.wave_ref
  12.7 3.1 %collective-permute-done.3.wave_ref = bf16[2,2,64,512]{3,2,1,0:T(8,128)(2,1)S(1)} collective-permute-done((bf16[2,2,64,512]{3,2,1,0:T(8,128)(2,1)}, bf16[2,2,64,512]{3,2,1,0:T(8,128)(2,1)S(1)}, u32[]{:S(2)}, u32[]{:S(2)}) %collective-permute-start.3) | collective-permute-done | bytes 262176 | tf_op jit(solution)/shard_map/ppermute | solution.py:192
  15.8 0.0 collective-permute-start.4
  15.8 0.0 copy-done.1
  15.8 0.6 product.3
  16.4 1.3 %collective-permute-start.12 = (bf16[2,512,512]{2,1,0:T(8,128)(2,1)S(1)}, bf16[2,512,512]{2,1,0:T(8,128)(2,1)S(1)}, u32[]{:S(2)}, u32[]{:S(2)}) collective-permute-start(bf16[2,512,512]{2,1,0:T(8,128)(2,1)S(1)} %get-tuple-element.26.chip_map), channel_id=1, source_target_pairs={{2,4},{3,5},{4,6},{5,7},{10,12},{11,13},{12,14},{13,15},{18,20},{1... | collective-permute-start | bytes 3145736 | tf_op jit(solution)/shard_map/ppermute | solution.py:198
  17.7 1.3 %collective-permute-start.13 = (bf16[2,512,512]{2,1,0:T(8,128)(2,1)S(1)}, bf16[2,512,512]{2,1,0:T(8,128)(2,1)S(1)}, u32[]{:S(2)}, u32[]{:S(2)}) collective-permute-start(bf16[2,512,512]{2,1,0:T(8,128)(2,1)S(1)} %get-tuple-element.26.chip_map), channel_id=1, source_target_pairs={{2,6},{3,7},{10,14},{11,15},{18,22},{19,23},{26,30},{27,31}} | collective-permute-start | bytes 3145736 | tf_op jit(solution)/shard_map/ppermute | solution.py:198
  19.0 2.6 %collective-permute-start.6 = (bf16[2,2,64,512]{3,2,1,0:T(8,128)(2,1)S(1)}, bf16[2,2,64,512]{3,2,1,0:T(8,128)(2,1)S(1)}, u32[]{:S(2)}, u32[]{:S(2)}) collective-permute-start(bf16[2,2,64,512]{3,2,1,0:T(8,128)(2,1)S(1)} %product.3), channel_id=1, source_target_pairs={{0,16},{1,17},{2,18},{3,19},{4,20},{5,21},{6,22},{7,23},{8,24},{9,... | collective-permute-start | bytes 786440 | tf_op jit(solution)/shard_map/ppermute | solution.py:192
  21.7 1.1 %product.4 = bf16[2,2,64,512]{3,2,1,0:T(8,128)(2,1)S(1)} custom-call(s32[17]{0:T(128)S(1)} %pad_add_fusion.whole, f32[18]{0:T(128)S(1)} %pad_maximum_fusion.real_valued, bf16[2,2,64,512]{3,2,1,0:T(8,128)(2,1)S(1)} %collective-permute-done.2.wave_ref, bf16[2,2,512,512]{3,2,1,0:T(8,128)(2,1)S(1)} %bitcast.12), custom_call_target="tpu_custom_call" | custom-call | flops 1000000000 | bytes 1 | tf_op jit(solution)/shard_map/product/pallas_call | solution.py:19
  22.8 0.0 collective-permute-done.4.wave_ref
  22.8 1.5 %collective-permute-start.5 = (bf16[2,2,64,512]{3,2,1,0:T(8,128)(2,1)S(1)}, bf16[2,2,64,512]{3,2,1,0:T(8,128)(2,1)S(1)}, u32[]{:S(2)}, u32[]{:S(2)}) collective-permute-start(bf16[2,2,64,512]{3,2,1,0:T(8,128)(2,1)S(1)} %product.4), channel_id=1, source_target_pairs={{0,8},{1,9},{2,10},{3,11},{4,12},{5,13},{6,14},{7,15},{8,0},{9,1},... | collective-permute-start | bytes 786440 | tf_op jit(solution)/shard_map/ppermute | solution.py:192
  24.3 1.1 %product.5 = bf16[2,2,64,512]{3,2,1,0:T(8,128)(2,1)S(1)} custom-call(s32[17]{0:T(128)S(1)} %pad_add_fusion.whole, f32[18]{0:T(128)S(1)} %pad_maximum_fusion.real_valued, bf16[2,2,64,512]{3,2,1,0:T(8,128)(2,1)S(1)} %collective-permute-done.4.wave_ref, bf16[2,2,512,512]{3,2,1,0:T(8,128)(2,1)S(1)} %bitcast.13), custom_call_target="tpu_custom_call" | custom-call | flops 1000000000 | bytes 1 | tf_op jit(solution)/shard_map/product/pallas_call | solution.py:19
  25.4 0.2 collective-permute-start.7
  25.6 6.6 %collective-permute-done.6.refs_1_ = bf16[2,2,64,512]{3,2,1,0:T(8,128)(2,1)S(1)} collective-permute-done((bf16[2,2,64,512]{3,2,1,0:T(8,128)(2,1)S(1)}, bf16[2,2,64,512]{3,2,1,0:T(8,128)(2,1)S(1)}, u32[]{:S(2)}, u32[]{:S(2)}) %collective-permute-start.6) | collective-permute-done | bytes 262176 | tf_op jit(solution)/shard_map/ppermute | solution.py:192
  32.2 1.2 %collective-permute-done.5.refs_0_ = bf16[2,2,64,512]{3,2,1,0:T(8,128)(2,1)S(1)} collective-permute-done((bf16[2,2,64,512]{3,2,1,0:T(8,128)(2,1)S(1)}, bf16[2,2,64,512]{3,2,1,0:T(8,128)(2,1)S(1)}, u32[]{:S(2)}, u32[]{:S(2)}) %collective-permute-start.5) | collective-permute-done | bytes 262176 | tf_op jit(solution)/shard_map/ppermute | solution.py:192
  33.3 11.2 %collective-permute-done.7.refs_2_ = bf16[2,2,64,512]{3,2,1,0:T(8,128)(2,1)S(1)} collective-permute-done((bf16[2,2,64,512]{3,2,1,0:T(8,128)(2,1)S(1)}, bf16[2,2,64,512]{3,2,1,0:T(8,128)(2,1)S(1)}, u32[]{:S(2)}, u32[]{:S(2)}) %collective-permute-start.7) | collective-permute-done | bytes 262176 | tf_op jit(solution)/shard_map/ppermute | solution.py:192
  44.5 0.1 term.1
  44.6 1.5 %collective-permute-start.8 = (bf16[2,64,512]{2,1,0:T(8,128)(2,1)S(1)}, bf16[2,64,512]{2,1,0:T(8,128)(2,1)S(1)}, u32[]{:S(2)}, u32[]{:S(2)}) collective-permute-start(bf16[2,64,512]{2,1,0:T(8,128)(2,1)S(1)} %get-tuple-element.33), channel_id=1, source_target_pairs={{0,1},{1,0},{2,3},{3,2},{4,5},{5,4},{6,7},{7,6},{8,9},{9,8},{10,11... | collective-permute-start | bytes 393224 | tf_op jit(solution)/shard_map/ppermute | solution.py:192
  46.2 1.0 %collective-permute-done.8.other = bf16[2,64,512]{2,1,0:T(8,128)(2,1)S(1)} collective-permute-done((bf16[2,64,512]{2,1,0:T(8,128)(2,1)S(1)}, bf16[2,64,512]{2,1,0:T(8,128)(2,1)S(1)}, u32[]{:S(2)}, u32[]{:S(2)}) %collective-permute-start.8) | collective-permute-done | bytes 131104 | tf_op jit(solution)/shard_map/ppermute | solution.py:192
  47.1 1.2 %source.1 = (f32[2,64,512]{2,1,0:T(8,128)S(1)}, f32[2,64,512]{2,1,0:T(8,128)S(1)}, bf16[2,64,512]{2,1,0:T(8,128)(2,1)S(1)}) custom-call(bf16[2,64,512]{2,1,0:T(8,128)(2,1)S(1)} %get-tuple-element.32.own, bf16[2,64,512]{2,1,0:T(8,128)(2,1)S(1)} %collective-permute-done.8.other, bf16[2,2,512,512]{3,2,1,0:T(8,128)(2,1)S(1)} %get-tuple-element.22.steps, ...), custom_call_target="tpu_custom_call" | custom-call | flops 1000000000 | bytes 1 | tf_op jit(solution)/shard_map/source/pallas_call | solution.py:19
  48.4 1.3 %collective-permute-start.9 = (bf16[2,64,512]{2,1,0:T(8,128)(2,1)S(1)}, bf16[2,64,512]{2,1,0:T(8,128)(2,1)S(1)}, u32[]{:S(2)}, u32[]{:S(2)}) collective-permute-start(bf16[2,64,512]{2,1,0:T(8,128)(2,1)S(1)} %get-tuple-element.37), channel_id=1, source_target_pairs={{0,2},{1,3},{2,4},{3,5},{4,6},{5,7},{8,10},{9,11},{10,12},{11,13},... | collective-permute-start | bytes 393224 | tf_op jit(solution)/shard_map/ppermute | solution.py:198
  49.7 1.3 %collective-permute-start.10 = (bf16[2,64,512]{2,1,0:T(8,128)(2,1)S(1)}, bf16[2,64,512]{2,1,0:T(8,128)(2,1)S(1)}, u32[]{:S(2)}, u32[]{:S(2)}) collective-permute-start(bf16[2,64,512]{2,1,0:T(8,128)(2,1)S(1)} %get-tuple-element.37), channel_id=1, source_target_pairs={{0,4},{1,5},{2,6},{3,7},{8,12},{9,13},{10,14},{11,15},{16,20},{17,... | collective-permute-start | bytes 393224 | tf_op jit(solution)/shard_map/ppermute | solution.py:198
  51.0 1.3 %collective-permute-start.11 = (bf16[2,64,512]{2,1,0:T(8,128)(2,1)S(1)}, bf16[2,64,512]{2,1,0:T(8,128)(2,1)S(1)}, u32[]{:S(2)}, u32[]{:S(2)}) collective-permute-start(bf16[2,64,512]{2,1,0:T(8,128)(2,1)S(1)} %get-tuple-element.37), channel_id=1, source_target_pairs={{0,6},{1,7},{8,14},{9,15},{16,22},{17,23},{24,30},{25,31}} | collective-permute-start | bytes 393224 | tf_op jit(solution)/shard_map/ppermute | solution.py:198
  52.3 2.8 %collective-permute-done.9.refs_0_ = bf16[2,64,512]{2,1,0:T(8,128)(2,1)S(1)} collective-permute-done((bf16[2,64,512]{2,1,0:T(8,128)(2,1)S(1)}, bf16[2,64,512]{2,1,0:T(8,128)(2,1)S(1)}, u32[]{:S(2)}, u32[]{:S(2)}) %collective-permute-start.9) | collective-permute-done | bytes 131104 | tf_op jit(solution)/shard_map/ppermute | solution.py:198
  55.1 2.4 %collective-permute-done.10.refs_1_ = bf16[2,64,512]{2,1,0:T(8,128)(2,1)S(1)} collective-permute-done((bf16[2,64,512]{2,1,0:T(8,128)(2,1)S(1)}, bf16[2,64,512]{2,1,0:T(8,128)(2,1)S(1)}, u32[]{:S(2)}, u32[]{:S(2)}) %collective-permute-start.10) | collective-permute-done | bytes 131104 | tf_op jit(solution)/shard_map/ppermute | solution.py:198
  57.5 1.8 %collective-permute-done.11.refs_2_ = bf16[2,64,512]{2,1,0:T(8,128)(2,1)S(1)} collective-permute-done((bf16[2,64,512]{2,1,0:T(8,128)(2,1)S(1)}, bf16[2,64,512]{2,1,0:T(8,128)(2,1)S(1)}, u32[]{:S(2)}, u32[]{:S(2)}) %collective-permute-start.11) | collective-permute-done | bytes 131104 | tf_op jit(solution)/shard_map/ppermute | solution.py:198
  59.4 0.0 collective-permute-done.12.refs_3_
  59.4 0.0 collective-permute-done.13.refs_4_
  59.4 0.0 copy-start.3
  59.4 1.6 %chain.1 = (bf16[2,64,512]{2,1,0:T(8,128)(2,1)S(1)}, bf16[2,64,512]{2,1,0:T(8,128)(2,1)S(1)}) custom-call(bf16[2,2,512,512]{3,2,1,0:T(8,128)(2,1)S(1)} %get-tuple-element.22.steps, bf16[2,512,512]{2,1,0:T(8,128)(2,1)S(1)} %get-tuple-element.26.chip_map, f32[2,64,512]{2,1,0:T(8,128)S(1)} %get-tuple-element.35.first, ...), custom_call_target="tpu_custom_call" | custom-call | flops 1000000000 | bytes 1 | tf_op jit(solution)/shard_map/chain/pallas_call | solution.py:19
  61.0 2.2 %collective-permute-start.14 = (bf16[2,64,512]{2,1,0:T(8,128)(2,1)S(1)}, bf16[2,64,512]{2,1,0:T(8,128)(2,1)S(1)}, u32[]{:S(2)}, u32[]{:S(2)}) collective-permute-start(bf16[2,64,512]{2,1,0:T(8,128)(2,1)S(1)} %get-tuple-element.39), channel_id=1, source_target_pairs={{0,1},{1,0},{2,3},{3,2},{4,5},{5,4},{6,7},{7,6},{8,9},{9,8},{10,11... | collective-permute-start | bytes 393224 | tf_op jit(solution)/shard_map/ppermute | solution.py:192
  63.9 0.3 collective-permute-done.14.other
  64.2 0.0 copy-done.3
  64.2 2.1 %green_blocks.1 = (bf16[2,2,64,512]{3,2,1,0:T(8,128)(2,1)}, bf16[2,2,512,512]{3,2,1,0:T(8,128)(2,1)}) custom-call(s32[1]{0:T(128)S(6)} %copy.14.counts, bf16[2,2,64,512]{3,2,1,0:T(8,128)(2,1)S(1)} %bitcast.17, bf16[2,64,512]{2,1,0:T(8,128)(2,1)S(1)} %get-tuple-element.38.own, bf16[2,64,512]{2,1,0:T(8,128)(2,1)S(1)} %collective-permute-done.14.other), custom_call_target="tpu_custom_call" | custom-call | flops 1000000000 | bytes 1 | tf_op jit(solution)/shard_map/green_blocks/pallas_call | solution.py:19
Async XLA Ops:
  0.6 9.1 %collective-permute-start = (bf16[2,2,512,512]{3,2,1,0:T(8,128)(2,1)}, bf16[2,2,512,512]{3,2,1,0:T(8,128)(2,1)S(1)}, u32[]{:S(2)}, u32[]{:S(2)}) collective-permute-start(bf16[2,2,512,512]{3,2,1,0:T(8,128)(2,1)} %bitcast.18), channel_id=1, source_target_pairs={{0,1},{1,0},{2,3},{3,2},{4,5},{5,4},{6,7},{7,6},{8,9},{9,8},{10,11... | collective-permute-start | bytes 6291464 | tf_op jit(solution)/shard_map/ppermute | solution.py:192
  1.4 8.4 %collective-permute-start.1 = (bf16[2,2,512,512]{3,2,1,0:T(8,128)(2,1)}, bf16[2,2,512,512]{3,2,1,0:T(8,128)(2,1)S(1)}, u32[]{:S(2)}, u32[]{:S(2)}) collective-permute-start(bf16[2,2,512,512]{3,2,1,0:T(8,128)(2,1)} %bitcast.20), channel_id=1, source_target_pairs={{0,1},{1,0},{2,3},{3,2},{4,5},{5,4},{6,7},{7,6},{8,9},{9,8},{10,11... | collective-permute-start | bytes 6291464 | tf_op jit(solution)/shard_map/ppermute | solution.py:192
  1.5 11.2 %collective-permute-start.2 = (bf16[2,2,64,512]{3,2,1,0:T(8,128)(2,1)}, bf16[2,2,64,512]{3,2,1,0:T(8,128)(2,1)S(1)}, u32[]{:S(2)}, u32[]{:S(2)}) collective-permute-start(bf16[2,2,64,512]{3,2,1,0:T(8,128)(2,1)} %bitcast.14), channel_id=1, source_target_pairs={{0,8},{1,9},{2,10},{3,11},{4,12},{5,13},{6,14},{7,15},{8,0},{9,1},... | collective-permute-start | bytes 786440 | tf_op jit(solution)/shard_map/ppermute | solution.py:192
  1.6 14.2 %collective-permute-start.3 = (bf16[2,2,64,512]{3,2,1,0:T(8,128)(2,1)}, bf16[2,2,64,512]{3,2,1,0:T(8,128)(2,1)S(1)}, u32[]{:S(2)}, u32[]{:S(2)}) collective-permute-start(bf16[2,2,64,512]{3,2,1,0:T(8,128)(2,1)} %bitcast.15), channel_id=1, source_target_pairs={{0,16},{1,17},{2,18},{3,19},{4,20},{5,21},{6,22},{7,23},{8,24},{9,... | collective-permute-start | bytes 786440 | tf_op jit(solution)/shard_map/ppermute | solution.py:192
  6.1 1.6 %copy-start = (bf16[2,2,1,512,512]{4,3,2,1,0:T(8,128)(2,1)S(1)}, bf16[2,2,1,512,512]{4,3,2,1,0:T(8,128)(2,1)}, u32[]{:S(2)}) copy-start(bf16[2,2,1,512,512]{4,3,2,1,0:T(8,128)(2,1)} %param.10) | copy-start | bytes 6291460
  7.7 0.9 %copy-start.2 = (bf16[2,2,1,64,512]{4,3,2,1,0:T(8,128)(2,1)S(1)}, bf16[2,2,1,64,512]{4,3,2,1,0:T(8,128)(2,1)}, u32[]{:S(2)}) copy-start(bf16[2,2,1,64,512]{4,3,2,1,0:T(8,128)(2,1)} %param.13) | copy-start | bytes 786436
  9.8 6.0 %copy-start.1 = (bf16[2,2,1,512,512]{4,3,2,1,0:T(8,128)(2,1)S(1)}, bf16[2,2,1,512,512]{4,3,2,1,0:T(8,128)(2,1)}, u32[]{:S(2)}) copy-start(bf16[2,2,1,512,512]{4,3,2,1,0:T(8,128)(2,1)} %param.10) | copy-start | bytes 6291460
  15.8 7.0 %collective-permute-start.4 = (bf16[2,2,64,512]{3,2,1,0:T(8,128)(2,1)S(1)}, bf16[2,2,64,512]{3,2,1,0:T(8,128)(2,1)S(1)}, u32[]{:S(2)}, u32[]{:S(2)}) collective-permute-start(bf16[2,2,64,512]{3,2,1,0:T(8,128)(2,1)S(1)} %collective-permute-done.3.wave_ref), channel_id=1, source_target_pairs={{0,8},{1,9},{2,10},{3,11},{4,12},{5,13},{6,14},{7,15},{8,0},{9,1},... | collective-permute-start | bytes 786440 | tf_op jit(solution)/shard_map/ppermute | solution.py:192
  16.4 42.9 %collective-permute-start.12 = (bf16[2,512,512]{2,1,0:T(8,128)(2,1)S(1)}, bf16[2,512,512]{2,1,0:T(8,128)(2,1)S(1)}, u32[]{:S(2)}, u32[]{:S(2)}) collective-permute-start(bf16[2,512,512]{2,1,0:T(8,128)(2,1)S(1)} %get-tuple-element.26.chip_map), channel_id=1, source_target_pairs={{2,4},{3,5},{4,6},{5,7},{10,12},{11,13},{12,14},{13,15},{18,20},{1... | collective-permute-start | bytes 3145736 | tf_op jit(solution)/shard_map/ppermute | solution.py:198
  17.7 41.6 %collective-permute-start.13 = (bf16[2,512,512]{2,1,0:T(8,128)(2,1)S(1)}, bf16[2,512,512]{2,1,0:T(8,128)(2,1)S(1)}, u32[]{:S(2)}, u32[]{:S(2)}) collective-permute-start(bf16[2,512,512]{2,1,0:T(8,128)(2,1)S(1)} %get-tuple-element.26.chip_map), channel_id=1, source_target_pairs={{2,6},{3,7},{10,14},{11,15},{18,22},{19,23},{26,30},{27,31}} | collective-permute-start | bytes 3145736 | tf_op jit(solution)/shard_map/ppermute | solution.py:198
  19.0 13.1 %collective-permute-start.6 = (bf16[2,2,64,512]{3,2,1,0:T(8,128)(2,1)S(1)}, bf16[2,2,64,512]{3,2,1,0:T(8,128)(2,1)S(1)}, u32[]{:S(2)}, u32[]{:S(2)}) collective-permute-start(bf16[2,2,64,512]{3,2,1,0:T(8,128)(2,1)S(1)} %product.3), channel_id=1, source_target_pairs={{0,16},{1,17},{2,18},{3,19},{4,20},{5,21},{6,22},{7,23},{8,24},{9,... | collective-permute-start | bytes 786440 | tf_op jit(solution)/shard_map/ppermute | solution.py:192
  22.8 10.6 %collective-permute-start.5 = (bf16[2,2,64,512]{3,2,1,0:T(8,128)(2,1)S(1)}, bf16[2,2,64,512]{3,2,1,0:T(8,128)(2,1)S(1)}, u32[]{:S(2)}, u32[]{:S(2)}) collective-permute-start(bf16[2,2,64,512]{3,2,1,0:T(8,128)(2,1)S(1)} %product.4), channel_id=1, source_target_pairs={{0,8},{1,9},{2,10},{3,11},{4,12},{5,13},{6,14},{7,15},{8,0},{9,1},... | collective-permute-start | bytes 786440 | tf_op jit(solution)/shard_map/ppermute | solution.py:192
  25.4 19.1 %collective-permute-start.7 = (bf16[2,2,64,512]{3,2,1,0:T(8,128)(2,1)S(1)}, bf16[2,2,64,512]{3,2,1,0:T(8,128)(2,1)S(1)}, u32[]{:S(2)}, u32[]{:S(2)}) collective-permute-start(bf16[2,2,64,512]{3,2,1,0:T(8,128)(2,1)S(1)} %product.5), channel_id=1, source_target_pairs={{0,24},{1,25},{2,26},{3,27},{4,28},{5,29},{6,30},{7,31},{8,16},{9,... | collective-permute-start | bytes 786440 | tf_op jit(solution)/shard_map/ppermute | solution.py:192
  44.6 2.5 %collective-permute-start.8 = (bf16[2,64,512]{2,1,0:T(8,128)(2,1)S(1)}, bf16[2,64,512]{2,1,0:T(8,128)(2,1)S(1)}, u32[]{:S(2)}, u32[]{:S(2)}) collective-permute-start(bf16[2,64,512]{2,1,0:T(8,128)(2,1)S(1)} %get-tuple-element.33), channel_id=1, source_target_pairs={{0,1},{1,0},{2,3},{3,2},{4,5},{5,4},{6,7},{7,6},{8,9},{9,8},{10,11... | collective-permute-start | bytes 393224 | tf_op jit(solution)/shard_map/ppermute | solution.py:192
  48.4 6.7 %collective-permute-start.9 = (bf16[2,64,512]{2,1,0:T(8,128)(2,1)S(1)}, bf16[2,64,512]{2,1,0:T(8,128)(2,1)S(1)}, u32[]{:S(2)}, u32[]{:S(2)}) collective-permute-start(bf16[2,64,512]{2,1,0:T(8,128)(2,1)S(1)} %get-tuple-element.37), channel_id=1, source_target_pairs={{0,2},{1,3},{2,4},{3,5},{4,6},{5,7},{8,10},{9,11},{10,12},{11,13},... | collective-permute-start | bytes 393224 | tf_op jit(solution)/shard_map/ppermute | solution.py:198
  49.7 7.8 %collective-permute-start.10 = (bf16[2,64,512]{2,1,0:T(8,128)(2,1)S(1)}, bf16[2,64,512]{2,1,0:T(8,128)(2,1)S(1)}, u32[]{:S(2)}, u32[]{:S(2)}) collective-permute-start(bf16[2,64,512]{2,1,0:T(8,128)(2,1)S(1)} %get-tuple-element.37), channel_id=1, source_target_pairs={{0,4},{1,5},{2,6},{3,7},{8,12},{9,13},{10,14},{11,15},{16,20},{17,... | collective-permute-start | bytes 393224 | tf_op jit(solution)/shard_map/ppermute | solution.py:198
  51.0 8.4 %collective-permute-start.11 = (bf16[2,64,512]{2,1,0:T(8,128)(2,1)S(1)}, bf16[2,64,512]{2,1,0:T(8,128)(2,1)S(1)}, u32[]{:S(2)}, u32[]{:S(2)}) collective-permute-start(bf16[2,64,512]{2,1,0:T(8,128)(2,1)S(1)} %get-tuple-element.37), channel_id=1, source_target_pairs={{0,6},{1,7},{8,14},{9,15},{16,22},{17,23},{24,30},{25,31}} | collective-permute-start | bytes 393224 | tf_op jit(solution)/shard_map/ppermute | solution.py:198
  59.4 4.8 %copy-start.3 = (bf16[2,2,1,64,512]{4,3,2,1,0:T(8,128)(2,1)S(1)}, bf16[2,2,1,64,512]{4,3,2,1,0:T(8,128)(2,1)}, u32[]{:S(2)}) copy-start(bf16[2,2,1,64,512]{4,3,2,1,0:T(8,128)(2,1)} %param.13) | copy-start | bytes 786436
  61.0 3.2 %collective-permute-start.14 = (bf16[2,64,512]{2,1,0:T(8,128)(2,1)S(1)}, bf16[2,64,512]{2,1,0:T(8,128)(2,1)S(1)}, u32[]{:S(2)}, u32[]{:S(2)}) collective-permute-start(bf16[2,64,512]{2,1,0:T(8,128)(2,1)S(1)} %get-tuple-element.39), channel_id=1, source_target_pairs={{0,1},{1,0},{2,3},{3,2},{4,5},{5,4},{6,7},{7,6},{8,9},{9,8},{10,11... | collective-permute-start | bytes 393224 | tf_op jit(solution)/shard_map/ppermute | solution.py:192

commit v3 on v2

--- a/solution.py
+++ b/solution.py
@@ -9,7 +9,7 @@
 
 VMEM = pl.BlockSpec(memory_space=pltpu.VMEM)
 SMEM = pl.BlockSpec(memory_space=pltpu.SMEM)
-COST = 1000000000
+COST = 3000000000
 F32, BF16 = jnp.float32, jnp.bfloat16
 
 
@@ -37,10 +37,10 @@
 
 
 def times(lhs, rhs):
-    return (
-        dot(lhs[0], rhs[0]) - dot(lhs[1], rhs[1]),
-        dot(lhs[0], rhs[1]) + dot(lhs[1], rhs[0]),
-    )
+    rows = lhs[0].shape[0]
+    both = jnp.concatenate([lhs[0], lhs[1]], axis=0)
+    by_real, by_imag = dot(both, rhs[0]), dot(both, rhs[1])
+    return by_real[:rows] - by_imag[rows:], by_imag[:rows] + by_real[rows:]
 
 
 def pair(ref, *index):
@@ -150,23 +150,53 @@
     return lax.dot_general(lhs, rhs, (((0,), (0,)), ((), ())), preferred_element_type=F32)
 
 
-def block_kernel(counts, incident, own, other, scattered, green_next, both):
-    core = this_core()
-    modes = own.shape[1]
-    for turn, chained in enumerate((own, other)):
-        slot = core if turn == 0 else 1 - core
-        live = slot < counts[0]
-        for c in range(2):
-            wave = chained[c].astype(F32)
-            scattered[c, slot] = jnp.where(live, wave, 0.0).astype(BF16)
-            combined = (incident[c, slot].astype(F32) + wave).astype(BF16)
-            both[0, c * modes : (c + 1) * modes] = combined
-            both[1, (1 - c) * modes : (2 - c) * modes] = -combined if c == 0 else combined
-        stacked = both[0]
-        real = across(both[1], stacked) / modes
-        imag = across(stacked, stacked) / modes
-        green_next[0, slot] = jnp.where(live, real, 0.0).astype(BF16)
-        green_next[1, slot] = jnp.where(live, imag, 0.0).astype(BF16)
+def block_kernel(turn, counts, incident, chained, *refs):
+    scattered, green_next, both, waves, blocks, sent = refs[-6:]
+    core = this_core()
+    slot = core if turn == 0 else 1 - core
+    live = slot < counts[0]
+    modes = chained.shape[1]
+    copies = []
+    for c in range(2):
+        wave = chained[c].astype(F32)
+        waves[c] = jnp.where(live, wave, 0.0).astype(BF16)
+        copies.append(pltpu.make_async_copy(waves.at[c], scattered.at[c, slot], sent.at[c]))
+        copies[-1].start()
+        combined = (incident[c, slot].astype(F32) + wave).astype(BF16)
+        both[0, c * modes : (c + 1) * modes] = combined
+        both[1, (1 - c) * modes : (2 - c) * modes] = -combined if c == 0 else combined
+    stacked = both[0]
+    for c in range(2):
+        block = across(both[1 - c], stacked) / modes
+        blocks[c] = jnp.where(live, block, 0.0).astype(BF16)
+        copies.append(pltpu.make_async_copy(blocks.at[c], green_next.at[c, slot], sent.at[2 + c]))
+        copies[-1].start()
+    for copy in copies:
+        copy.wait()
+
+
+def green_blocks(turn, counts, incident, chained, filled=()):
+    _, slots, modes, orbitals = incident.shape
+    anywhere = pl.BlockSpec(memory_space=pl.ANY)
+    return pl.pallas_call(
+        functools.partial(block_kernel, turn),
+        out_shape=[
+            jax.ShapeDtypeStruct((2, slots, modes, orbitals), BF16),
+            jax.ShapeDtypeStruct((2, slots, orbitals, orbitals), BF16),
+        ],
+        in_specs=[SMEM, VMEM, VMEM] + [anywhere] * len(filled),
+        out_specs=[anywhere] * 2,
+        input_output_aliases={3 + n: n for n in range(len(filled))},
+        scratch_shapes=[
+            pltpu.VMEM((2, 2 * modes, orbitals), BF16),
+            pltpu.VMEM((2, modes, orbitals), BF16),
+            pltpu.VMEM((2, orbitals, orbitals), BF16),
+            pltpu.SemaphoreType.DMA((4,)),
+        ],
+        compiler_params=pltpu.CompilerParams(vmem_limit_bytes=16 << 20),
+        cost_estimate=pl.CostEstimate(flops=COST, bytes_accessed=1, transcendentals=0),
+        name="green_blocks",
+    )(counts, incident, chained, *filled)
 
 
 def complex_matrix(lhs, rhs):
@@ -205,12 +235,11 @@
     every = (2, slots, modes, orbitals)
 
     waves = [incident] + [None] * (groups - 1)
-    if True:
-        for offset in range(1, groups):
+    for _ in range(1):
+        for offset in range(groups - 1, 0, -1):
             if offset == 1 or offset % 2 == 0:
                 waves[offset] = swap(incident, offset)
         prop_other, green_other = swap(prop_here, 0, 1), swap(green_here, 0, 1)
-        base = call(own_kernel, "own", [(every, F32)], scalars, [incident, g_here], total)[0]
         steps, greens, chip_map = pl.pallas_call(
             prepare_kernel,
             out_shape=[
@@ -225,20 +254,20 @@
             cost_estimate=pl.CostEstimate(flops=COST, bytes_accessed=1, transcendentals=0),
             name="prepare",
         )(hbm(prop_here), prop_other, hbm(green_here), green_other)
-    waves[1], waves[2], chip_map, base = lax.optimization_barrier((waves[1], waves[2], chip_map, base))
+    waves[1], waves[2], _ = lax.optimization_barrier((waves[1], waves[2], chip_map))
     for offset in range(3, groups, 2):
         waves[offset] = swap(waves[offset - 1], 1)
 
-    back = []
-    for offset in range(1, groups):
-        part = call(
+    parts = [
+        call(
             functools.partial(product_kernel, offset), "product", [(every, BF16)], scalars, [waves[offset], g_here], total
         )[0]
-        if offset == 1:
-            part, waves[-1] = lax.optimization_barrier((part, waves[-1]))
-        if offset == 2:
-            part, chip_map = lax.optimization_barrier((part, chip_map))
-        back.append(swap(part, offset))
+        for offset in range(1, groups)
+    ]
+    parts[0], parts[-1] = lax.optimization_barrier((parts[0], parts[-1]))
+    back = [swap(part, offset + 1) for offset, part in enumerate(parts)]
+    waves[0], parts[-1] = lax.optimization_barrier((incident, parts[-1]))
+    base = call(own_kernel, "own", [(every, F32)], scalars, [waves[0], g_here], total)[0]
     own, other = call(term_kernel, "term", [(wave, BF16)] * 2, [], [base] + back)
     other = swap(other, 0, 1)
 
@@ -269,13 +298,8 @@
         [((2,) + wave, BF16)])
 
     other = swap(other, 0, 1)
-    scattered, green_next = call(
-        block_kernel,
-        "green_blocks",
-        [((2, slots, modes, orbitals), BF16), ((2, slots, orbitals, orbitals), BF16)],
-        [counts],
-        [incident, own, other],
-        [((2, 2 * modes, orbitals), BF16)])
+    filled = green_blocks(0, counts, incident, own)
+    scattered, green_next = green_blocks(1, counts, incident, other, filled)
     return scattered[:, :, None], green_next[:, :, None]
 
 

time: 66.5 us -> 63.5 us (0.955)
  the two profiles are of different devices: /device:TPU:15 before, /device:TPU:1 now
where the time goes in v3:
time: 63.5 us; the launch traced here: 62.6 us
  starting transfers between devices  27.2 us (43%)
  waiting for transfers between devices  20.8 us (33%)
  Pallas kernels  11 us (17%)
  between operations  2.07 us (3%)
  other arithmetic  1.49 us (2%)
    ppermute x10, starting transfers between devices, swap(): return lax.ppermute(value, ('energy', 'wire'), pairs)  18.8 us
    ppermute x10, waiting for transfers between devices, swap(): return lax.ppermute(value, ('energy', 'wire'), pairs)  17.7 us
    ppermute x5, starting transfers between devices, later(): return lax.ppermute(value, 'wire', pairs)  8.4 us
    pallas_call x7, Pallas kernels, call(): pl.pallas_call(kernel, out_shape=shapes, in_specs=[SMEM] * len(scalars) +...  5.63 us
    ppermute x5, waiting for transfers between devices, later(): return lax.ppermute(value, 'wire', pairs)  3.12 us
    pallas_call x2, Pallas kernels, green_blocks(): pl.pallas_call(functools.partial(block_kernel, turn), out_shape=[jax.Shap...  2.69 us
    pallas_call x1, Pallas kernels, shards(): pl.pallas_call(prepare_kernel, out_shape=[jax.ShapeDtypeStruct((2,) + blo...  2.69 us
  transfers between devices with their start and end apart: 15, of which 7 were waited for; matrix products, arithmetic and copies ran while one was open for 2% of the time, Pallas kernels for 14%

profile of v3, /device:TPU:1, one launch (start us, length us, event | category | flops | bytes accessed | tf_op | source)
XLA Modules:
  0.0 62.6 jit_solution(4589076813103738235)
XLA Ops:
  0.6 0.1 collective-permute-start
  0.8 0.5 collective-permute-start.1
  1.2 2.4 %collective-permute-start.2 = (bf16[2,2,64,512]{3,2,1,0:T(8,128)(2,1)}, bf16[2,2,64,512]{3,2,1,0:T(8,128)(2,1)S(1)}, u32[]{:S(2)}, u32[]{:S(2)}) collective-permute-start(bf16[2,2,64,512]{3,2,1,0:T(8,128)(2,1)} %bitcast.14), channel_id=1, source_target_pairs={{0,8},{1,9},{2,10},{3,11},{4,12},{5,13},{6,14},{7,15},{8,0},{9,1},... | collective-permute-start | bytes 786440 | tf_op jit(solution)/shard_map/ppermute | solution.py:222
  3.6 2.3 %collective-permute-start.3 = (bf16[2,2,64,512]{3,2,1,0:T(8,128)(2,1)}, bf16[2,2,64,512]{3,2,1,0:T(8,128)(2,1)S(1)}, u32[]{:S(2)}, u32[]{:S(2)}) collective-permute-start(bf16[2,2,64,512]{3,2,1,0:T(8,128)(2,1)} %bitcast.15), channel_id=1, source_target_pairs={{0,16},{1,17},{2,18},{3,19},{4,20},{5,21},{6,22},{7,23},{8,24},{9,... | collective-permute-start | bytes 786440 | tf_op jit(solution)/shard_map/ppermute | solution.py:222
  6.5 0.7 %pad_maximum_fusion.real_valued = f32[18]{0:T(128)S(1)} fusion(f32[16]{0:T(128)} %param.18, f32[2]{0:T(128)} %param.19), kind=kLoop, calls=%fused_computation.1 | loop fusion | flops 18 | bytes 144 | tf_op jit(solution)/shard_map/concatenate | solution.py:232
  7.3 0.7 %pad_add_fusion.whole = s32[17]{0:T(128)S(1)} fusion(s32[1]{0:T(128)S(6)} %copy.19, s32[8]{0:T(128)} %param.15, s32[8]{0:T(128)} %param.14), kind=kLoop, calls=%fused_computation | loop fusion | flops 34 | bytes 136 | tf_op jit(solution)/shard_map/concatenate | solution.py:231
  8.0 0.0 copy-start
  8.0 0.0 collective-permute-done.prop_other
  8.0 0.0 collective-permute-done.1.green_other
  8.1 2.7 %prepare.1 = (bf16[2,2,512,512]{3,2,1,0:T(8,128)(2,1)S(1)}, bf16[2,2,512,512]{3,2,1,0:T(8,128)(2,1)S(1)}, bf16[2,512,512]{2,1,0:T(8,128)(2,1)S(1)}) custom-call(bf16[2,2,512,512]{3,2,1,0:T(8,128)(2,1)} %bitcast.20, bf16[2,2,512,512]{3,2,1,0:T(8,128)(2,1)S(1)} %collective-permute-done.prop_other, bf16[2,2,512,512]{3,2,1,0:T(8,128)(2,1)} %bitcast.22, ...), custom_call_target="tpu_custom_call" | custom-call | flops 3000000000 | bytes 1 | tf_op jit(solution)/shard_map/prepare/pallas_call | solution.py:243
  10.8 0.7 %collective-permute-start.12 = (bf16[2,512,512]{2,1,0:T(8,128)(2,1)S(1)}, bf16[2,512,512]{2,1,0:T(8,128)(2,1)S(1)}, u32[]{:S(2)}, u32[]{:S(2)}) collective-permute-start(bf16[2,512,512]{2,1,0:T(8,128)(2,1)S(1)} %get-tuple-element.22.chip_map), channel_id=1, source_target_pairs={{2,4},{3,5},{4,6},{5,7},{10,12},{11,13},{12,14},{13,15},{18,20},{1... | collective-permute-start | bytes 3145736 | tf_op jit(solution)/shard_map/ppermute | solution.py:228
  11.5 0.7 %collective-permute-start.13 = (bf16[2,512,512]{2,1,0:T(8,128)(2,1)S(1)}, bf16[2,512,512]{2,1,0:T(8,128)(2,1)S(1)}, u32[]{:S(2)}, u32[]{:S(2)}) collective-permute-start(bf16[2,512,512]{2,1,0:T(8,128)(2,1)S(1)} %get-tuple-element.22.chip_map), channel_id=1, source_target_pairs={{2,6},{3,7},{10,14},{11,15},{18,22},{19,23},{26,30},{27,31}} | collective-permute-start | bytes 3145736 | tf_op jit(solution)/shard_map/ppermute | solution.py:228
  12.2 3.3 %collective-permute-done.2.wave_ref = bf16[2,2,64,512]{3,2,1,0:T(8,128)(2,1)S(1)} collective-permute-done((bf16[2,2,64,512]{3,2,1,0:T(8,128)(2,1)}, bf16[2,2,64,512]{3,2,1,0:T(8,128)(2,1)S(1)}, u32[]{:S(2)}, u32[]{:S(2)}) %collective-permute-start.2) | collective-permute-done | bytes 262176 | tf_op jit(solution)/shard_map/ppermute | solution.py:222
  15.6 0.0 collective-permute-done.3.wave_ref
  15.6 2.3 %collective-permute-start.4 = (bf16[2,2,64,512]{3,2,1,0:T(8,128)(2,1)S(1)}, bf16[2,2,64,512]{3,2,1,0:T(8,128)(2,1)S(1)}, u32[]{:S(2)}, u32[]{:S(2)}) collective-permute-start(bf16[2,2,64,512]{3,2,1,0:T(8,128)(2,1)S(1)} %collective-permute-done.3.wave_ref), channel_id=1, source_target_pairs={{0,8},{1,9},{2,10},{3,11},{4,12},{5,13},{6,14},{7,15},{8,0},{9,1},... | collective-permute-start | bytes 786440 | tf_op jit(solution)/shard_map/ppermute | solution.py:222
  17.9 0.0 copy-done
  17.9 0.9 %product.5 = bf16[2,2,64,512]{3,2,1,0:T(8,128)(2,1)S(1)} custom-call(s32[17]{0:T(128)S(1)} %pad_add_fusion.whole, f32[18]{0:T(128)S(1)} %pad_maximum_fusion.real_valued, bf16[2,2,64,512]{3,2,1,0:T(8,128)(2,1)S(1)} %collective-permute-done.3.wave_ref, bf16[2,2,512,512]{3,2,1,0:T(8,128)(2,1)S(1)} %bitcast.10), custom_call_target="tpu_custom_call" | custom-call | flops 3000000000 | bytes 1 | tf_op jit(solution)/shard_map/product/pallas_call | solution.py:19
  18.9 1.9 %collective-permute-start.6 = (bf16[2,2,64,512]{3,2,1,0:T(8,128)(2,1)S(1)}, bf16[2,2,64,512]{3,2,1,0:T(8,128)(2,1)S(1)}, u32[]{:S(2)}, u32[]{:S(2)}) collective-permute-start(bf16[2,2,64,512]{3,2,1,0:T(8,128)(2,1)S(1)} %product.5), channel_id=1, source_target_pairs={{0,16},{1,17},{2,18},{3,19},{4,20},{5,21},{6,22},{7,23},{8,24},{9,... | collective-permute-start | bytes 786440 | tf_op jit(solution)/shard_map/ppermute | solution.py:222
  20.7 0.9 %product.3 = bf16[2,2,64,512]{3,2,1,0:T(8,128)(2,1)S(1)} custom-call(s32[17]{0:T(128)S(1)} %pad_add_fusion.whole, f32[18]{0:T(128)S(1)} %pad_maximum_fusion.real_valued, bf16[2,2,64,512]{3,2,1,0:T(8,128)(2,1)S(1)} %collective-permute-done.2.wave_ref, bf16[2,2,512,512]{3,2,1,0:T(8,128)(2,1)S(1)} %bitcast.11), custom_call_target="tpu_custom_call" | custom-call | flops 3000000000 | bytes 1 | tf_op jit(solution)/shard_map/product/pallas_call | solution.py:19
  21.6 0.0 copy-start.1
  21.7 0.5 collective-permute-done.4.wave_ref
  22.2 0.9 %product.4 = bf16[2,2,64,512]{3,2,1,0:T(8,128)(2,1)S(1)} custom-call(s32[17]{0:T(128)S(1)} %pad_add_fusion.whole, f32[18]{0:T(128)S(1)} %pad_maximum_fusion.real_valued, bf16[2,2,64,512]{3,2,1,0:T(8,128)(2,1)S(1)} %collective-permute-done.4.wave_ref, bf16[2,2,512,512]{3,2,1,0:T(8,128)(2,1)S(1)} %bitcast.12), custom_call_target="tpu_custom_call" | custom-call | flops 3000000000 | bytes 1 | tf_op jit(solution)/shard_map/product/pallas_call | solution.py:19
  23.1 6.6 %collective-permute-start.7 = (bf16[2,2,64,512]{3,2,1,0:T(8,128)(2,1)S(1)}, bf16[2,2,64,512]{3,2,1,0:T(8,128)(2,1)S(1)}, u32[]{:S(2)}, u32[]{:S(2)}) collective-permute-start(bf16[2,2,64,512]{3,2,1,0:T(8,128)(2,1)S(1)} %product.4), channel_id=1, source_target_pairs={{0,24},{1,25},{2,26},{3,27},{4,28},{5,29},{6,30},{7,31},{8,16},{9,... | collective-permute-start | bytes 786440 | tf_op jit(solution)/shard_map/ppermute | solution.py:222
  29.8 0.0 collective-permute-start.5
  29.8 0.0 copy-done.1
  29.8 1.0 %own.1.base = f32[2,2,64,512]{3,2,1,0:T(8,128)S(1)} custom-call(s32[17]{0:T(128)S(1)} %pad_add_fusion.whole, f32[18]{0:T(128)S(1)} %pad_maximum_fusion.real_valued, bf16[2,2,64,512]{3,2,1,0:T(8,128)(2,1)S(1)} %bitcast.16, bf16[2,2,512,512]{3,2,1,0:T(8,128)(2,1)S(1)} %bitcast.13), custom_call_target="tpu_custom_call" | custom-call | flops 3000000000 | bytes 1 | tf_op jit(solution)/shard_map/own/pallas_call | solution.py:19
  30.7 0.0 collective-permute-done.6.refs_1_
  30.7 4.2 %collective-permute-done.7.refs_2_ = bf16[2,2,64,512]{3,2,1,0:T(8,128)(2,1)S(1)} collective-permute-done((bf16[2,2,64,512]{3,2,1,0:T(8,128)(2,1)S(1)}, bf16[2,2,64,512]{3,2,1,0:T(8,128)(2,1)S(1)}, u32[]{:S(2)}, u32[]{:S(2)}) %collective-permute-start.7) | collective-permute-done | bytes 262176 | tf_op jit(solution)/shard_map/ppermute | solution.py:222
  34.9 8.6 %collective-permute-done.5.refs_0_ = bf16[2,2,64,512]{3,2,1,0:T(8,128)(2,1)S(1)} collective-permute-done((bf16[2,2,64,512]{3,2,1,0:T(8,128)(2,1)S(1)}, bf16[2,2,64,512]{3,2,1,0:T(8,128)(2,1)S(1)}, u32[]{:S(2)}, u32[]{:S(2)}) %collective-permute-start.5) | collective-permute-done | bytes 262176 | tf_op jit(solution)/shard_map/ppermute | solution.py:222
  43.6 0.1 term.1
  43.7 1.5 %collective-permute-start.8 = (bf16[2,64,512]{2,1,0:T(8,128)(2,1)S(1)}, bf16[2,64,512]{2,1,0:T(8,128)(2,1)S(1)}, u32[]{:S(2)}, u32[]{:S(2)}) collective-permute-start(bf16[2,64,512]{2,1,0:T(8,128)(2,1)S(1)} %get-tuple-element.29), channel_id=1, source_target_pairs={{0,1},{1,0},{2,3},{3,2},{4,5},{5,4},{6,7},{7,6},{8,9},{9,8},{10,11... | collective-permute-start | bytes 393224 | tf_op jit(solution)/shard_map/ppermute | solution.py:222
  45.2 1.0 %collective-permute-done.8.other = bf16[2,64,512]{2,1,0:T(8,128)(2,1)S(1)} collective-permute-done((bf16[2,64,512]{2,1,0:T(8,128)(2,1)S(1)}, bf16[2,64,512]{2,1,0:T(8,128)(2,1)S(1)}, u32[]{:S(2)}, u32[]{:S(2)}) %collective-permute-start.8) | collective-permute-done | bytes 131104 | tf_op jit(solution)/shard_map/ppermute | solution.py:222
  46.1 0.7 %source.1 = (f32[2,64,512]{2,1,0:T(8,128)S(1)}, f32[2,64,512]{2,1,0:T(8,128)S(1)}, bf16[2,64,512]{2,1,0:T(8,128)(2,1)S(1)}) custom-call(bf16[2,64,512]{2,1,0:T(8,128)(2,1)S(1)} %get-tuple-element.28.own, bf16[2,64,512]{2,1,0:T(8,128)(2,1)S(1)} %collective-permute-done.8.other, bf16[2,2,512,512]{3,2,1,0:T(8,128)(2,1)S(1)} %get-tuple-element.21.steps, ...), custom_call_target="tpu_custom_call" | custom-call | flops 3000000000 | bytes 1 | tf_op jit(solution)/shard_map/source/pallas_call | solution.py:19
  46.9 3.2 %collective-permute-start.10 = (bf16[2,64,512]{2,1,0:T(8,128)(2,1)S(1)}, bf16[2,64,512]{2,1,0:T(8,128)(2,1)S(1)}, u32[]{:S(2)}, u32[]{:S(2)}) collective-permute-start(bf16[2,64,512]{2,1,0:T(8,128)(2,1)S(1)} %get-tuple-element.33), channel_id=1, source_target_pairs={{0,4},{1,5},{2,6},{3,7},{8,12},{9,13},{10,14},{11,15},{16,20},{17,... | collective-permute-start | bytes 393224 | tf_op jit(solution)/shard_map/ppermute | solution.py:228
  50.0 2.2 %collective-permute-start.11 = (bf16[2,64,512]{2,1,0:T(8,128)(2,1)S(1)}, bf16[2,64,512]{2,1,0:T(8,128)(2,1)S(1)}, u32[]{:S(2)}, u32[]{:S(2)}) collective-permute-start(bf16[2,64,512]{2,1,0:T(8,128)(2,1)S(1)} %get-tuple-element.33), channel_id=1, source_target_pairs={{0,6},{1,7},{8,14},{9,15},{16,22},{17,23},{24,30},{25,31}} | collective-permute-start | bytes 393224 | tf_op jit(solution)/shard_map/ppermute | solution.py:228
  52.3 1.6 %collective-permute-start.9 = (bf16[2,64,512]{2,1,0:T(8,128)(2,1)S(1)}, bf16[2,64,512]{2,1,0:T(8,128)(2,1)S(1)}, u32[]{:S(2)}, u32[]{:S(2)}) collective-permute-start(bf16[2,64,512]{2,1,0:T(8,128)(2,1)S(1)} %get-tuple-element.33), channel_id=1, source_target_pairs={{0,2},{1,3},{2,4},{3,5},{4,6},{5,7},{8,10},{9,11},{10,12},{11,13},... | collective-permute-start | bytes 393224 | tf_op jit(solution)/shard_map/ppermute | solution.py:228
  54.5 0.0 collective-permute-done.10.refs_1_
  54.5 0.3 collective-permute-done.11.refs_2_
  54.8 2.8 %collective-permute-done.9.refs_0_ = bf16[2,64,512]{2,1,0:T(8,128)(2,1)S(1)} collective-permute-done((bf16[2,64,512]{2,1,0:T(8,128)(2,1)S(1)}, bf16[2,64,512]{2,1,0:T(8,128)(2,1)S(1)}, u32[]{:S(2)}, u32[]{:S(2)}) %collective-permute-start.9) | collective-permute-done | bytes 131104 | tf_op jit(solution)/shard_map/ppermute | solution.py:228
  57.6 0.0 collective-permute-done.12.refs_3_
  57.6 0.0 collective-permute-done.13.refs_4_
  57.6 1.0 %chain.1 = (bf16[2,64,512]{2,1,0:T(8,128)(2,1)S(1)}, bf16[2,64,512]{2,1,0:T(8,128)(2,1)S(1)}) custom-call(bf16[2,2,512,512]{3,2,1,0:T(8,128)(2,1)S(1)} %get-tuple-element.21.steps, bf16[2,512,512]{2,1,0:T(8,128)(2,1)S(1)} %get-tuple-element.22.chip_map, f32[2,64,512]{2,1,0:T(8,128)S(1)} %get-tuple-element.31.first, ...), custom_call_target="tpu_custom_call" | custom-call | flops 3000000000 | bytes 1 | tf_op jit(solution)/shard_map/chain/pallas_call | solution.py:19
  58.7 1.2 %collective-permute-start.14 = (bf16[2,64,512]{2,1,0:T(8,128)(2,1)S(1)}, bf16[2,64,512]{2,1,0:T(8,128)(2,1)S(1)}, u32[]{:S(2)}, u32[]{:S(2)}) collective-permute-start(bf16[2,64,512]{2,1,0:T(8,128)(2,1)S(1)} %get-tuple-element.34), channel_id=1, source_target_pairs={{0,1},{1,0},{2,3},{3,2},{4,5},{5,4},{6,7},{7,6},{8,9},{9,8},{10,11... | collective-permute-start | bytes 393224 | tf_op jit(solution)/shard_map/ppermute | solution.py:222
  59.9 1.3 %green_blocks.2 = (bf16[2,2,64,512]{3,2,1,0:T(8,128)(2,1)}, bf16[2,2,512,512]{3,2,1,0:T(8,128)(2,1)}) custom-call(s32[1]{0:T(128)S(6)} %copy.18.counts, bf16[2,2,64,512]{3,2,1,0:T(8,128)(2,1)S(1)} %bitcast.17, bf16[2,64,512]{2,1,0:T(8,128)(2,1)S(1)} %get-tuple-element.35.chained), custom_call_target="tpu_custom_call" | custom-call | flops 3000000000 | bytes 1 | tf_op jit(solution)/shard_map/green_blocks/pallas_call | solution.py:181
  61.3 0.0 collective-permute-done.14.chained
  61.3 1.3 %green_blocks.3 = (bf16[2,2,64,512]{3,2,1,0:T(8,128)(2,1)}, bf16[2,2,512,512]{3,2,1,0:T(8,128)(2,1)}) custom-call(s32[1]{0:T(128)S(6)} %copy.18.counts, bf16[2,2,64,512]{3,2,1,0:T(8,128)(2,1)S(1)} %bitcast.18, bf16[2,64,512]{2,1,0:T(8,128)(2,1)S(1)} %collective-permute-done.14.chained, ...), custom_call_target="tpu_custom_call", output_to_operand_aliasing={{0}: (3, {}), {1}: (4, {})} | custom-call | flops 3000000000 | bytes 1 | tf_op jit(solution)/shard_map/green_blocks/pallas_call | solution.py:181
Async XLA Ops:
  0.6 7.4 %collective-permute-start = (bf16[2,2,512,512]{3,2,1,0:T(8,128)(2,1)}, bf16[2,2,512,512]{3,2,1,0:T(8,128)(2,1)S(1)}, u32[]{:S(2)}, u32[]{:S(2)}) collective-permute-start(bf16[2,2,512,512]{3,2,1,0:T(8,128)(2,1)} %bitcast.19), channel_id=1, source_target_pairs={{0,1},{1,0},{2,3},{3,2},{4,5},{5,4},{6,7},{7,6},{8,9},{9,8},{10,11... | collective-permute-start | bytes 6291464 | tf_op jit(solution)/shard_map/ppermute | solution.py:222
  0.8 7.3 %collective-permute-start.1 = (bf16[2,2,512,512]{3,2,1,0:T(8,128)(2,1)}, bf16[2,2,512,512]{3,2,1,0:T(8,128)(2,1)S(1)}, u32[]{:S(2)}, u32[]{:S(2)}) collective-permute-start(bf16[2,2,512,512]{3,2,1,0:T(8,128)(2,1)} %bitcast.21), channel_id=1, source_target_pairs={{0,1},{1,0},{2,3},{3,2},{4,5},{5,4},{6,7},{7,6},{8,9},{9,8},{10,11... | collective-permute-start | bytes 6291464 | tf_op jit(solution)/shard_map/ppermute | solution.py:222
  1.2 14.4 %collective-permute-start.2 = (bf16[2,2,64,512]{3,2,1,0:T(8,128)(2,1)}, bf16[2,2,64,512]{3,2,1,0:T(8,128)(2,1)S(1)}, u32[]{:S(2)}, u32[]{:S(2)}) collective-permute-start(bf16[2,2,64,512]{3,2,1,0:T(8,128)(2,1)} %bitcast.14), channel_id=1, source_target_pairs={{0,8},{1,9},{2,10},{3,11},{4,12},{5,13},{6,14},{7,15},{8,0},{9,1},... | collective-permute-start | bytes 786440 | tf_op jit(solution)/shard_map/ppermute | solution.py:222
  3.6 12.0 %collective-permute-start.3 = (bf16[2,2,64,512]{3,2,1,0:T(8,128)(2,1)}, bf16[2,2,64,512]{3,2,1,0:T(8,128)(2,1)S(1)}, u32[]{:S(2)}, u32[]{:S(2)}) collective-permute-start(bf16[2,2,64,512]{3,2,1,0:T(8,128)(2,1)} %bitcast.15), channel_id=1, source_target_pairs={{0,16},{1,17},{2,18},{3,19},{4,20},{5,21},{6,22},{7,23},{8,24},{9,... | collective-permute-start | bytes 786440 | tf_op jit(solution)/shard_map/ppermute | solution.py:222
  8.0 9.9 %copy-start = (bf16[2,2,1,512,512]{4,3,2,1,0:T(8,128)(2,1)S(1)}, bf16[2,2,1,512,512]{4,3,2,1,0:T(8,128)(2,1)}, u32[]{:S(2)}) copy-start(bf16[2,2,1,512,512]{4,3,2,1,0:T(8,128)(2,1)} %param.10) | copy-start | bytes 6291460
  10.8 46.9 %collective-permute-start.12 = (bf16[2,512,512]{2,1,0:T(8,128)(2,1)S(1)}, bf16[2,512,512]{2,1,0:T(8,128)(2,1)S(1)}, u32[]{:S(2)}, u32[]{:S(2)}) collective-permute-start(bf16[2,512,512]{2,1,0:T(8,128)(2,1)S(1)} %get-tuple-element.22.chip_map), channel_id=1, source_target_pairs={{2,4},{3,5},{4,6},{5,7},{10,12},{11,13},{12,14},{13,15},{18,20},{1... | collective-permute-start | bytes 3145736 | tf_op jit(solution)/shard_map/ppermute | solution.py:228
  11.5 46.1 %collective-permute-start.13 = (bf16[2,512,512]{2,1,0:T(8,128)(2,1)S(1)}, bf16[2,512,512]{2,1,0:T(8,128)(2,1)S(1)}, u32[]{:S(2)}, u32[]{:S(2)}) collective-permute-start(bf16[2,512,512]{2,1,0:T(8,128)(2,1)S(1)} %get-tuple-element.22.chip_map), channel_id=1, source_target_pairs={{2,6},{3,7},{10,14},{11,15},{18,22},{19,23},{26,30},{27,31}} | collective-permute-start | bytes 3145736 | tf_op jit(solution)/shard_map/ppermute | solution.py:228
  15.6 6.6 %collective-permute-start.4 = (bf16[2,2,64,512]{3,2,1,0:T(8,128)(2,1)S(1)}, bf16[2,2,64,512]{3,2,1,0:T(8,128)(2,1)S(1)}, u32[]{:S(2)}, u32[]{:S(2)}) collective-permute-start(bf16[2,2,64,512]{3,2,1,0:T(8,128)(2,1)S(1)} %collective-permute-done.3.wave_ref), channel_id=1, source_target_pairs={{0,8},{1,9},{2,10},{3,11},{4,12},{5,13},{6,14},{7,15},{8,0},{9,1},... | collective-permute-start | bytes 786440 | tf_op jit(solution)/shard_map/ppermute | solution.py:222
  18.9 11.9 %collective-permute-start.6 = (bf16[2,2,64,512]{3,2,1,0:T(8,128)(2,1)S(1)}, bf16[2,2,64,512]{3,2,1,0:T(8,128)(2,1)S(1)}, u32[]{:S(2)}, u32[]{:S(2)}) collective-permute-start(bf16[2,2,64,512]{3,2,1,0:T(8,128)(2,1)S(1)} %product.5), channel_id=1, source_target_pairs={{0,16},{1,17},{2,18},{3,19},{4,20},{5,21},{6,22},{7,23},{8,24},{9,... | collective-permute-start | bytes 786440 | tf_op jit(solution)/shard_map/ppermute | solution.py:222
  21.6 8.1 %copy-start.1 = (bf16[2,2,1,64,512]{4,3,2,1,0:T(8,128)(2,1)S(1)}, bf16[2,2,1,64,512]{4,3,2,1,0:T(8,128)(2,1)}, u32[]{:S(2)}) copy-start(bf16[2,2,1,64,512]{4,3,2,1,0:T(8,128)(2,1)} %param.13) | copy-start | bytes 786436
  23.1 11.8 %collective-permute-start.7 = (bf16[2,2,64,512]{3,2,1,0:T(8,128)(2,1)S(1)}, bf16[2,2,64,512]{3,2,1,0:T(8,128)(2,1)S(1)}, u32[]{:S(2)}, u32[]{:S(2)}) collective-permute-start(bf16[2,2,64,512]{3,2,1,0:T(8,128)(2,1)S(1)} %product.4), channel_id=1, source_target_pairs={{0,24},{1,25},{2,26},{3,27},{4,28},{5,29},{6,30},{7,31},{8,16},{9,... | collective-permute-start | bytes 786440 | tf_op jit(solution)/shard_map/ppermute | solution.py:222
  29.8 13.8 %collective-permute-start.5 = (bf16[2,2,64,512]{3,2,1,0:T(8,128)(2,1)S(1)}, bf16[2,2,64,512]{3,2,1,0:T(8,128)(2,1)S(1)}, u32[]{:S(2)}, u32[]{:S(2)}) collective-permute-start(bf16[2,2,64,512]{3,2,1,0:T(8,128)(2,1)S(1)} %product.3), channel_id=1, source_target_pairs={{0,8},{1,9},{2,10},{3,11},{4,12},{5,13},{6,14},{7,15},{8,0},{9,1},... | collective-permute-start | bytes 786440 | tf_op jit(solution)/shard_map/ppermute | solution.py:222
  43.7 2.5 %collective-permute-start.8 = (bf16[2,64,512]{2,1,0:T(8,128)(2,1)S(1)}, bf16[2,64,512]{2,1,0:T(8,128)(2,1)S(1)}, u32[]{:S(2)}, u32[]{:S(2)}) collective-permute-start(bf16[2,64,512]{2,1,0:T(8,128)(2,1)S(1)} %get-tuple-element.29), channel_id=1, source_target_pairs={{0,1},{1,0},{2,3},{3,2},{4,5},{5,4},{6,7},{7,6},{8,9},{9,8},{10,11... | collective-permute-start | bytes 393224 | tf_op jit(solution)/shard_map/ppermute | solution.py:222
  46.9 7.6 %collective-permute-start.10 = (bf16[2,64,512]{2,1,0:T(8,128)(2,1)S(1)}, bf16[2,64,512]{2,1,0:T(8,128)(2,1)S(1)}, u32[]{:S(2)}, u32[]{:S(2)}) collective-permute-start(bf16[2,64,512]{2,1,0:T(8,128)(2,1)S(1)} %get-tuple-element.33), channel_id=1, source_target_pairs={{0,4},{1,5},{2,6},{3,7},{8,12},{9,13},{10,14},{11,15},{16,20},{17,... | collective-permute-start | bytes 393224 | tf_op jit(solution)/shard_map/ppermute | solution.py:228
  50.0 4.8 %collective-permute-start.11 = (bf16[2,64,512]{2,1,0:T(8,128)(2,1)S(1)}, bf16[2,64,512]{2,1,0:T(8,128)(2,1)S(1)}, u32[]{:S(2)}, u32[]{:S(2)}) collective-permute-start(bf16[2,64,512]{2,1,0:T(8,128)(2,1)S(1)} %get-tuple-element.33), channel_id=1, source_target_pairs={{0,6},{1,7},{8,14},{9,15},{16,22},{17,23},{24,30},{25,31}} | collective-permute-start | bytes 393224 | tf_op jit(solution)/shard_map/ppermute | solution.py:228
  52.3 5.3 %collective-permute-start.9 = (bf16[2,64,512]{2,1,0:T(8,128)(2,1)S(1)}, bf16[2,64,512]{2,1,0:T(8,128)(2,1)S(1)}, u32[]{:S(2)}, u32[]{:S(2)}) collective-permute-start(bf16[2,64,512]{2,1,0:T(8,128)(2,1)S(1)} %get-tuple-element.33), channel_id=1, source_target_pairs={{0,2},{1,3},{2,4},{3,5},{4,6},{5,7},{8,10},{9,11},{10,12},{11,13},... | collective-permute-start | bytes 393224 | tf_op jit(solution)/shard_map/ppermute | solution.py:228
  58.7 2.6 %collective-permute-start.14 = (bf16[2,64,512]{2,1,0:T(8,128)(2,1)S(1)}, bf16[2,64,512]{2,1,0:T(8,128)(2,1)S(1)}, u32[]{:S(2)}, u32[]{:S(2)}) collective-permute-start(bf16[2,64,512]{2,1,0:T(8,128)(2,1)S(1)} %get-tuple-element.34), channel_id=1, source_target_pairs={{0,1},{1,0},{2,3},{3,2},{4,5},{5,4},{6,7},{7,6},{8,9},{9,8},{10,11... | collective-permute-start | bytes 393224 | tf_op jit(solution)/shard_map/ppermute | solution.py:222

commit v4 on v3

--- a/solution.py
+++ b/solution.py
@@ -129,21 +129,41 @@
         send_ref[c] = chip.astype(BF16)
 
 
-def chain_kernel(count, steps, chip_map, first, chip, *refs):
-    waves, maps = refs[:count], refs[count : 2 * count - 1]
-    own_ref, other_ref, keep = refs[2 * count - 1 :]
-    core = this_core()
-    entering = (waves[-1][0], waves[-1][1])
-    for n in range(count - 2, -1, -1):
-        moved = times(entering, (maps[n][0], maps[n][1]))
-        entering = tuple((moved[c] + waves[n][c].astype(F32)).astype(BF16) for c in range(2))
-    at_first = times(entering, (steps[0, 0], steps[0, 1]))
-    at_second = times(entering, (chip_map[0], chip_map[1]))
+def chain_kernel(chips, steps, chip_map, first, chip_wave, *refs):
+    waves, maps = refs[: chips - 1], refs[chips - 1 : -4]
+    own_ref, other_ref, entering, keep = refs[-4:]
+    core, chip = this_core(), lax.div(lax.axis_index("wire"), 2)
+
+    @pl.when(chip == 0)
+    def _():
+        entering[...] = jnp.zeros_like(entering)
+
+    for here in range(1, chips):
+
+        @pl.when(chip == here)
+        def _():
+            wave = pair(waves[here - 1])
+            for source in range(1, here):
+                moved = times(wave, pair(maps[here - source - 1]))
+                added = pair(waves[(here ^ source) - 1])
+                wave = tuple((moved[c] + added[c].astype(F32)).astype(BF16) for c in range(2))
+            entering[0], entering[1] = wave
+
+    finish(core, pair(entering), steps, chip_map, first, chip_wave, own_ref, other_ref, keep)
+
+
+def finish(core, wave, steps, chip_map, first, chip_wave, own_ref, other_ref, keep):
+    at_first = times(wave, (steps[0, 0], steps[0, 1]))
+    at_second = times(wave, pair(chip_map))
     for c in range(2):
         keep[0, c] = (at_first[c] + first[c]).astype(BF16)
-        keep[1, c] = (at_second[c] + chip[c]).astype(BF16)
+        keep[1, c] = (at_second[c] + chip_wave[c]).astype(BF16)
     own_ref[...] = keep[core]
     other_ref[...] = keep[1 - core]
+
+
+def passed_kernel(steps, chip_map, first, chip_wave, entering, own_ref, other_ref, keep):
+    finish(this_core(), pair(entering), steps, chip_map, first, chip_wave, own_ref, other_ref, keep)
 
 
 def across(lhs, rhs):
@@ -221,6 +241,10 @@
         ]
         return lax.ppermute(value, ("energy", "wire"), pairs)
 
+    def exchange(value, offset):
+        pairs = [(w, w ^ (2 * offset)) for w in range(segments)]
+        return lax.ppermute(value, "wire", pairs)
+
     def later(value, hops, least=0):
         pairs = []
         for chip in range(least, chips - hops):
@@ -278,24 +302,20 @@
         [],
         [own, other, steps, greens],
         [((2,) + wave, BF16)])
-    if chips <= 4:
-        maps = [later(chip_map, hops, 1) for hops in range(1, chips - 1)]
-        arrived = [later(chip_send, hops) for hops in range(1, chips)]
+    kept = [((2,) + wave, BF16)]
+    if chips in (1, 2, 4):
+        kernel, kept = functools.partial(chain_kernel, chips), [(wave, BF16)] + kept
+        arrived = [exchange(chip_send, offset) for offset in range(1, chips)]
+        arrived += [later(chip_map, hops, 1) for hops in range(1, chips - 1)]
     else:
-        maps = []
+        kernel = passed_kernel
         entering = jnp.zeros_like(chip_send)
         for at in range(chips - 1):
             leaving = (complex_matrix(entering, chip_map) + chip).astype(BF16)
             pairs = [(2 * at + b, 2 * at + 2 + b) for b in range(2)]
             entering = entering + lax.ppermute(leaving, "wire", pairs)
         arrived = [entering]
-    own, other = call(
-        functools.partial(chain_kernel, len(arrived)),
-        "chain",
-        [(wave, BF16)] * 2,
-        [],
-        [steps, chip_map, first, chip] + arrived + maps,
-        [((2,) + wave, BF16)])
+    own, other = call(kernel, "chain", [(wave, BF16)] * 2, [], [steps, chip_map, first, chip] + arrived, kept)
 
     other = swap(other, 0, 1)
     filled = green_blocks(0, counts, incident, own)

time: 63.5 us -> 60.8 us (0.957); the launches traced: 62.6 us -> 60.7 us
  starting transfers between devices: 27.2 us -> 23.4 us
  waiting for transfers between devices: 20.8 us -> 23.5 us
  Pallas kernels: 11 us -> 10.2 us
    ppermute x5 -> x2, starting transfers between devices: 8.4 us -> 1.46 us  [later(): return lax.ppermute(value, 'wire', pairs)]
    ppermute x0 -> x3, waiting for transfers between devices: none -> 5.18 us  [exchange(): return lax.ppermute(value, 'wire', pairs)]
    ppermute x5 -> x2, waiting for transfers between devices: 3.12 us -> 0.01 us  [later(): return lax.ppermute(value, 'wire', pairs)]
    ppermute x0 -> x3, starting transfers between devices: none -> 2.71 us  [exchange(): return lax.ppermute(value, 'wire', pairs)]
    pallas_call x7, Pallas kernels: 5.63 us -> 4.8 us  [call(): pl.pallas_call(kernel, out_shape=shapes, in_specs=[SMEM] * len(scalars) +...]
  transfers between devices with their start and end apart: 15 -> 15, of which waited for: 7 -> 8; matrix products, arithmetic and copies ran while one was open for 2% -> 2% of each run, Pallas kernels for 14% -> 14%
where the time goes in v4:
time: 60.8 us; the launch traced here: 60.7 us
  waiting for transfers between devices  23.5 us (39%)
  starting transfers between devices  23.4 us (38%)
  Pallas kernels  10.2 us (17%)
  between operations  2.05 us (3%)
  other arithmetic  1.49 us (2%)
    ppermute x10, starting transfers between devices, swap(): return lax.ppermute(value, ('energy', 'wire'), pairs)  19.3 us
    ppermute x10, waiting for transfers between devices, swap(): return lax.ppermute(value, ('energy', 'wire'), pairs)  18.3 us
    ppermute x3, waiting for transfers between devices, exchange(): return lax.ppermute(value, 'wire', pairs)  5.18 us
    pallas_call x7, Pallas kernels, call(): pl.pallas_call(kernel, out_shape=shapes, in_specs=[SMEM] * len(scalars) +...  4.8 us
    ppermute x3, starting transfers between devices, exchange(): return lax.ppermute(value, 'wire', pairs)  2.71 us
    pallas_call x2, Pallas kernels, green_blocks(): pl.pallas_call(functools.partial(block_kernel, turn), out_shape=[jax.Shap...  2.69 us
    pallas_call x1, Pallas kernels, shards(): pl.pallas_call(prepare_kernel, out_shape=[jax.ShapeDtypeStruct((2,) + blo...  2.69 us
    ppermute x2, starting transfers between devices, later(): return lax.ppermute(value, 'wire', pairs)  1.46 us
  transfers between devices with their start and end apart: 15, of which 8 were waited for; matrix products, arithmetic and copies ran while one was open for 2% of the time, Pallas kernels for 14%

profile of v4, /device:TPU:1, one launch (start us, length us, event | category | flops | bytes accessed | tf_op | source)
XLA Modules:
  0.0 60.7 jit_solution(8825502817986670227)
XLA Ops:
  0.6 0.1 collective-permute-start
  0.8 0.5 collective-permute-start.1
  1.2 2.4 %collective-permute-start.2 = (bf16[2,2,64,512]{3,2,1,0:T(8,128)(2,1)}, bf16[2,2,64,512]{3,2,1,0:T(8,128)(2,1)S(1)}, u32[]{:S(2)}, u32[]{:S(2)}) collective-permute-start(bf16[2,2,64,512]{3,2,1,0:T(8,128)(2,1)} %bitcast.14), channel_id=1, source_target_pairs={{0,8},{1,9},{2,10},{3,11},{4,12},{5,13},{6,14},{7,15},{8,0},{9,1},... | collective-permute-start | bytes 786440 | tf_op jit(solution)/shard_map/ppermute | solution.py:242
  3.6 2.3 %collective-permute-start.3 = (bf16[2,2,64,512]{3,2,1,0:T(8,128)(2,1)}, bf16[2,2,64,512]{3,2,1,0:T(8,128)(2,1)S(1)}, u32[]{:S(2)}, u32[]{:S(2)}) collective-permute-start(bf16[2,2,64,512]{3,2,1,0:T(8,128)(2,1)} %bitcast.15), channel_id=1, source_target_pairs={{0,16},{1,17},{2,18},{3,19},{4,20},{5,21},{6,22},{7,23},{8,24},{9,... | collective-permute-start | bytes 786440 | tf_op jit(solution)/shard_map/ppermute | solution.py:242
  6.5 0.7 %pad_maximum_fusion.real_valued = f32[18]{0:T(128)S(1)} fusion(f32[16]{0:T(128)} %param.18, f32[2]{0:T(128)} %param.19), kind=kLoop, calls=%fused_computation.1 | loop fusion | flops 18 | bytes 144 | tf_op jit(solution)/shard_map/concatenate | solution.py:256
  7.3 0.7 %pad_add_fusion.whole = s32[17]{0:T(128)S(1)} fusion(s32[1]{0:T(128)S(6)} %copy.19, s32[8]{0:T(128)} %param.15, s32[8]{0:T(128)} %param.14), kind=kLoop, calls=%fused_computation | loop fusion | flops 34 | bytes 136 | tf_op jit(solution)/shard_map/concatenate | solution.py:255
  8.0 0.0 copy-start
  8.0 0.0 collective-permute-done.prop_other
  8.0 0.0 collective-permute-done.1.green_other
  8.1 2.7 %prepare.1 = (bf16[2,2,512,512]{3,2,1,0:T(8,128)(2,1)S(1)}, bf16[2,2,512,512]{3,2,1,0:T(8,128)(2,1)S(1)}, bf16[2,512,512]{2,1,0:T(8,128)(2,1)S(1)}) custom-call(bf16[2,2,512,512]{3,2,1,0:T(8,128)(2,1)} %bitcast.20, bf16[2,2,512,512]{3,2,1,0:T(8,128)(2,1)S(1)} %collective-permute-done.prop_other, bf16[2,2,512,512]{3,2,1,0:T(8,128)(2,1)} %bitcast.22, ...), custom_call_target="tpu_custom_call" | custom-call | flops 3000000000 | bytes 1 | tf_op jit(solution)/shard_map/prepare/pallas_call | solution.py:267
  10.8 0.7 %collective-permute-start.12 = (bf16[2,512,512]{2,1,0:T(8,128)(2,1)S(1)}, bf16[2,512,512]{2,1,0:T(8,128)(2,1)S(1)}, u32[]{:S(2)}, u32[]{:S(2)}) collective-permute-start(bf16[2,512,512]{2,1,0:T(8,128)(2,1)S(1)} %get-tuple-element.22.chip_map), channel_id=1, source_target_pairs={{2,4},{3,5},{4,6},{5,7},{10,12},{11,13},{12,14},{13,15},{18,20},{1... | collective-permute-start | bytes 3145736 | tf_op jit(solution)/shard_map/ppermute | solution.py:252
  11.5 0.7 %collective-permute-start.13 = (bf16[2,512,512]{2,1,0:T(8,128)(2,1)S(1)}, bf16[2,512,512]{2,1,0:T(8,128)(2,1)S(1)}, u32[]{:S(2)}, u32[]{:S(2)}) collective-permute-start(bf16[2,512,512]{2,1,0:T(8,128)(2,1)S(1)} %get-tuple-element.22.chip_map), channel_id=1, source_target_pairs={{2,6},{3,7},{10,14},{11,15},{18,22},{19,23},{26,30},{27,31}} | collective-permute-start | bytes 3145736 | tf_op jit(solution)/shard_map/ppermute | solution.py:252
  12.2 3.3 %collective-permute-done.2.wave_ref = bf16[2,2,64,512]{3,2,1,0:T(8,128)(2,1)S(1)} collective-permute-done((bf16[2,2,64,512]{3,2,1,0:T(8,128)(2,1)}, bf16[2,2,64,512]{3,2,1,0:T(8,128)(2,1)S(1)}, u32[]{:S(2)}, u32[]{:S(2)}) %collective-permute-start.2) | collective-permute-done | bytes 262176 | tf_op jit(solution)/shard_map/ppermute | solution.py:242
  15.6 0.0 collective-permute-done.3.wave_ref
  15.6 2.3 %collective-permute-start.4 = (bf16[2,2,64,512]{3,2,1,0:T(8,128)(2,1)S(1)}, bf16[2,2,64,512]{3,2,1,0:T(8,128)(2,1)S(1)}, u32[]{:S(2)}, u32[]{:S(2)}) collective-permute-start(bf16[2,2,64,512]{3,2,1,0:T(8,128)(2,1)S(1)} %collective-permute-done.3.wave_ref), channel_id=1, source_target_pairs={{0,8},{1,9},{2,10},{3,11},{4,12},{5,13},{6,14},{7,15},{8,0},{9,1},... | collective-permute-start | bytes 786440 | tf_op jit(solution)/shard_map/ppermute | solution.py:242
  17.9 0.0 copy-done
  17.9 0.9 %product.5 = bf16[2,2,64,512]{3,2,1,0:T(8,128)(2,1)S(1)} custom-call(s32[17]{0:T(128)S(1)} %pad_add_fusion.whole, f32[18]{0:T(128)S(1)} %pad_maximum_fusion.real_valued, bf16[2,2,64,512]{3,2,1,0:T(8,128)(2,1)S(1)} %collective-permute-done.3.wave_ref, bf16[2,2,512,512]{3,2,1,0:T(8,128)(2,1)S(1)} %bitcast.10), custom_call_target="tpu_custom_call" | custom-call | flops 3000000000 | bytes 1 | tf_op jit(solution)/shard_map/product/pallas_call | solution.py:19
  18.9 1.9 %collective-permute-start.6 = (bf16[2,2,64,512]{3,2,1,0:T(8,128)(2,1)S(1)}, bf16[2,2,64,512]{3,2,1,0:T(8,128)(2,1)S(1)}, u32[]{:S(2)}, u32[]{:S(2)}) collective-permute-start(bf16[2,2,64,512]{3,2,1,0:T(8,128)(2,1)S(1)} %product.5), channel_id=1, source_target_pairs={{0,16},{1,17},{2,18},{3,19},{4,20},{5,21},{6,22},{7,23},{8,24},{9,... | collective-permute-start | bytes 786440 | tf_op jit(solution)/shard_map/ppermute | solution.py:242
  20.7 0.9 %product.3 = bf16[2,2,64,512]{3,2,1,0:T(8,128)(2,1)S(1)} custom-call(s32[17]{0:T(128)S(1)} %pad_add_fusion.whole, f32[18]{0:T(128)S(1)} %pad_maximum_fusion.real_valued, bf16[2,2,64,512]{3,2,1,0:T(8,128)(2,1)S(1)} %collective-permute-done.2.wave_ref, bf16[2,2,512,512]{3,2,1,0:T(8,128)(2,1)S(1)} %bitcast.11), custom_call_target="tpu_custom_call" | custom-call | flops 3000000000 | bytes 1 | tf_op jit(solution)/shard_map/product/pallas_call | solution.py:19
  21.6 0.0 copy-start.1
  21.7 0.5 collective-permute-done.4.wave_ref
  22.2 0.9 %product.4 = bf16[2,2,64,512]{3,2,1,0:T(8,128)(2,1)S(1)} custom-call(s32[17]{0:T(128)S(1)} %pad_add_fusion.whole, f32[18]{0:T(128)S(1)} %pad_maximum_fusion.real_valued, bf16[2,2,64,512]{3,2,1,0:T(8,128)(2,1)S(1)} %collective-permute-done.4.wave_ref, bf16[2,2,512,512]{3,2,1,0:T(8,128)(2,1)S(1)} %bitcast.12), custom_call_target="tpu_custom_call" | custom-call | flops 3000000000 | bytes 1 | tf_op jit(solution)/shard_map/product/pallas_call | solution.py:19
  23.1 7.3 %collective-permute-start.7 = (bf16[2,2,64,512]{3,2,1,0:T(8,128)(2,1)S(1)}, bf16[2,2,64,512]{3,2,1,0:T(8,128)(2,1)S(1)}, u32[]{:S(2)}, u32[]{:S(2)}) collective-permute-start(bf16[2,2,64,512]{3,2,1,0:T(8,128)(2,1)S(1)} %product.4), channel_id=1, source_target_pairs={{0,24},{1,25},{2,26},{3,27},{4,28},{5,29},{6,30},{7,31},{8,16},{9,... | collective-permute-start | bytes 786440 | tf_op jit(solution)/shard_map/ppermute | solution.py:242
  30.4 0.0 collective-permute-start.5
  30.4 0.0 copy-done.1
  30.4 0.7 %own.1.base = f32[2,2,64,512]{3,2,1,0:T(8,128)S(1)} custom-call(s32[17]{0:T(128)S(1)} %pad_add_fusion.whole, f32[18]{0:T(128)S(1)} %pad_maximum_fusion.real_valued, bf16[2,2,64,512]{3,2,1,0:T(8,128)(2,1)S(1)} %bitcast.16, bf16[2,2,512,512]{3,2,1,0:T(8,128)(2,1)S(1)} %bitcast.13), custom_call_target="tpu_custom_call" | custom-call | flops 3000000000 | bytes 1 | tf_op jit(solution)/shard_map/own/pallas_call | solution.py:19
  31.0 0.0 collective-permute-done.6.refs_1_
  31.1 3.9 %collective-permute-done.7.refs_2_ = bf16[2,2,64,512]{3,2,1,0:T(8,128)(2,1)S(1)} collective-permute-done((bf16[2,2,64,512]{3,2,1,0:T(8,128)(2,1)S(1)}, bf16[2,2,64,512]{3,2,1,0:T(8,128)(2,1)S(1)}, u32[]{:S(2)}, u32[]{:S(2)}) %collective-permute-start.7) | collective-permute-done | bytes 262176 | tf_op jit(solution)/shard_map/ppermute | solution.py:242
  34.9 9.6 %collective-permute-done.5.refs_0_ = bf16[2,2,64,512]{3,2,1,0:T(8,128)(2,1)S(1)} collective-permute-done((bf16[2,2,64,512]{3,2,1,0:T(8,128)(2,1)S(1)}, bf16[2,2,64,512]{3,2,1,0:T(8,128)(2,1)S(1)}, u32[]{:S(2)}, u32[]{:S(2)}) %collective-permute-start.5) | collective-permute-done | bytes 262176 | tf_op jit(solution)/shard_map/ppermute | solution.py:242
  44.5 0.1 term.1
  44.6 1.0 %collective-permute-start.8 = (bf16[2,64,512]{2,1,0:T(8,128)(2,1)S(1)}, bf16[2,64,512]{2,1,0:T(8,128)(2,1)S(1)}, u32[]{:S(2)}, u32[]{:S(2)}) collective-permute-start(bf16[2,64,512]{2,1,0:T(8,128)(2,1)S(1)} %get-tuple-element.29), channel_id=1, source_target_pairs={{0,1},{1,0},{2,3},{3,2},{4,5},{5,4},{6,7},{7,6},{8,9},{9,8},{10,11... | collective-permute-start | bytes 393224 | tf_op jit(solution)/shard_map/ppermute | solution.py:242
  45.6 1.0 %collective-permute-done.8.other = bf16[2,64,512]{2,1,0:T(8,128)(2,1)S(1)} collective-permute-done((bf16[2,64,512]{2,1,0:T(8,128)(2,1)S(1)}, bf16[2,64,512]{2,1,0:T(8,128)(2,1)S(1)}, u32[]{:S(2)}, u32[]{:S(2)}) %collective-permute-start.8) | collective-permute-done | bytes 131104 | tf_op jit(solution)/shard_map/ppermute | solution.py:242
  46.6 0.7 %source.1 = (f32[2,64,512]{2,1,0:T(8,128)S(1)}, f32[2,64,512]{2,1,0:T(8,128)S(1)}, bf16[2,64,512]{2,1,0:T(8,128)(2,1)S(1)}) custom-call(bf16[2,64,512]{2,1,0:T(8,128)(2,1)S(1)} %get-tuple-element.28.own, bf16[2,64,512]{2,1,0:T(8,128)(2,1)S(1)} %collective-permute-done.8.other, bf16[2,2,512,512]{3,2,1,0:T(8,128)(2,1)S(1)} %get-tuple-element.21.steps, ...), custom_call_target="tpu_custom_call" | custom-call | flops 3000000000 | bytes 1 | tf_op jit(solution)/shard_map/source/pallas_call | solution.py:19
  47.3 1.3 %collective-permute-start.10 = (bf16[2,64,512]{2,1,0:T(8,128)(2,1)S(1)}, bf16[2,64,512]{2,1,0:T(8,128)(2,1)S(1)}, u32[]{:S(2)}, u32[]{:S(2)}) collective-permute-start(bf16[2,64,512]{2,1,0:T(8,128)(2,1)S(1)} %get-tuple-element.33), channel_id=1, source_target_pairs={{0,4},{1,5},{2,6},{3,7},{4,0},{5,1},{6,2},{7,3},{8,12},{9,13},{10,... | collective-permute-start | bytes 393224 | tf_op jit(solution)/shard_map/ppermute | solution.py:246
  48.7 1.0 %collective-permute-start.11 = (bf16[2,64,512]{2,1,0:T(8,128)(2,1)S(1)}, bf16[2,64,512]{2,1,0:T(8,128)(2,1)S(1)}, u32[]{:S(2)}, u32[]{:S(2)}) collective-permute-start(bf16[2,64,512]{2,1,0:T(8,128)(2,1)S(1)} %get-tuple-element.33), channel_id=1, source_target_pairs={{0,6},{1,7},{2,4},{3,5},{4,2},{5,3},{6,0},{7,1},{8,14},{9,15},{10,... | collective-permute-start | bytes 393224 | tf_op jit(solution)/shard_map/ppermute | solution.py:246
  49.7 0.4 collective-permute-start.9
  50.7 2.5 %collective-permute-done.10.refs_1_ = bf16[2,64,512]{2,1,0:T(8,128)(2,1)S(1)} collective-permute-done((bf16[2,64,512]{2,1,0:T(8,128)(2,1)S(1)}, bf16[2,64,512]{2,1,0:T(8,128)(2,1)S(1)}, u32[]{:S(2)}, u32[]{:S(2)}) %collective-permute-start.10) | collective-permute-done | bytes 131104 | tf_op jit(solution)/shard_map/ppermute | solution.py:246
  53.3 0.8 %collective-permute-done.11.refs_2_ = bf16[2,64,512]{2,1,0:T(8,128)(2,1)S(1)} collective-permute-done((bf16[2,64,512]{2,1,0:T(8,128)(2,1)S(1)}, bf16[2,64,512]{2,1,0:T(8,128)(2,1)S(1)}, u32[]{:S(2)}, u32[]{:S(2)}) %collective-permute-start.11) | collective-permute-done | bytes 131104 | tf_op jit(solution)/shard_map/ppermute | solution.py:246
  54.0 1.9 %collective-permute-done.9.refs_0_ = bf16[2,64,512]{2,1,0:T(8,128)(2,1)S(1)} collective-permute-done((bf16[2,64,512]{2,1,0:T(8,128)(2,1)S(1)}, bf16[2,64,512]{2,1,0:T(8,128)(2,1)S(1)}, u32[]{:S(2)}, u32[]{:S(2)}) %collective-permute-start.9) | collective-permute-done | bytes 131104 | tf_op jit(solution)/shard_map/ppermute | solution.py:246
  55.9 0.0 collective-permute-done.12.refs_3_
  55.9 0.0 collective-permute-done.13.refs_4_
  55.9 0.5 chain.1
  56.4 1.5 %collective-permute-start.14 = (bf16[2,64,512]{2,1,0:T(8,128)(2,1)S(1)}, bf16[2,64,512]{2,1,0:T(8,128)(2,1)S(1)}, u32[]{:S(2)}, u32[]{:S(2)}) collective-permute-start(bf16[2,64,512]{2,1,0:T(8,128)(2,1)S(1)} %get-tuple-element.34), channel_id=1, source_target_pairs={{0,1},{1,0},{2,3},{3,2},{4,5},{5,4},{6,7},{7,6},{8,9},{9,8},{10,11... | collective-permute-start | bytes 393224 | tf_op jit(solution)/shard_map/ppermute | solution.py:242
  58.0 1.3 %green_blocks.2 = (bf16[2,2,64,512]{3,2,1,0:T(8,128)(2,1)}, bf16[2,2,512,512]{3,2,1,0:T(8,128)(2,1)}) custom-call(s32[1]{0:T(128)S(6)} %copy.18.counts, bf16[2,2,64,512]{3,2,1,0:T(8,128)(2,1)S(1)} %bitcast.17, bf16[2,64,512]{2,1,0:T(8,128)(2,1)S(1)} %get-tuple-element.35.chained), custom_call_target="tpu_custom_call" | custom-call | flops 3000000000 | bytes 1 | tf_op jit(solution)/shard_map/green_blocks/pallas_call | solution.py:201
  59.3 0.0 collective-permute-done.14.chained
  59.3 1.3 %green_blocks.3 = (bf16[2,2,64,512]{3,2,1,0:T(8,128)(2,1)}, bf16[2,2,512,512]{3,2,1,0:T(8,128)(2,1)}) custom-call(s32[1]{0:T(128)S(6)} %copy.18.counts, bf16[2,2,64,512]{3,2,1,0:T(8,128)(2,1)S(1)} %bitcast.18, bf16[2,64,512]{2,1,0:T(8,128)(2,1)S(1)} %collective-permute-done.14.chained, ...), custom_call_target="tpu_custom_call", output_to_operand_aliasing={{0}: (3, {}), {1}: (4, {})} | custom-call | flops 3000000000 | bytes 1 | tf_op jit(solution)/shard_map/green_blocks/pallas_call | solution.py:201
Async XLA Ops:
  0.6 7.4 %collective-permute-start = (bf16[2,2,512,512]{3,2,1,0:T(8,128)(2,1)}, bf16[2,2,512,512]{3,2,1,0:T(8,128)(2,1)S(1)}, u32[]{:S(2)}, u32[]{:S(2)}) collective-permute-start(bf16[2,2,512,512]{3,2,1,0:T(8,128)(2,1)} %bitcast.19), channel_id=1, source_target_pairs={{0,1},{1,0},{2,3},{3,2},{4,5},{5,4},{6,7},{7,6},{8,9},{9,8},{10,11... | collective-permute-start | bytes 6291464 | tf_op jit(solution)/shard_map/ppermute | solution.py:242
  0.8 7.3 %collective-permute-start.1 = (bf16[2,2,512,512]{3,2,1,0:T(8,128)(2,1)}, bf16[2,2,512,512]{3,2,1,0:T(8,128)(2,1)S(1)}, u32[]{:S(2)}, u32[]{:S(2)}) collective-permute-start(bf16[2,2,512,512]{3,2,1,0:T(8,128)(2,1)} %bitcast.21), channel_id=1, source_target_pairs={{0,1},{1,0},{2,3},{3,2},{4,5},{5,4},{6,7},{7,6},{8,9},{9,8},{10,11... | collective-permute-start | bytes 6291464 | tf_op jit(solution)/shard_map/ppermute | solution.py:242
  1.2 14.4 %collective-permute-start.2 = (bf16[2,2,64,512]{3,2,1,0:T(8,128)(2,1)}, bf16[2,2,64,512]{3,2,1,0:T(8,128)(2,1)S(1)}, u32[]{:S(2)}, u32[]{:S(2)}) collective-permute-start(bf16[2,2,64,512]{3,2,1,0:T(8,128)(2,1)} %bitcast.14), channel_id=1, source_target_pairs={{0,8},{1,9},{2,10},{3,11},{4,12},{5,13},{6,14},{7,15},{8,0},{9,1},... | collective-permute-start | bytes 786440 | tf_op jit(solution)/shard_map/ppermute | solution.py:242
  3.6 12.0 %collective-permute-start.3 = (bf16[2,2,64,512]{3,2,1,0:T(8,128)(2,1)}, bf16[2,2,64,512]{3,2,1,0:T(8,128)(2,1)S(1)}, u32[]{:S(2)}, u32[]{:S(2)}) collective-permute-start(bf16[2,2,64,512]{3,2,1,0:T(8,128)(2,1)} %bitcast.15), channel_id=1, source_target_pairs={{0,16},{1,17},{2,18},{3,19},{4,20},{5,21},{6,22},{7,23},{8,24},{9,... | collective-permute-start | bytes 786440 | tf_op jit(solution)/shard_map/ppermute | solution.py:242
  8.0 9.9 %copy-start = (bf16[2,2,1,512,512]{4,3,2,1,0:T(8,128)(2,1)S(1)}, bf16[2,2,1,512,512]{4,3,2,1,0:T(8,128)(2,1)}, u32[]{:S(2)}) copy-start(bf16[2,2,1,512,512]{4,3,2,1,0:T(8,128)(2,1)} %param.10) | copy-start | bytes 6291460
  10.8 45.1 %collective-permute-start.12 = (bf16[2,512,512]{2,1,0:T(8,128)(2,1)S(1)}, bf16[2,512,512]{2,1,0:T(8,128)(2,1)S(1)}, u32[]{:S(2)}, u32[]{:S(2)}) collective-permute-start(bf16[2,512,512]{2,1,0:T(8,128)(2,1)S(1)} %get-tuple-element.22.chip_map), channel_id=1, source_target_pairs={{2,4},{3,5},{4,6},{5,7},{10,12},{11,13},{12,14},{13,15},{18,20},{1... | collective-permute-start | bytes 3145736 | tf_op jit(solution)/shard_map/ppermute | solution.py:252
  11.5 44.4 %collective-permute-start.13 = (bf16[2,512,512]{2,1,0:T(8,128)(2,1)S(1)}, bf16[2,512,512]{2,1,0:T(8,128)(2,1)S(1)}, u32[]{:S(2)}, u32[]{:S(2)}) collective-permute-start(bf16[2,512,512]{2,1,0:T(8,128)(2,1)S(1)} %get-tuple-element.22.chip_map), channel_id=1, source_target_pairs={{2,6},{3,7},{10,14},{11,15},{18,22},{19,23},{26,30},{27,31}} | collective-permute-start | bytes 3145736 | tf_op jit(solution)/shard_map/ppermute | solution.py:252
  15.6 6.6 %collective-permute-start.4 = (bf16[2,2,64,512]{3,2,1,0:T(8,128)(2,1)S(1)}, bf16[2,2,64,512]{3,2,1,0:T(8,128)(2,1)S(1)}, u32[]{:S(2)}, u32[]{:S(2)}) collective-permute-start(bf16[2,2,64,512]{3,2,1,0:T(8,128)(2,1)S(1)} %collective-permute-done.3.wave_ref), channel_id=1, source_target_pairs={{0,8},{1,9},{2,10},{3,11},{4,12},{5,13},{6,14},{7,15},{8,0},{9,1},... | collective-permute-start | bytes 786440 | tf_op jit(solution)/shard_map/ppermute | solution.py:242
  18.9 12.2 %collective-permute-start.6 = (bf16[2,2,64,512]{3,2,1,0:T(8,128)(2,1)S(1)}, bf16[2,2,64,512]{3,2,1,0:T(8,128)(2,1)S(1)}, u32[]{:S(2)}, u32[]{:S(2)}) collective-permute-start(bf16[2,2,64,512]{3,2,1,0:T(8,128)(2,1)S(1)} %product.5), channel_id=1, source_target_pairs={{0,16},{1,17},{2,18},{3,19},{4,20},{5,21},{6,22},{7,23},{8,24},{9,... | collective-permute-start | bytes 786440 | tf_op jit(solution)/shard_map/ppermute | solution.py:242
  21.6 8.7 %copy-start.1 = (bf16[2,2,1,64,512]{4,3,2,1,0:T(8,128)(2,1)S(1)}, bf16[2,2,1,64,512]{4,3,2,1,0:T(8,128)(2,1)}, u32[]{:S(2)}) copy-start(bf16[2,2,1,64,512]{4,3,2,1,0:T(8,128)(2,1)} %param.13) | copy-start | bytes 786436
  23.1 11.8 %collective-permute-start.7 = (bf16[2,2,64,512]{3,2,1,0:T(8,128)(2,1)S(1)}, bf16[2,2,64,512]{3,2,1,0:T(8,128)(2,1)S(1)}, u32[]{:S(2)}, u32[]{:S(2)}) collective-permute-start(bf16[2,2,64,512]{3,2,1,0:T(8,128)(2,1)S(1)} %product.4), channel_id=1, source_target_pairs={{0,24},{1,25},{2,26},{3,27},{4,28},{5,29},{6,30},{7,31},{8,16},{9,... | collective-permute-start | bytes 786440 | tf_op jit(solution)/shard_map/ppermute | solution.py:242
  30.4 14.1 %collective-permute-start.5 = (bf16[2,2,64,512]{3,2,1,0:T(8,128)(2,1)S(1)}, bf16[2,2,64,512]{3,2,1,0:T(8,128)(2,1)S(1)}, u32[]{:S(2)}, u32[]{:S(2)}) collective-permute-start(bf16[2,2,64,512]{3,2,1,0:T(8,128)(2,1)S(1)} %product.3), channel_id=1, source_target_pairs={{0,8},{1,9},{2,10},{3,11},{4,12},{5,13},{6,14},{7,15},{8,0},{9,1},... | collective-permute-start | bytes 786440 | tf_op jit(solution)/shard_map/ppermute | solution.py:242
  44.6 2.0 %collective-permute-start.8 = (bf16[2,64,512]{2,1,0:T(8,128)(2,1)S(1)}, bf16[2,64,512]{2,1,0:T(8,128)(2,1)S(1)}, u32[]{:S(2)}, u32[]{:S(2)}) collective-permute-start(bf16[2,64,512]{2,1,0:T(8,128)(2,1)S(1)} %get-tuple-element.29), channel_id=1, source_target_pairs={{0,1},{1,0},{2,3},{3,2},{4,5},{5,4},{6,7},{7,6},{8,9},{9,8},{10,11... | collective-permute-start | bytes 393224 | tf_op jit(solution)/shard_map/ppermute | solution.py:242
  47.3 5.9 %collective-permute-start.10 = (bf16[2,64,512]{2,1,0:T(8,128)(2,1)S(1)}, bf16[2,64,512]{2,1,0:T(8,128)(2,1)S(1)}, u32[]{:S(2)}, u32[]{:S(2)}) collective-permute-start(bf16[2,64,512]{2,1,0:T(8,128)(2,1)S(1)} %get-tuple-element.33), channel_id=1, source_target_pairs={{0,4},{1,5},{2,6},{3,7},{4,0},{5,1},{6,2},{7,3},{8,12},{9,13},{10,... | collective-permute-start | bytes 393224 | tf_op jit(solution)/shard_map/ppermute | solution.py:246
  48.7 5.4 %collective-permute-start.11 = (bf16[2,64,512]{2,1,0:T(8,128)(2,1)S(1)}, bf16[2,64,512]{2,1,0:T(8,128)(2,1)S(1)}, u32[]{:S(2)}, u32[]{:S(2)}) collective-permute-start(bf16[2,64,512]{2,1,0:T(8,128)(2,1)S(1)} %get-tuple-element.33), channel_id=1, source_target_pairs={{0,6},{1,7},{2,4},{3,5},{4,2},{5,3},{6,0},{7,1},{8,14},{9,15},{10,... | collective-permute-start | bytes 393224 | tf_op jit(solution)/shard_map/ppermute | solution.py:246
  49.7 6.2 %collective-permute-start.9 = (bf16[2,64,512]{2,1,0:T(8,128)(2,1)S(1)}, bf16[2,64,512]{2,1,0:T(8,128)(2,1)S(1)}, u32[]{:S(2)}, u32[]{:S(2)}) collective-permute-start(bf16[2,64,512]{2,1,0:T(8,128)(2,1)S(1)} %get-tuple-element.33), channel_id=1, source_target_pairs={{0,2},{1,3},{2,0},{3,1},{4,6},{5,7},{6,4},{7,5},{8,10},{9,11},{10,... | collective-permute-start | bytes 393224 | tf_op jit(solution)/shard_map/ppermute | solution.py:246
  56.4 2.9 %collective-permute-start.14 = (bf16[2,64,512]{2,1,0:T(8,128)(2,1)S(1)}, bf16[2,64,512]{2,1,0:T(8,128)(2,1)S(1)}, u32[]{:S(2)}, u32[]{:S(2)}) collective-permute-start(bf16[2,64,512]{2,1,0:T(8,128)(2,1)S(1)} %get-tuple-element.34), channel_id=1, source_target_pairs={{0,1},{1,0},{2,3},{3,2},{4,5},{5,4},{6,7},{7,6},{8,9},{9,8},{10,11... | collective-permute-start | bytes 393224 | tf_op jit(solution)/shard_map/ppermute | solution.py:242

commit v5 on v4

--- a/solution.py
+++ b/solution.py
@@ -9,7 +9,7 @@
 
 VMEM = pl.BlockSpec(memory_space=pltpu.VMEM)
 SMEM = pl.BlockSpec(memory_space=pltpu.SMEM)
-COST = 3000000000
+COST = 2000000000
 F32, BF16 = jnp.float32, jnp.bfloat16
 
 
@@ -115,18 +115,80 @@
         copy.wait()
 
 
-def source_kernel(own, other, steps, greens, first_ref, chip_ref, send_ref, term):
-    core = this_core()
-    term[core], term[1 - core] = own[...], other[...]
-    first = times((term[0, 0], term[0, 1]), (greens[0, 0], greens[0, 1]))
-    first_ref[0], first_ref[1] = first
-    rounded = (first[0].astype(BF16), first[1].astype(BF16))
-    passed = times(rounded, (steps[1, 0], steps[1, 1]))
-    added = times((term[1, 0], term[1, 1]), (greens[1, 0], greens[1, 1]))
+def fold_kernel(steps, greens, folded):
+    half = folded.shape[1] // 2
+    for rows in (slice(0, half), slice(half, None)):
+        moved = times((greens[0, 0, rows], greens[0, 1, rows]), (steps[1, 0], steps[1, 1]))
+        for c in range(2):
+            folded[c, rows] = moved[c].astype(BF16)
+
+
+def from_segment(first, term, greens, folded, out_ref):
+    @pl.when(first)
+    def _():
+        out_ref[0], out_ref[1] = times(pair(term), pair(folded))
+
+    @pl.when(jnp.logical_not(first))
+    def _():
+        out_ref[0], out_ref[1] = times(pair(term), (greens[1, 0], greens[1, 1]))
+
+
+def own_part_kernel(own, greens, folded, out_ref):
+    from_segment(this_core() == 0, own, greens, folded, out_ref)
+
+
+def chip_kernel(part, other, greens, folded, chip_ref, send_ref, added):
+    from_segment(this_core() == 1, other, greens, folded, added)
     for c in range(2):
-        chip = passed[c] + added[c]
+        chip = part[c] + added[c]
         chip_ref[c] = chip
         send_ref[c] = chip.astype(BF16)
+
+
+def first_kernel(own, other, greens, first_ref):
+    for core, term in enumerate((own, other)):
+
+        @pl.when(this_core() == core)
+        def _():
+            first_ref[0], first_ref[1] = times(pair(term), (greens[0, 0], greens[0, 1]))
+
+
+def far_kernel(straight, across_corner, near_map, far_map, out_ref):
+    chip = lax.div(lax.axis_index("wire"), 2)
+    for here, (begin, added, step) in {
+        2: (straight, across_corner, near_map),
+        3: (across_corner, straight, far_map),
+    }.items():
+
+        @pl.when(chip == here)
+        def _():
+            moved = times(pair(begin), pair(step))
+            for c in range(2):
+                out_ref[c] = (moved[c] + added[c].astype(F32)).astype(BF16)
+
+    @pl.when(chip < 2)
+    def _():
+        out_ref[...] = jnp.zeros_like(out_ref)
+
+
+def near_kernel(steps, chip_map, first, chip_wave, beside, far, near_map, own_ref, other_ref, entering, keep):
+    chip = lax.div(lax.axis_index("wire"), 2)
+
+    @pl.when(chip == 1)
+    def _():
+        entering[...] = beside[...]
+
+    @pl.when(chip == 3)
+    def _():
+        moved = times(pair(far), pair(near_map))
+        for c in range(2):
+            entering[c] = (moved[c] + beside[c].astype(F32)).astype(BF16)
+
+    @pl.when(lax.rem(chip, 2) == 0)
+    def _():
+        entering[...] = far[...]
+
+    finish(this_core(), pair(entering), steps, chip_map, first, chip_wave, own_ref, other_ref, keep)
 
 
 def chain_kernel(chips, steps, chip_map, first, chip_wave, *refs):
@@ -186,11 +248,17 @@
         both[0, c * modes : (c + 1) * modes] = combined
         both[1, (1 - c) * modes : (2 - c) * modes] = -combined if c == 0 else combined
     stacked = both[0]
+    pieces = 2
+    size = stacked.shape[1] // pieces
     for c in range(2):
-        block = across(both[1 - c], stacked) / modes
-        blocks[c] = jnp.where(live, block, 0.0).astype(BF16)
-        copies.append(pltpu.make_async_copy(blocks.at[c], green_next.at[c, slot], sent.at[2 + c]))
-        copies[-1].start()
+        for n in range(pieces):
+            rows = slice(n * size, (n + 1) * size)
+            block = across(both[1 - c, :, rows], stacked) * (1.0 / modes)
+            blocks[c, rows] = jnp.where(live, block, 0.0).astype(BF16)
+            copies.append(
+                pltpu.make_async_copy(blocks.at[c, rows], green_next.at[c, slot, rows], sent.at[2 + c * pieces + n])
+            )
+            copies[-1].start()
     for copy in copies:
         copy.wait()
 
@@ -211,7 +279,7 @@
             pltpu.VMEM((2, 2 * modes, orbitals), BF16),
             pltpu.VMEM((2, modes, orbitals), BF16),
             pltpu.VMEM((2, orbitals, orbitals), BF16),
-            pltpu.SemaphoreType.DMA((4,)),
+            pltpu.SemaphoreType.DMA((6,)),
         ],
         compiler_params=pltpu.CompilerParams(vmem_limit_bytes=16 << 20),
         cost_estimate=pl.CostEstimate(flops=COST, bytes_accessed=1, transcendentals=0),
@@ -292,18 +360,24 @@
     back = [swap(part, offset + 1) for offset, part in enumerate(parts)]
     waves[0], parts[-1] = lax.optimization_barrier((incident, parts[-1]))
     base = call(own_kernel, "own", [(every, F32)], scalars, [waves[0], g_here], total)[0]
+    steps_late, greens_late, base = lax.optimization_barrier((steps, greens, base))
+    folded = call(fold_kernel, "fold", [(block, BF16)], [], [steps_late, greens_late])[0]
     own, other = call(term_kernel, "term", [(wave, BF16)] * 2, [], [base] + back)
     other = swap(other, 0, 1)
 
-    first, chip, chip_send = call(
-        source_kernel,
-        "source",
-        [(wave, F32), (wave, F32), (wave, BF16)],
-        [],
-        [own, other, steps, greens],
-        [((2,) + wave, BF16)])
+    part = call(own_part_kernel, "own_part", [(wave, F32)], [], [own, greens, folded])[0]
+    chip, chip_send = call(
+        chip_kernel, "chip_wave", [(wave, F32), (wave, BF16)], [], [part, other, greens, folded], [(wave, F32)]
+    )
+    first = call(first_kernel, "first", [(wave, F32)], [], [own, other, greens])[0]
     kept = [((2,) + wave, BF16)]
-    if chips in (1, 2, 4):
+    if chips == 4:
+        beside, straight, corner = [exchange(chip_send, offset) for offset in range(1, chips)]
+        near_map, far_map = [later(chip_map, hops, 1) for hops in range(1, chips - 1)]
+        far = call(far_kernel, "far", [(wave, BF16)], [], [straight, corner, near_map, far_map])[0]
+        kernel, kept = near_kernel, [(wave, BF16)] + kept
+        arrived = [beside, far, near_map]
+    elif chips < 3:
         kernel, kept = functools.partial(chain_kernel, chips), [(wave, BF16)] + kept
         arrived = [exchange(chip_send, offset) for offset in range(1, chips)]
         arrived += [later(chip_map, hops, 1) for hops in range(1, chips - 1)]

time: 60.8 us -> 60 us (0.987)
  waiting for transfers between devices: 23.5 us -> 21 us
  Pallas kernels: 10.2 us -> 11.2 us
    ppermute x10, waiting for transfers between devices: 18.3 us -> 15.5 us  [swap(): return lax.ppermute(value, ('energy', 'wire'), pairs)]
    pallas_call x7 -> x11, Pallas kernels: 4.8 us -> 5.97 us  [call(): pl.pallas_call(kernel, out_shape=shapes, in_specs=[SMEM] * len(scalars) +...]
  transfers between devices with their start and end apart: 15 -> 15, of which waited for: 8 -> 8; matrix products, arithmetic and copies ran while one was open for 2% -> 3% of each run, Pallas kernels for 14% -> 16%
where the time goes in v5:
time: 60 us; the launch traced here: 59.7 us
  starting transfers between devices  23.9 us (40%)
  waiting for transfers between devices  21 us (35%)
  Pallas kernels  11.2 us (19%)
  between operations  2.08 us (3%)
  other arithmetic  1.49 us (2%)
    ppermute x10, starting transfers between devices, swap(): return lax.ppermute(value, ('energy', 'wire'), pairs)  19.7 us
    ppermute x10, waiting for transfers between devices, swap(): return lax.ppermute(value, ('energy', 'wire'), pairs)  15.5 us
    pallas_call x11, Pallas kernels, call(): pl.pallas_call(kernel, out_shape=shapes, in_specs=[SMEM] * len(scalars) +...  5.97 us
    ppermute x3, waiting for transfers between devices, exchange(): return lax.ppermute(value, 'wire', pairs)  5.51 us
    ppermute x3, starting transfers between devices, exchange(): return lax.ppermute(value, 'wire', pairs)  2.71 us
    pallas_call x1, Pallas kernels, shards(): pl.pallas_call(prepare_kernel, out_shape=[jax.ShapeDtypeStruct((2,) + blo...  2.69 us
    pallas_call x2, Pallas kernels, green_blocks(): pl.pallas_call(functools.partial(block_kernel, turn), out_shape=[jax.Shap...  2.58 us
    ppermute x2, starting transfers between devices, later(): return lax.ppermute(value, 'wire', pairs)  1.46 us
  transfers between devices with their start and end apart: 15, of which 8 were waited for; matrix products, arithmetic and copies ran while one was open for 3% of the time, Pallas kernels for 16%

profile of v5, /device:TPU:1, one launch (start us, length us, event | category | flops | bytes accessed | tf_op | source)
XLA Modules:
  0.0 59.7 jit_solution(2573005602516607527)
XLA Ops:
  0.6 0.1 collective-permute-start
  0.8 0.5 collective-permute-start.1
  1.2 2.4 %collective-permute-start.2 = (bf16[2,2,64,512]{3,2,1,0:T(8,128)(2,1)}, bf16[2,2,64,512]{3,2,1,0:T(8,128)(2,1)S(1)}, u32[]{:S(2)}, u32[]{:S(2)}) collective-permute-start(bf16[2,2,64,512]{3,2,1,0:T(8,128)(2,1)} %bitcast.14), channel_id=1, source_target_pairs={{0,8},{1,9},{2,10},{3,11},{4,12},{5,13},{6,14},{7,15},{8,0},{9,1},... | collective-permute-start | bytes 786440 | tf_op jit(solution)/shard_map/ppermute | solution.py:310
  3.6 2.3 %collective-permute-start.3 = (bf16[2,2,64,512]{3,2,1,0:T(8,128)(2,1)}, bf16[2,2,64,512]{3,2,1,0:T(8,128)(2,1)S(1)}, u32[]{:S(2)}, u32[]{:S(2)}) collective-permute-start(bf16[2,2,64,512]{3,2,1,0:T(8,128)(2,1)} %bitcast.15), channel_id=1, source_target_pairs={{0,16},{1,17},{2,18},{3,19},{4,20},{5,21},{6,22},{7,23},{8,24},{9,... | collective-permute-start | bytes 786440 | tf_op jit(solution)/shard_map/ppermute | solution.py:310
  7.2 0.7 %pad_maximum_fusion.real_valued = f32[18]{0:T(128)S(1)} fusion(f32[16]{0:T(128)} %param.18, f32[2]{0:T(128)} %param.19), kind=kLoop, calls=%fused_computation.1 | loop fusion | flops 18 | bytes 144 | tf_op jit(solution)/shard_map/concatenate | solution.py:324
  7.9 0.7 %pad_add_fusion.whole = s32[17]{0:T(128)S(1)} fusion(s32[1]{0:T(128)S(6)} %copy.19, s32[8]{0:T(128)} %param.15, s32[8]{0:T(128)} %param.14), kind=kLoop, calls=%fused_computation | loop fusion | flops 34 | bytes 136 | tf_op jit(solution)/shard_map/concatenate | solution.py:323
  8.7 0.0 copy-start
  8.7 0.0 collective-permute-done.prop_other
  8.7 0.0 collective-permute-done.1.green_other
  8.7 2.7 %prepare.1 = (bf16[2,2,512,512]{3,2,1,0:T(8,128)(2,1)S(1)}, bf16[2,2,512,512]{3,2,1,0:T(8,128)(2,1)S(1)}, bf16[2,512,512]{2,1,0:T(8,128)(2,1)S(1)}) custom-call(bf16[2,2,512,512]{3,2,1,0:T(8,128)(2,1)} %bitcast.20, bf16[2,2,512,512]{3,2,1,0:T(8,128)(2,1)S(1)} %collective-permute-done.prop_other, bf16[2,2,512,512]{3,2,1,0:T(8,128)(2,1)} %bitcast.22, ...), custom_call_target="tpu_custom_call" | custom-call | flops 2000000000 | bytes 1 | tf_op jit(solution)/shard_map/prepare/pallas_call | solution.py:335
  11.4 0.7 %collective-permute-start.12 = (bf16[2,512,512]{2,1,0:T(8,128)(2,1)S(1)}, bf16[2,512,512]{2,1,0:T(8,128)(2,1)S(1)}, u32[]{:S(2)}, u32[]{:S(2)}) collective-permute-start(bf16[2,512,512]{2,1,0:T(8,128)(2,1)S(1)} %get-tuple-element.24.chip_map), channel_id=1, source_target_pairs={{2,4},{3,5},{4,6},{5,7},{10,12},{11,13},{12,14},{13,15},{18,20},{1... | collective-permute-start | bytes 3145736 | tf_op jit(solution)/shard_map/ppermute | solution.py:320
  12.1 0.7 %collective-permute-start.13 = (bf16[2,512,512]{2,1,0:T(8,128)(2,1)S(1)}, bf16[2,512,512]{2,1,0:T(8,128)(2,1)S(1)}, u32[]{:S(2)}, u32[]{:S(2)}) collective-permute-start(bf16[2,512,512]{2,1,0:T(8,128)(2,1)S(1)} %get-tuple-element.24.chip_map), channel_id=1, source_target_pairs={{2,6},{3,7},{10,14},{11,15},{18,22},{19,23},{26,30},{27,31}} | collective-permute-start | bytes 3145736 | tf_op jit(solution)/shard_map/ppermute | solution.py:320
  12.9 2.7 %collective-permute-done.2.wave_ref = bf16[2,2,64,512]{3,2,1,0:T(8,128)(2,1)S(1)} collective-permute-done((bf16[2,2,64,512]{3,2,1,0:T(8,128)(2,1)}, bf16[2,2,64,512]{3,2,1,0:T(8,128)(2,1)S(1)}, u32[]{:S(2)}, u32[]{:S(2)}) %collective-permute-start.2) | collective-permute-done | bytes 262176 | tf_op jit(solution)/shard_map/ppermute | solution.py:310
  15.6 0.0 collective-permute-done.3.wave_ref
  15.6 2.3 %collective-permute-start.4 = (bf16[2,2,64,512]{3,2,1,0:T(8,128)(2,1)S(1)}, bf16[2,2,64,512]{3,2,1,0:T(8,128)(2,1)S(1)}, u32[]{:S(2)}, u32[]{:S(2)}) collective-permute-start(bf16[2,2,64,512]{3,2,1,0:T(8,128)(2,1)S(1)} %collective-permute-done.3.wave_ref), channel_id=1, source_target_pairs={{0,8},{1,9},{2,10},{3,11},{4,12},{5,13},{6,14},{7,15},{8,0},{9,1},... | collective-permute-start | bytes 786440 | tf_op jit(solution)/shard_map/ppermute | solution.py:310
  17.9 0.0 copy-done
  17.9 0.6 %product.5 = bf16[2,2,64,512]{3,2,1,0:T(8,128)(2,1)S(1)} custom-call(s32[17]{0:T(128)S(1)} %pad_add_fusion.whole, f32[18]{0:T(128)S(1)} %pad_maximum_fusion.real_valued, bf16[2,2,64,512]{3,2,1,0:T(8,128)(2,1)S(1)} %collective-permute-done.3.wave_ref, bf16[2,2,512,512]{3,2,1,0:T(8,128)(2,1)S(1)} %bitcast.10), custom_call_target="tpu_custom_call" | custom-call | flops 2000000000 | bytes 1 | tf_op jit(solution)/shard_map/product/pallas_call | solution.py:19
  18.6 2.5 %collective-permute-start.6 = (bf16[2,2,64,512]{3,2,1,0:T(8,128)(2,1)S(1)}, bf16[2,2,64,512]{3,2,1,0:T(8,128)(2,1)S(1)}, u32[]{:S(2)}, u32[]{:S(2)}) collective-permute-start(bf16[2,2,64,512]{3,2,1,0:T(8,128)(2,1)S(1)} %product.5), channel_id=1, source_target_pairs={{0,16},{1,17},{2,18},{3,19},{4,20},{5,21},{6,22},{7,23},{8,24},{9,... | collective-permute-start | bytes 786440 | tf_op jit(solution)/shard_map/ppermute | solution.py:310
  21.0 0.9 %product.3 = bf16[2,2,64,512]{3,2,1,0:T(8,128)(2,1)S(1)} custom-call(s32[17]{0:T(128)S(1)} %pad_add_fusion.whole, f32[18]{0:T(128)S(1)} %pad_maximum_fusion.real_valued, bf16[2,2,64,512]{3,2,1,0:T(8,128)(2,1)S(1)} %collective-permute-done.2.wave_ref, bf16[2,2,512,512]{3,2,1,0:T(8,128)(2,1)S(1)} %bitcast.11), custom_call_target="tpu_custom_call" | custom-call | flops 2000000000 | bytes 1 | tf_op jit(solution)/shard_map/product/pallas_call | solution.py:19
  22.0 0.0 copy-start.1
  22.0 0.2 collective-permute-done.4.wave_ref
  22.2 0.9 %product.4 = bf16[2,2,64,512]{3,2,1,0:T(8,128)(2,1)S(1)} custom-call(s32[17]{0:T(128)S(1)} %pad_add_fusion.whole, f32[18]{0:T(128)S(1)} %pad_maximum_fusion.real_valued, bf16[2,2,64,512]{3,2,1,0:T(8,128)(2,1)S(1)} %collective-permute-done.4.wave_ref, bf16[2,2,512,512]{3,2,1,0:T(8,128)(2,1)S(1)} %bitcast.12), custom_call_target="tpu_custom_call" | custom-call | flops 2000000000 | bytes 1 | tf_op jit(solution)/shard_map/product/pallas_call | solution.py:19
  23.1 6.9 %collective-permute-start.7 = (bf16[2,2,64,512]{3,2,1,0:T(8,128)(2,1)S(1)}, bf16[2,2,64,512]{3,2,1,0:T(8,128)(2,1)S(1)}, u32[]{:S(2)}, u32[]{:S(2)}) collective-permute-start(bf16[2,2,64,512]{3,2,1,0:T(8,128)(2,1)S(1)} %product.4), channel_id=1, source_target_pairs={{0,24},{1,25},{2,26},{3,27},{4,28},{5,29},{6,30},{7,31},{8,16},{9,... | collective-permute-start | bytes 786440 | tf_op jit(solution)/shard_map/ppermute | solution.py:310
  30.1 0.0 collective-permute-start.5
  30.1 0.0 copy-done.1
  30.1 0.7 %own.1.base = f32[2,2,64,512]{3,2,1,0:T(8,128)S(1)} custom-call(s32[17]{0:T(128)S(1)} %pad_add_fusion.whole, f32[18]{0:T(128)S(1)} %pad_maximum_fusion.real_valued, bf16[2,2,64,512]{3,2,1,0:T(8,128)(2,1)S(1)} %bitcast.16, bf16[2,2,512,512]{3,2,1,0:T(8,128)(2,1)S(1)} %bitcast.13), custom_call_target="tpu_custom_call" | custom-call | flops 2000000000 | bytes 1 | tf_op jit(solution)/shard_map/own/pallas_call | solution.py:19
  30.7 1.3 %fold.1.folded = bf16[2,512,512]{2,1,0:T(8,128)(2,1)S(1)} custom-call(bf16[2,2,512,512]{3,2,1,0:T(8,128)(2,1)S(1)} %get-tuple-element.34.steps, bf16[2,2,512,512]{3,2,1,0:T(8,128)(2,1)S(1)} %get-tuple-element.35.greens), custom_call_target="tpu_custom_call" | custom-call | flops 2000000000 | bytes 1 | tf_op jit(solution)/shard_map/fold/pallas_call | solution.py:19
  32.0 0.0 collective-permute-done.6.refs_1_
  32.0 2.9 %collective-permute-done.7.refs_2_ = bf16[2,2,64,512]{3,2,1,0:T(8,128)(2,1)S(1)} collective-permute-done((bf16[2,2,64,512]{3,2,1,0:T(8,128)(2,1)S(1)}, bf16[2,2,64,512]{3,2,1,0:T(8,128)(2,1)S(1)}, u32[]{:S(2)}, u32[]{:S(2)}) %collective-permute-start.7) | collective-permute-done | bytes 262176 | tf_op jit(solution)/shard_map/ppermute | solution.py:310
  34.9 8.9 %collective-permute-done.5.refs_0_ = bf16[2,2,64,512]{3,2,1,0:T(8,128)(2,1)S(1)} collective-permute-done((bf16[2,2,64,512]{3,2,1,0:T(8,128)(2,1)S(1)}, bf16[2,2,64,512]{3,2,1,0:T(8,128)(2,1)S(1)}, u32[]{:S(2)}, u32[]{:S(2)}) %collective-permute-start.5) | collective-permute-done | bytes 262176 | tf_op jit(solution)/shard_map/ppermute | solution.py:310
  43.8 0.1 term.1
  44.0 1.2 %collective-permute-start.8 = (bf16[2,64,512]{2,1,0:T(8,128)(2,1)S(1)}, bf16[2,64,512]{2,1,0:T(8,128)(2,1)S(1)}, u32[]{:S(2)}, u32[]{:S(2)}) collective-permute-start(bf16[2,64,512]{2,1,0:T(8,128)(2,1)S(1)} %get-tuple-element.33), channel_id=1, source_target_pairs={{0,1},{1,0},{2,3},{3,2},{4,5},{5,4},{6,7},{7,6},{8,9},{9,8},{10,11... | collective-permute-start | bytes 393224 | tf_op jit(solution)/shard_map/ppermute | solution.py:310
  45.2 0.3 own_part.1.part
  45.5 0.7 %collective-permute-done.8.other = bf16[2,64,512]{2,1,0:T(8,128)(2,1)S(1)} collective-permute-done((bf16[2,64,512]{2,1,0:T(8,128)(2,1)S(1)}, bf16[2,64,512]{2,1,0:T(8,128)(2,1)S(1)}, u32[]{:S(2)}, u32[]{:S(2)}) %collective-permute-start.8) | collective-permute-done | bytes 131104 | tf_op jit(solution)/shard_map/ppermute | solution.py:310
  46.1 0.3 chip_wave.1
  46.5 1.3 %collective-permute-start.10 = (bf16[2,64,512]{2,1,0:T(8,128)(2,1)S(1)}, bf16[2,64,512]{2,1,0:T(8,128)(2,1)S(1)}, u32[]{:S(2)}, u32[]{:S(2)}) collective-permute-start(bf16[2,64,512]{2,1,0:T(8,128)(2,1)S(1)} %get-tuple-element.37), channel_id=1, source_target_pairs={{0,4},{1,5},{2,6},{3,7},{4,0},{5,1},{6,2},{7,3},{8,12},{9,13},{10,... | collective-permute-start | bytes 393224 | tf_op jit(solution)/shard_map/ppermute | solution.py:314
  47.8 1.0 %collective-permute-start.11 = (bf16[2,64,512]{2,1,0:T(8,128)(2,1)S(1)}, bf16[2,64,512]{2,1,0:T(8,128)(2,1)S(1)}, u32[]{:S(2)}, u32[]{:S(2)}) collective-permute-start(bf16[2,64,512]{2,1,0:T(8,128)(2,1)S(1)} %get-tuple-element.37), channel_id=1, source_target_pairs={{0,6},{1,7},{2,4},{3,5},{4,2},{5,3},{6,0},{7,1},{8,14},{9,15},{10,... | collective-permute-start | bytes 393224 | tf_op jit(solution)/shard_map/ppermute | solution.py:314
  48.8 0.4 collective-permute-start.9
  49.2 0.3 first.1
  49.5 2.9 %collective-permute-done.10.straight = bf16[2,64,512]{2,1,0:T(8,128)(2,1)S(1)} collective-permute-done((bf16[2,64,512]{2,1,0:T(8,128)(2,1)S(1)}, bf16[2,64,512]{2,1,0:T(8,128)(2,1)S(1)}, u32[]{:S(2)}, u32[]{:S(2)}) %collective-permute-start.10) | collective-permute-done | bytes 131104 | tf_op jit(solution)/shard_map/ppermute | solution.py:314
  52.4 0.8 %collective-permute-done.11.across_corner = bf16[2,64,512]{2,1,0:T(8,128)(2,1)S(1)} collective-permute-done((bf16[2,64,512]{2,1,0:T(8,128)(2,1)S(1)}, bf16[2,64,512]{2,1,0:T(8,128)(2,1)S(1)}, u32[]{:S(2)}, u32[]{:S(2)}) %collective-permute-start.11) | collective-permute-done | bytes 131104 | tf_op jit(solution)/shard_map/ppermute | solution.py:314
  53.2 0.0 collective-permute-done.12.near_map
  53.2 0.0 collective-permute-done.13.far_map
  53.2 1.8 %collective-permute-done.9.beside = bf16[2,64,512]{2,1,0:T(8,128)(2,1)S(1)} collective-permute-done((bf16[2,64,512]{2,1,0:T(8,128)(2,1)S(1)}, bf16[2,64,512]{2,1,0:T(8,128)(2,1)S(1)}, u32[]{:S(2)}, u32[]{:S(2)}) %collective-permute-start.9) | collective-permute-done | bytes 131104 | tf_op jit(solution)/shard_map/ppermute | solution.py:314
  55.1 0.5 chain.1
  55.6 1.5 %collective-permute-start.14 = (bf16[2,64,512]{2,1,0:T(8,128)(2,1)S(1)}, bf16[2,64,512]{2,1,0:T(8,128)(2,1)S(1)}, u32[]{:S(2)}, u32[]{:S(2)}) collective-permute-start(bf16[2,64,512]{2,1,0:T(8,128)(2,1)S(1)} %get-tuple-element.38), channel_id=1, source_target_pairs={{0,1},{1,0},{2,3},{3,2},{4,5},{5,4},{6,7},{7,6},{8,9},{9,8},{10,11... | collective-permute-start | bytes 393224 | tf_op jit(solution)/shard_map/ppermute | solution.py:310
  57.1 1.3 %green_blocks.2 = (bf16[2,2,64,512]{3,2,1,0:T(8,128)(2,1)}, bf16[2,2,512,512]{3,2,1,0:T(8,128)(2,1)}) custom-call(s32[1]{0:T(128)S(6)} %copy.18.counts, bf16[2,2,64,512]{3,2,1,0:T(8,128)(2,1)S(1)} %bitcast.17, bf16[2,64,512]{2,1,0:T(8,128)(2,1)S(1)} %get-tuple-element.39.chained), custom_call_target="tpu_custom_call" | custom-call | flops 2000000000 | bytes 1 | tf_op jit(solution)/shard_map/green_blocks/pallas_call | solution.py:269
  58.4 0.0 collective-permute-done.14.chained
  58.4 1.3 %green_blocks.3 = (bf16[2,2,64,512]{3,2,1,0:T(8,128)(2,1)}, bf16[2,2,512,512]{3,2,1,0:T(8,128)(2,1)}) custom-call(s32[1]{0:T(128)S(6)} %copy.18.counts, bf16[2,2,64,512]{3,2,1,0:T(8,128)(2,1)S(1)} %bitcast.18, bf16[2,64,512]{2,1,0:T(8,128)(2,1)S(1)} %collective-permute-done.14.chained, ...), custom_call_target="tpu_custom_call", output_to_operand_aliasing={{0}: (3, {}), {1}: (4, {})} | custom-call | flops 2000000000 | bytes 1 | tf_op jit(solution)/shard_map/green_blocks/pallas_call | solution.py:269
  (1 shorter events, 0.0 us)
Async XLA Ops:
  0.6 8.1 %collective-permute-start = (bf16[2,2,512,512]{3,2,1,0:T(8,128)(2,1)}, bf16[2,2,512,512]{3,2,1,0:T(8,128)(2,1)S(1)}, u32[]{:S(2)}, u32[]{:S(2)}) collective-permute-start(bf16[2,2,512,512]{3,2,1,0:T(8,128)(2,1)} %bitcast.19), channel_id=1, source_target_pairs={{0,1},{1,0},{2,3},{3,2},{4,5},{5,4},{6,7},{7,6},{8,9},{9,8},{10,11... | collective-permute-start | bytes 6291464 | tf_op jit(solution)/shard_map/ppermute | solution.py:310
  0.8 7.9 %collective-permute-start.1 = (bf16[2,2,512,512]{3,2,1,0:T(8,128)(2,1)}, bf16[2,2,512,512]{3,2,1,0:T(8,128)(2,1)S(1)}, u32[]{:S(2)}, u32[]{:S(2)}) collective-permute-start(bf16[2,2,512,512]{3,2,1,0:T(8,128)(2,1)} %bitcast.21), channel_id=1, source_target_pairs={{0,1},{1,0},{2,3},{3,2},{4,5},{5,4},{6,7},{7,6},{8,9},{9,8},{10,11... | collective-permute-start | bytes 6291464 | tf_op jit(solution)/shard_map/ppermute | solution.py:310
  1.2 14.4 %collective-permute-start.2 = (bf16[2,2,64,512]{3,2,1,0:T(8,128)(2,1)}, bf16[2,2,64,512]{3,2,1,0:T(8,128)(2,1)S(1)}, u32[]{:S(2)}, u32[]{:S(2)}) collective-permute-start(bf16[2,2,64,512]{3,2,1,0:T(8,128)(2,1)} %bitcast.14), channel_id=1, source_target_pairs={{0,8},{1,9},{2,10},{3,11},{4,12},{5,13},{6,14},{7,15},{8,0},{9,1},... | collective-permute-start | bytes 786440 | tf_op jit(solution)/shard_map/ppermute | solution.py:310
  3.6 12.0 %collective-permute-start.3 = (bf16[2,2,64,512]{3,2,1,0:T(8,128)(2,1)}, bf16[2,2,64,512]{3,2,1,0:T(8,128)(2,1)S(1)}, u32[]{:S(2)}, u32[]{:S(2)}) collective-permute-start(bf16[2,2,64,512]{3,2,1,0:T(8,128)(2,1)} %bitcast.15), channel_id=1, source_target_pairs={{0,16},{1,17},{2,18},{3,19},{4,20},{5,21},{6,22},{7,23},{8,24},{9,... | collective-permute-start | bytes 786440 | tf_op jit(solution)/shard_map/ppermute | solution.py:310
  8.7 9.2 %copy-start = (bf16[2,2,1,512,512]{4,3,2,1,0:T(8,128)(2,1)S(1)}, bf16[2,2,1,512,512]{4,3,2,1,0:T(8,128)(2,1)}, u32[]{:S(2)}) copy-start(bf16[2,2,1,512,512]{4,3,2,1,0:T(8,128)(2,1)} %param.10) | copy-start | bytes 6291460
  11.4 41.8 %collective-permute-start.12 = (bf16[2,512,512]{2,1,0:T(8,128)(2,1)S(1)}, bf16[2,512,512]{2,1,0:T(8,128)(2,1)S(1)}, u32[]{:S(2)}, u32[]{:S(2)}) collective-permute-start(bf16[2,512,512]{2,1,0:T(8,128)(2,1)S(1)} %get-tuple-element.24.chip_map), channel_id=1, source_target_pairs={{2,4},{3,5},{4,6},{5,7},{10,12},{11,13},{12,14},{13,15},{18,20},{1... | collective-permute-start | bytes 3145736 | tf_op jit(solution)/shard_map/ppermute | solution.py:320
  12.1 41.1 %collective-permute-start.13 = (bf16[2,512,512]{2,1,0:T(8,128)(2,1)S(1)}, bf16[2,512,512]{2,1,0:T(8,128)(2,1)S(1)}, u32[]{:S(2)}, u32[]{:S(2)}) collective-permute-start(bf16[2,512,512]{2,1,0:T(8,128)(2,1)S(1)} %get-tuple-element.24.chip_map), channel_id=1, source_target_pairs={{2,6},{3,7},{10,14},{11,15},{18,22},{19,23},{26,30},{27,31}} | collective-permute-start | bytes 3145736 | tf_op jit(solution)/shard_map/ppermute | solution.py:320
  15.6 6.6 %collective-permute-start.4 = (bf16[2,2,64,512]{3,2,1,0:T(8,128)(2,1)S(1)}, bf16[2,2,64,512]{3,2,1,0:T(8,128)(2,1)S(1)}, u32[]{:S(2)}, u32[]{:S(2)}) collective-permute-start(bf16[2,2,64,512]{3,2,1,0:T(8,128)(2,1)S(1)} %collective-permute-done.3.wave_ref), channel_id=1, source_target_pairs={{0,8},{1,9},{2,10},{3,11},{4,12},{5,13},{6,14},{7,15},{8,0},{9,1},... | collective-permute-start | bytes 786440 | tf_op jit(solution)/shard_map/ppermute | solution.py:310
  18.6 13.4 %collective-permute-start.6 = (bf16[2,2,64,512]{3,2,1,0:T(8,128)(2,1)S(1)}, bf16[2,2,64,512]{3,2,1,0:T(8,128)(2,1)S(1)}, u32[]{:S(2)}, u32[]{:S(2)}) collective-permute-start(bf16[2,2,64,512]{3,2,1,0:T(8,128)(2,1)S(1)} %product.5), channel_id=1, source_target_pairs={{0,16},{1,17},{2,18},{3,19},{4,20},{5,21},{6,22},{7,23},{8,24},{9,... | collective-permute-start | bytes 786440 | tf_op jit(solution)/shard_map/ppermute | solution.py:310
  22.0 8.1 %copy-start.1 = (bf16[2,2,1,64,512]{4,3,2,1,0:T(8,128)(2,1)S(1)}, bf16[2,2,1,64,512]{4,3,2,1,0:T(8,128)(2,1)}, u32[]{:S(2)}) copy-start(bf16[2,2,1,64,512]{4,3,2,1,0:T(8,128)(2,1)} %param.13) | copy-start | bytes 786436
  23.1 11.8 %collective-permute-start.7 = (bf16[2,2,64,512]{3,2,1,0:T(8,128)(2,1)S(1)}, bf16[2,2,64,512]{3,2,1,0:T(8,128)(2,1)S(1)}, u32[]{:S(2)}, u32[]{:S(2)}) collective-permute-start(bf16[2,2,64,512]{3,2,1,0:T(8,128)(2,1)S(1)} %product.4), channel_id=1, source_target_pairs={{0,24},{1,25},{2,26},{3,27},{4,28},{5,29},{6,30},{7,31},{8,16},{9,... | collective-permute-start | bytes 786440 | tf_op jit(solution)/shard_map/ppermute | solution.py:310
  30.1 13.8 %collective-permute-start.5 = (bf16[2,2,64,512]{3,2,1,0:T(8,128)(2,1)S(1)}, bf16[2,2,64,512]{3,2,1,0:T(8,128)(2,1)S(1)}, u32[]{:S(2)}, u32[]{:S(2)}) collective-permute-start(bf16[2,2,64,512]{3,2,1,0:T(8,128)(2,1)S(1)} %product.3), channel_id=1, source_target_pairs={{0,8},{1,9},{2,10},{3,11},{4,12},{5,13},{6,14},{7,15},{8,0},{9,1},... | collective-permute-start | bytes 786440 | tf_op jit(solution)/shard_map/ppermute | solution.py:310
  44.0 2.2 %collective-permute-start.8 = (bf16[2,64,512]{2,1,0:T(8,128)(2,1)S(1)}, bf16[2,64,512]{2,1,0:T(8,128)(2,1)S(1)}, u32[]{:S(2)}, u32[]{:S(2)}) collective-permute-start(bf16[2,64,512]{2,1,0:T(8,128)(2,1)S(1)} %get-tuple-element.33), channel_id=1, source_target_pairs={{0,1},{1,0},{2,3},{3,2},{4,5},{5,4},{6,7},{7,6},{8,9},{9,8},{10,11... | collective-permute-start | bytes 393224 | tf_op jit(solution)/shard_map/ppermute | solution.py:310
  46.5 5.9 %collective-permute-start.10 = (bf16[2,64,512]{2,1,0:T(8,128)(2,1)S(1)}, bf16[2,64,512]{2,1,0:T(8,128)(2,1)S(1)}, u32[]{:S(2)}, u32[]{:S(2)}) collective-permute-start(bf16[2,64,512]{2,1,0:T(8,128)(2,1)S(1)} %get-tuple-element.37), channel_id=1, source_target_pairs={{0,4},{1,5},{2,6},{3,7},{4,0},{5,1},{6,2},{7,3},{8,12},{9,13},{10,... | collective-permute-start | bytes 393224 | tf_op jit(solution)/shard_map/ppermute | solution.py:314
  47.8 5.4 %collective-permute-start.11 = (bf16[2,64,512]{2,1,0:T(8,128)(2,1)S(1)}, bf16[2,64,512]{2,1,0:T(8,128)(2,1)S(1)}, u32[]{:S(2)}, u32[]{:S(2)}) collective-permute-start(bf16[2,64,512]{2,1,0:T(8,128)(2,1)S(1)} %get-tuple-element.37), channel_id=1, source_target_pairs={{0,6},{1,7},{2,4},{3,5},{4,2},{5,3},{6,0},{7,1},{8,14},{9,15},{10,... | collective-permute-start | bytes 393224 | tf_op jit(solution)/shard_map/ppermute | solution.py:314
  48.8 6.2 %collective-permute-start.9 = (bf16[2,64,512]{2,1,0:T(8,128)(2,1)S(1)}, bf16[2,64,512]{2,1,0:T(8,128)(2,1)S(1)}, u32[]{:S(2)}, u32[]{:S(2)}) collective-permute-start(bf16[2,64,512]{2,1,0:T(8,128)(2,1)S(1)} %get-tuple-element.37), channel_id=1, source_target_pairs={{0,2},{1,3},{2,0},{3,1},{4,6},{5,7},{6,4},{7,5},{8,10},{9,11},{10,... | collective-permute-start | bytes 393224 | tf_op jit(solution)/shard_map/ppermute | solution.py:314
  55.6 2.8 %collective-permute-start.14 = (bf16[2,64,512]{2,1,0:T(8,128)(2,1)S(1)}, bf16[2,64,512]{2,1,0:T(8,128)(2,1)S(1)}, u32[]{:S(2)}, u32[]{:S(2)}) collective-permute-start(bf16[2,64,512]{2,1,0:T(8,128)(2,1)S(1)} %get-tuple-element.38), channel_id=1, source_target_pairs={{0,1},{1,0},{2,3},{3,2},{4,5},{5,4},{6,7},{7,6},{8,9},{9,8},{10,11... | collective-permute-start | bytes 393224 | tf_op jit(solution)/shard_map/ppermute | solution.py:310

commit v6 on v5

--- a/solution.py
+++ b/solution.py
@@ -356,7 +356,6 @@
         )[0]
         for offset in range(1, groups)
     ]
-    parts[0], parts[-1] = lax.optimization_barrier((parts[0], parts[-1]))
     back = [swap(part, offset + 1) for offset, part in enumerate(parts)]
     waves[0], parts[-1] = lax.optimization_barrier((incident, parts[-1]))
     base = call(own_kernel, "own", [(every, F32)], scalars, [waves[0], g_here], total)[0]

time: 60 us -> 58.9 us (0.982)
  waiting for transfers between devices: 21 us -> 18.5 us
  starting transfers between devices: 23.9 us -> 25.4 us
    ppermute x10, waiting for transfers between devices: 15.5 us -> 13 us  [swap(): return lax.ppermute(value, ('energy', 'wire'), pairs)]
    ppermute x10, starting transfers between devices: 19.7 us -> 21.2 us  [swap(): return lax.ppermute(value, ('energy', 'wire'), pairs)]
where the time goes in v6:
time: 58.9 us; the launch traced here: 58.7 us
  starting transfers between devices  25.4 us (43%)
  waiting for transfers between devices  18.5 us (31%)
  Pallas kernels  11.2 us (19%)
  between operations  2.08 us (4%)
  other arithmetic  1.49 us (3%)
    ppermute x10, starting transfers between devices, swap(): return lax.ppermute(value, ('energy', 'wire'), pairs)  21.2 us
    ppermute x10, waiting for transfers between devices, swap(): return lax.ppermute(value, ('energy', 'wire'), pairs)  13 us
    pallas_call x11, Pallas kernels, call(): pl.pallas_call(kernel, out_shape=shapes, in_specs=[SMEM] * len(scalars) +...  5.96 us
    ppermute x3, waiting for transfers between devices, exchange(): return lax.ppermute(value, 'wire', pairs)  5.5 us
    ppermute x3, starting transfers between devices, exchange(): return lax.ppermute(value, 'wire', pairs)  2.71 us
    pallas_call x1, Pallas kernels, shards(): pl.pallas_call(prepare_kernel, out_shape=[jax.ShapeDtypeStruct((2,) + blo...  2.69 us
    pallas_call x2, Pallas kernels, green_blocks(): pl.pallas_call(functools.partial(block_kernel, turn), out_shape=[jax.Shap...  2.58 us
    ppermute x2, starting transfers between devices, later(): return lax.ppermute(value, 'wire', pairs)  1.46 us
  transfers between devices with their start and end apart: 15, of which 8 were waited for; matrix products, arithmetic and copies ran while one was open for 3% of the time, Pallas kernels for 16%

profile of v6, /device:TPU:1, one launch (start us, length us, event | category | flops | bytes accessed | tf_op | source)
XLA Modules:
  0.0 58.7 jit_solution(6007627615152989796)
XLA Ops:
  0.6 0.1 collective-permute-start
  0.8 0.5 collective-permute-start.1
  1.2 2.4 %collective-permute-start.2 = (bf16[2,2,64,512]{3,2,1,0:T(8,128)(2,1)}, bf16[2,2,64,512]{3,2,1,0:T(8,128)(2,1)S(1)}, u32[]{:S(2)}, u32[]{:S(2)}) collective-permute-start(bf16[2,2,64,512]{3,2,1,0:T(8,128)(2,1)} %bitcast.14), channel_id=1, source_target_pairs={{0,8},{1,9},{2,10},{3,11},{4,12},{5,13},{6,14},{7,15},{8,0},{9,1},... | collective-permute-start | bytes 786440 | tf_op jit(solution)/shard_map/ppermute | solution.py:310
  3.6 2.3 %collective-permute-start.3 = (bf16[2,2,64,512]{3,2,1,0:T(8,128)(2,1)}, bf16[2,2,64,512]{3,2,1,0:T(8,128)(2,1)S(1)}, u32[]{:S(2)}, u32[]{:S(2)}) collective-permute-start(bf16[2,2,64,512]{3,2,1,0:T(8,128)(2,1)} %bitcast.15), channel_id=1, source_target_pairs={{0,16},{1,17},{2,18},{3,19},{4,20},{5,21},{6,22},{7,23},{8,24},{9,... | collective-permute-start | bytes 786440 | tf_op jit(solution)/shard_map/ppermute | solution.py:310
  7.2 0.7 %pad_maximum_fusion.real_valued = f32[18]{0:T(128)S(1)} fusion(f32[16]{0:T(128)} %param.18, f32[2]{0:T(128)} %param.19), kind=kLoop, calls=%fused_computation.1 | loop fusion | flops 18 | bytes 144 | tf_op jit(solution)/shard_map/concatenate | solution.py:324
  7.9 0.7 %pad_add_fusion.whole = s32[17]{0:T(128)S(1)} fusion(s32[1]{0:T(128)S(6)} %copy.19, s32[8]{0:T(128)} %param.15, s32[8]{0:T(128)} %param.14), kind=kLoop, calls=%fused_computation | loop fusion | flops 34 | bytes 136 | tf_op jit(solution)/shard_map/concatenate | solution.py:323
  8.7 0.0 copy-start
  8.7 0.0 collective-permute-done.prop_other
  8.7 0.0 collective-permute-done.1.green_other
  8.7 2.7 %prepare.1 = (bf16[2,2,512,512]{3,2,1,0:T(8,128)(2,1)S(1)}, bf16[2,2,512,512]{3,2,1,0:T(8,128)(2,1)S(1)}, bf16[2,512,512]{2,1,0:T(8,128)(2,1)S(1)}) custom-call(bf16[2,2,512,512]{3,2,1,0:T(8,128)(2,1)} %bitcast.20, bf16[2,2,512,512]{3,2,1,0:T(8,128)(2,1)S(1)} %collective-permute-done.prop_other, bf16[2,2,512,512]{3,2,1,0:T(8,128)(2,1)} %bitcast.22, ...), custom_call_target="tpu_custom_call" | custom-call | flops 2000000000 | bytes 1 | tf_op jit(solution)/shard_map/prepare/pallas_call | solution.py:335
  11.4 0.7 %collective-permute-start.12 = (bf16[2,512,512]{2,1,0:T(8,128)(2,1)S(1)}, bf16[2,512,512]{2,1,0:T(8,128)(2,1)S(1)}, u32[]{:S(2)}, u32[]{:S(2)}) collective-permute-start(bf16[2,512,512]{2,1,0:T(8,128)(2,1)S(1)} %get-tuple-element.22.chip_map), channel_id=1, source_target_pairs={{2,4},{3,5},{4,6},{5,7},{10,12},{11,13},{12,14},{13,15},{18,20},{1... | collective-permute-start | bytes 3145736 | tf_op jit(solution)/shard_map/ppermute | solution.py:320
  12.1 0.7 %collective-permute-start.13 = (bf16[2,512,512]{2,1,0:T(8,128)(2,1)S(1)}, bf16[2,512,512]{2,1,0:T(8,128)(2,1)S(1)}, u32[]{:S(2)}, u32[]{:S(2)}) collective-permute-start(bf16[2,512,512]{2,1,0:T(8,128)(2,1)S(1)} %get-tuple-element.22.chip_map), channel_id=1, source_target_pairs={{2,6},{3,7},{10,14},{11,15},{18,22},{19,23},{26,30},{27,31}} | collective-permute-start | bytes 3145736 | tf_op jit(solution)/shard_map/ppermute | solution.py:320
  12.9 2.7 %collective-permute-done.2.wave_ref = bf16[2,2,64,512]{3,2,1,0:T(8,128)(2,1)S(1)} collective-permute-done((bf16[2,2,64,512]{3,2,1,0:T(8,128)(2,1)}, bf16[2,2,64,512]{3,2,1,0:T(8,128)(2,1)S(1)}, u32[]{:S(2)}, u32[]{:S(2)}) %collective-permute-start.2) | collective-permute-done | bytes 262176 | tf_op jit(solution)/shard_map/ppermute | solution.py:310
  15.6 0.0 collective-permute-done.3.wave_ref
  15.6 2.3 %collective-permute-start.4 = (bf16[2,2,64,512]{3,2,1,0:T(8,128)(2,1)S(1)}, bf16[2,2,64,512]{3,2,1,0:T(8,128)(2,1)S(1)}, u32[]{:S(2)}, u32[]{:S(2)}) collective-permute-start(bf16[2,2,64,512]{3,2,1,0:T(8,128)(2,1)S(1)} %collective-permute-done.3.wave_ref), channel_id=1, source_target_pairs={{0,8},{1,9},{2,10},{3,11},{4,12},{5,13},{6,14},{7,15},{8,0},{9,1},... | collective-permute-start | bytes 786440 | tf_op jit(solution)/shard_map/ppermute | solution.py:310
  17.9 0.0 copy-done
  17.9 0.6 %product.5 = bf16[2,2,64,512]{3,2,1,0:T(8,128)(2,1)S(1)} custom-call(s32[17]{0:T(128)S(1)} %pad_add_fusion.whole, f32[18]{0:T(128)S(1)} %pad_maximum_fusion.real_valued, bf16[2,2,64,512]{3,2,1,0:T(8,128)(2,1)S(1)} %collective-permute-done.3.wave_ref, bf16[2,2,512,512]{3,2,1,0:T(8,128)(2,1)S(1)} %bitcast.10), custom_call_target="tpu_custom_call" | custom-call | flops 2000000000 | bytes 1 | tf_op jit(solution)/shard_map/product/pallas_call | solution.py:19
  18.6 2.5 %collective-permute-start.6 = (bf16[2,2,64,512]{3,2,1,0:T(8,128)(2,1)S(1)}, bf16[2,2,64,512]{3,2,1,0:T(8,128)(2,1)S(1)}, u32[]{:S(2)}, u32[]{:S(2)}) collective-permute-start(bf16[2,2,64,512]{3,2,1,0:T(8,128)(2,1)S(1)} %product.5), channel_id=1, source_target_pairs={{0,16},{1,17},{2,18},{3,19},{4,20},{5,21},{6,22},{7,23},{8,24},{9,... | collective-permute-start | bytes 786440 | tf_op jit(solution)/shard_map/ppermute | solution.py:310
  21.0 0.9 %product.4 = bf16[2,2,64,512]{3,2,1,0:T(8,128)(2,1)S(1)} custom-call(s32[17]{0:T(128)S(1)} %pad_add_fusion.whole, f32[18]{0:T(128)S(1)} %pad_maximum_fusion.real_valued, bf16[2,2,64,512]{3,2,1,0:T(8,128)(2,1)S(1)} %collective-permute-done.2.wave_ref, bf16[2,2,512,512]{3,2,1,0:T(8,128)(2,1)S(1)} %bitcast.11), custom_call_target="tpu_custom_call" | custom-call | flops 2000000000 | bytes 1 | tf_op jit(solution)/shard_map/product/pallas_call | solution.py:19
  22.0 0.0 copy-start.1
  22.0 0.1 collective-permute-start.5
  22.0 0.1 collective-permute-done.4.wave_ref
  22.2 0.9 %product.3 = bf16[2,2,64,512]{3,2,1,0:T(8,128)(2,1)S(1)} custom-call(s32[17]{0:T(128)S(1)} %pad_add_fusion.whole, f32[18]{0:T(128)S(1)} %pad_maximum_fusion.real_valued, bf16[2,2,64,512]{3,2,1,0:T(8,128)(2,1)S(1)} %collective-permute-done.4.wave_ref, bf16[2,2,512,512]{3,2,1,0:T(8,128)(2,1)S(1)} %bitcast.12), custom_call_target="tpu_custom_call" | custom-call | flops 2000000000 | bytes 1 | tf_op jit(solution)/shard_map/product/pallas_call | solution.py:19
  23.1 7.3 %collective-permute-start.7 = (bf16[2,2,64,512]{3,2,1,0:T(8,128)(2,1)S(1)}, bf16[2,2,64,512]{3,2,1,0:T(8,128)(2,1)S(1)}, u32[]{:S(2)}, u32[]{:S(2)}) collective-permute-start(bf16[2,2,64,512]{3,2,1,0:T(8,128)(2,1)S(1)} %product.3), channel_id=1, source_target_pairs={{0,24},{1,25},{2,26},{3,27},{4,28},{5,29},{6,30},{7,31},{8,16},{9,... | collective-permute-start | bytes 786440 | tf_op jit(solution)/shard_map/ppermute | solution.py:310
  30.4 0.0 copy-done.1
  30.4 0.7 %own.1.base = f32[2,2,64,512]{3,2,1,0:T(8,128)S(1)} custom-call(s32[17]{0:T(128)S(1)} %pad_add_fusion.whole, f32[18]{0:T(128)S(1)} %pad_maximum_fusion.real_valued, bf16[2,2,64,512]{3,2,1,0:T(8,128)(2,1)S(1)} %bitcast.16, bf16[2,2,512,512]{3,2,1,0:T(8,128)(2,1)S(1)} %bitcast.13), custom_call_target="tpu_custom_call" | custom-call | flops 2000000000 | bytes 1 | tf_op jit(solution)/shard_map/own/pallas_call | solution.py:19
  31.1 1.3 %fold.1.folded = bf16[2,512,512]{2,1,0:T(8,128)(2,1)S(1)} custom-call(bf16[2,2,512,512]{3,2,1,0:T(8,128)(2,1)S(1)} %get-tuple-element.30.steps, bf16[2,2,512,512]{3,2,1,0:T(8,128)(2,1)S(1)} %get-tuple-element.31.greens), custom_call_target="tpu_custom_call" | custom-call | flops 2000000000 | bytes 1 | tf_op jit(solution)/shard_map/fold/pallas_call | solution.py:19
  32.3 0.0 collective-permute-done.6.refs_1_
  32.3 1.1 %collective-permute-done.5.refs_0_ = bf16[2,2,64,512]{3,2,1,0:T(8,128)(2,1)S(1)} collective-permute-done((bf16[2,2,64,512]{3,2,1,0:T(8,128)(2,1)S(1)}, bf16[2,2,64,512]{3,2,1,0:T(8,128)(2,1)S(1)}, u32[]{:S(2)}, u32[]{:S(2)}) %collective-permute-start.5) | collective-permute-done | bytes 262176 | tf_op jit(solution)/shard_map/ppermute | solution.py:310
  33.5 8.3 %collective-permute-done.7.refs_2_ = bf16[2,2,64,512]{3,2,1,0:T(8,128)(2,1)S(1)} collective-permute-done((bf16[2,2,64,512]{3,2,1,0:T(8,128)(2,1)S(1)}, bf16[2,2,64,512]{3,2,1,0:T(8,128)(2,1)S(1)}, u32[]{:S(2)}, u32[]{:S(2)}) %collective-permute-start.7) | collective-permute-done | bytes 262176 | tf_op jit(solution)/shard_map/ppermute | solution.py:310
  41.7 0.1 term.1
  41.8 2.3 %collective-permute-start.8 = (bf16[2,64,512]{2,1,0:T(8,128)(2,1)S(1)}, bf16[2,64,512]{2,1,0:T(8,128)(2,1)S(1)}, u32[]{:S(2)}, u32[]{:S(2)}) collective-permute-start(bf16[2,64,512]{2,1,0:T(8,128)(2,1)S(1)} %get-tuple-element.29), channel_id=1, source_target_pairs={{0,1},{1,0},{2,3},{3,2},{4,5},{5,4},{6,7},{7,6},{8,9},{9,8},{10,11... | collective-permute-start | bytes 393224 | tf_op jit(solution)/shard_map/ppermute | solution.py:310
  44.2 0.3 own_part.1.part
  44.5 0.7 %collective-permute-done.8.other = bf16[2,64,512]{2,1,0:T(8,128)(2,1)S(1)} collective-permute-done((bf16[2,64,512]{2,1,0:T(8,128)(2,1)S(1)}, bf16[2,64,512]{2,1,0:T(8,128)(2,1)S(1)}, u32[]{:S(2)}, u32[]{:S(2)}) %collective-permute-start.8) | collective-permute-done | bytes 131104 | tf_op jit(solution)/shard_map/ppermute | solution.py:310
  45.2 0.3 chip_wave.1
  45.5 1.3 %collective-permute-start.10 = (bf16[2,64,512]{2,1,0:T(8,128)(2,1)S(1)}, bf16[2,64,512]{2,1,0:T(8,128)(2,1)S(1)}, u32[]{:S(2)}, u32[]{:S(2)}) collective-permute-start(bf16[2,64,512]{2,1,0:T(8,128)(2,1)S(1)} %get-tuple-element.33), channel_id=1, source_target_pairs={{0,4},{1,5},{2,6},{3,7},{4,0},{5,1},{6,2},{7,3},{8,12},{9,13},{10,... | collective-permute-start | bytes 393224 | tf_op jit(solution)/shard_map/ppermute | solution.py:314
  46.8 1.3 %collective-permute-start.11 = (bf16[2,64,512]{2,1,0:T(8,128)(2,1)S(1)}, bf16[2,64,512]{2,1,0:T(8,128)(2,1)S(1)}, u32[]{:S(2)}, u32[]{:S(2)}) collective-permute-start(bf16[2,64,512]{2,1,0:T(8,128)(2,1)S(1)} %get-tuple-element.33), channel_id=1, source_target_pairs={{0,6},{1,7},{2,4},{3,5},{4,2},{5,3},{6,0},{7,1},{8,14},{9,15},{10,... | collective-permute-start | bytes 393224 | tf_op jit(solution)/shard_map/ppermute | solution.py:314
  48.1 0.1 collective-permute-start.9
  48.2 0.3 first.1
  48.5 2.9 %collective-permute-done.10.straight = bf16[2,64,512]{2,1,0:T(8,128)(2,1)S(1)} collective-permute-done((bf16[2,64,512]{2,1,0:T(8,128)(2,1)S(1)}, bf16[2,64,512]{2,1,0:T(8,128)(2,1)S(1)}, u32[]{:S(2)}, u32[]{:S(2)}) %collective-permute-start.10) | collective-permute-done | bytes 131104 | tf_op jit(solution)/shard_map/ppermute | solution.py:314
  51.4 0.8 %collective-permute-done.11.across_corner = bf16[2,64,512]{2,1,0:T(8,128)(2,1)S(1)} collective-permute-done((bf16[2,64,512]{2,1,0:T(8,128)(2,1)S(1)}, bf16[2,64,512]{2,1,0:T(8,128)(2,1)S(1)}, u32[]{:S(2)}, u32[]{:S(2)}) %collective-permute-start.11) | collective-permute-done | bytes 131104 | tf_op jit(solution)/shard_map/ppermute | solution.py:314
  52.2 0.0 collective-permute-done.12.near_map
  52.2 0.0 collective-permute-done.13.far_map
  52.2 1.8 %collective-permute-done.9.beside = bf16[2,64,512]{2,1,0:T(8,128)(2,1)S(1)} collective-permute-done((bf16[2,64,512]{2,1,0:T(8,128)(2,1)S(1)}, bf16[2,64,512]{2,1,0:T(8,128)(2,1)S(1)}, u32[]{:S(2)}, u32[]{:S(2)}) %collective-permute-start.9) | collective-permute-done | bytes 131104 | tf_op jit(solution)/shard_map/ppermute | solution.py:314
  54.0 0.5 chain.1
  54.6 1.5 %collective-permute-start.14 = (bf16[2,64,512]{2,1,0:T(8,128)(2,1)S(1)}, bf16[2,64,512]{2,1,0:T(8,128)(2,1)S(1)}, u32[]{:S(2)}, u32[]{:S(2)}) collective-permute-start(bf16[2,64,512]{2,1,0:T(8,128)(2,1)S(1)} %get-tuple-element.34), channel_id=1, source_target_pairs={{0,1},{1,0},{2,3},{3,2},{4,5},{5,4},{6,7},{7,6},{8,9},{9,8},{10,11... | collective-permute-start | bytes 393224 | tf_op jit(solution)/shard_map/ppermute | solution.py:310
  56.1 1.3 %green_blocks.2 = (bf16[2,2,64,512]{3,2,1,0:T(8,128)(2,1)}, bf16[2,2,512,512]{3,2,1,0:T(8,128)(2,1)}) custom-call(s32[1]{0:T(128)S(6)} %copy.18.counts, bf16[2,2,64,512]{3,2,1,0:T(8,128)(2,1)S(1)} %bitcast.17, bf16[2,64,512]{2,1,0:T(8,128)(2,1)S(1)} %get-tuple-element.35.chained), custom_call_target="tpu_custom_call" | custom-call | flops 2000000000 | bytes 1 | tf_op jit(solution)/shard_map/green_blocks/pallas_call | solution.py:269
  57.4 0.0 collective-permute-done.14.chained
  57.4 1.3 %green_blocks.3 = (bf16[2,2,64,512]{3,2,1,0:T(8,128)(2,1)}, bf16[2,2,512,512]{3,2,1,0:T(8,128)(2,1)}) custom-call(s32[1]{0:T(128)S(6)} %copy.18.counts, bf16[2,2,64,512]{3,2,1,0:T(8,128)(2,1)S(1)} %bitcast.18, bf16[2,64,512]{2,1,0:T(8,128)(2,1)S(1)} %collective-permute-done.14.chained, ...), custom_call_target="tpu_custom_call", output_to_operand_aliasing={{0}: (3, {}), {1}: (4, {})} | custom-call | flops 2000000000 | bytes 1 | tf_op jit(solution)/shard_map/green_blocks/pallas_call | solution.py:269
  (1 shorter events, 0.0 us)
Async XLA Ops:
  0.6 8.1 %collective-permute-start = (bf16[2,2,512,512]{3,2,1,0:T(8,128)(2,1)}, bf16[2,2,512,512]{3,2,1,0:T(8,128)(2,1)S(1)}, u32[]{:S(2)}, u32[]{:S(2)}) collective-permute-start(bf16[2,2,512,512]{3,2,1,0:T(8,128)(2,1)} %bitcast.19), channel_id=1, source_target_pairs={{0,1},{1,0},{2,3},{3,2},{4,5},{5,4},{6,7},{7,6},{8,9},{9,8},{10,11... | collective-permute-start | bytes 6291464 | tf_op jit(solution)/shard_map/ppermute | solution.py:310
  0.8 7.9 %collective-permute-start.1 = (bf16[2,2,512,512]{3,2,1,0:T(8,128)(2,1)}, bf16[2,2,512,512]{3,2,1,0:T(8,128)(2,1)S(1)}, u32[]{:S(2)}, u32[]{:S(2)}) collective-permute-start(bf16[2,2,512,512]{3,2,1,0:T(8,128)(2,1)} %bitcast.21), channel_id=1, source_target_pairs={{0,1},{1,0},{2,3},{3,2},{4,5},{5,4},{6,7},{7,6},{8,9},{9,8},{10,11... | collective-permute-start | bytes 6291464 | tf_op jit(solution)/shard_map/ppermute | solution.py:310
  1.2 14.4 %collective-permute-start.2 = (bf16[2,2,64,512]{3,2,1,0:T(8,128)(2,1)}, bf16[2,2,64,512]{3,2,1,0:T(8,128)(2,1)S(1)}, u32[]{:S(2)}, u32[]{:S(2)}) collective-permute-start(bf16[2,2,64,512]{3,2,1,0:T(8,128)(2,1)} %bitcast.14), channel_id=1, source_target_pairs={{0,8},{1,9},{2,10},{3,11},{4,12},{5,13},{6,14},{7,15},{8,0},{9,1},... | collective-permute-start | bytes 786440 | tf_op jit(solution)/shard_map/ppermute | solution.py:310
  3.6 12.0 %collective-permute-start.3 = (bf16[2,2,64,512]{3,2,1,0:T(8,128)(2,1)}, bf16[2,2,64,512]{3,2,1,0:T(8,128)(2,1)S(1)}, u32[]{:S(2)}, u32[]{:S(2)}) collective-permute-start(bf16[2,2,64,512]{3,2,1,0:T(8,128)(2,1)} %bitcast.15), channel_id=1, source_target_pairs={{0,16},{1,17},{2,18},{3,19},{4,20},{5,21},{6,22},{7,23},{8,24},{9,... | collective-permute-start | bytes 786440 | tf_op jit(solution)/shard_map/ppermute | solution.py:310
  8.7 9.2 %copy-start = (bf16[2,2,1,512,512]{4,3,2,1,0:T(8,128)(2,1)S(1)}, bf16[2,2,1,512,512]{4,3,2,1,0:T(8,128)(2,1)}, u32[]{:S(2)}) copy-start(bf16[2,2,1,512,512]{4,3,2,1,0:T(8,128)(2,1)} %param.10) | copy-start | bytes 6291460
  11.4 40.8 %collective-permute-start.12 = (bf16[2,512,512]{2,1,0:T(8,128)(2,1)S(1)}, bf16[2,512,512]{2,1,0:T(8,128)(2,1)S(1)}, u32[]{:S(2)}, u32[]{:S(2)}) collective-permute-start(bf16[2,512,512]{2,1,0:T(8,128)(2,1)S(1)} %get-tuple-element.22.chip_map), channel_id=1, source_target_pairs={{2,4},{3,5},{4,6},{5,7},{10,12},{11,13},{12,14},{13,15},{18,20},{1... | collective-permute-start | bytes 3145736 | tf_op jit(solution)/shard_map/ppermute | solution.py:320
  12.1 40.1 %collective-permute-start.13 = (bf16[2,512,512]{2,1,0:T(8,128)(2,1)S(1)}, bf16[2,512,512]{2,1,0:T(8,128)(2,1)S(1)}, u32[]{:S(2)}, u32[]{:S(2)}) collective-permute-start(bf16[2,512,512]{2,1,0:T(8,128)(2,1)S(1)} %get-tuple-element.22.chip_map), channel_id=1, source_target_pairs={{2,6},{3,7},{10,14},{11,15},{18,22},{19,23},{26,30},{27,31}} | collective-permute-start | bytes 3145736 | tf_op jit(solution)/shard_map/ppermute | solution.py:320
  15.6 6.6 %collective-permute-start.4 = (bf16[2,2,64,512]{3,2,1,0:T(8,128)(2,1)S(1)}, bf16[2,2,64,512]{3,2,1,0:T(8,128)(2,1)S(1)}, u32[]{:S(2)}, u32[]{:S(2)}) collective-permute-start(bf16[2,2,64,512]{3,2,1,0:T(8,128)(2,1)S(1)} %collective-permute-done.3.wave_ref), channel_id=1, source_target_pairs={{0,8},{1,9},{2,10},{3,11},{4,12},{5,13},{6,14},{7,15},{8,0},{9,1},... | collective-permute-start | bytes 786440 | tf_op jit(solution)/shard_map/ppermute | solution.py:310
  18.6 13.8 %collective-permute-start.6 = (bf16[2,2,64,512]{3,2,1,0:T(8,128)(2,1)S(1)}, bf16[2,2,64,512]{3,2,1,0:T(8,128)(2,1)S(1)}, u32[]{:S(2)}, u32[]{:S(2)}) collective-permute-start(bf16[2,2,64,512]{3,2,1,0:T(8,128)(2,1)S(1)} %product.5), channel_id=1, source_target_pairs={{0,16},{1,17},{2,18},{3,19},{4,20},{5,21},{6,22},{7,23},{8,24},{9,... | collective-permute-start | bytes 786440 | tf_op jit(solution)/shard_map/ppermute | solution.py:310
  22.0 8.4 %copy-start.1 = (bf16[2,2,1,64,512]{4,3,2,1,0:T(8,128)(2,1)S(1)}, bf16[2,2,1,64,512]{4,3,2,1,0:T(8,128)(2,1)}, u32[]{:S(2)}) copy-start(bf16[2,2,1,64,512]{4,3,2,1,0:T(8,128)(2,1)} %param.13) | copy-start | bytes 786436
  22.0 11.5 %collective-permute-start.5 = (bf16[2,2,64,512]{3,2,1,0:T(8,128)(2,1)S(1)}, bf16[2,2,64,512]{3,2,1,0:T(8,128)(2,1)S(1)}, u32[]{:S(2)}, u32[]{:S(2)}) collective-permute-start(bf16[2,2,64,512]{3,2,1,0:T(8,128)(2,1)S(1)} %product.4), channel_id=1, source_target_pairs={{0,8},{1,9},{2,10},{3,11},{4,12},{5,13},{6,14},{7,15},{8,0},{9,1},... | collective-permute-start | bytes 786440 | tf_op jit(solution)/shard_map/ppermute | solution.py:310
  23.1 18.6 %collective-permute-start.7 = (bf16[2,2,64,512]{3,2,1,0:T(8,128)(2,1)S(1)}, bf16[2,2,64,512]{3,2,1,0:T(8,128)(2,1)S(1)}, u32[]{:S(2)}, u32[]{:S(2)}) collective-permute-start(bf16[2,2,64,512]{3,2,1,0:T(8,128)(2,1)S(1)} %product.3), channel_id=1, source_target_pairs={{0,24},{1,25},{2,26},{3,27},{4,28},{5,29},{6,30},{7,31},{8,16},{9,... | collective-permute-start | bytes 786440 | tf_op jit(solution)/shard_map/ppermute | solution.py:310
  41.8 3.3 %collective-permute-start.8 = (bf16[2,64,512]{2,1,0:T(8,128)(2,1)S(1)}, bf16[2,64,512]{2,1,0:T(8,128)(2,1)S(1)}, u32[]{:S(2)}, u32[]{:S(2)}) collective-permute-start(bf16[2,64,512]{2,1,0:T(8,128)(2,1)S(1)} %get-tuple-element.29), channel_id=1, source_target_pairs={{0,1},{1,0},{2,3},{3,2},{4,5},{5,4},{6,7},{7,6},{8,9},{9,8},{10,11... | collective-permute-start | bytes 393224 | tf_op jit(solution)/shard_map/ppermute | solution.py:310
  45.5 5.9 %collective-permute-start.10 = (bf16[2,64,512]{2,1,0:T(8,128)(2,1)S(1)}, bf16[2,64,512]{2,1,0:T(8,128)(2,1)S(1)}, u32[]{:S(2)}, u32[]{:S(2)}) collective-permute-start(bf16[2,64,512]{2,1,0:T(8,128)(2,1)S(1)} %get-tuple-element.33), channel_id=1, source_target_pairs={{0,4},{1,5},{2,6},{3,7},{4,0},{5,1},{6,2},{7,3},{8,12},{9,13},{10,... | collective-permute-start | bytes 393224 | tf_op jit(solution)/shard_map/ppermute | solution.py:314
  46.8 5.4 %collective-permute-start.11 = (bf16[2,64,512]{2,1,0:T(8,128)(2,1)S(1)}, bf16[2,64,512]{2,1,0:T(8,128)(2,1)S(1)}, u32[]{:S(2)}, u32[]{:S(2)}) collective-permute-start(bf16[2,64,512]{2,1,0:T(8,128)(2,1)S(1)} %get-tuple-element.33), channel_id=1, source_target_pairs={{0,6},{1,7},{2,4},{3,5},{4,2},{5,3},{6,0},{7,1},{8,14},{9,15},{10,... | collective-permute-start | bytes 393224 | tf_op jit(solution)/shard_map/ppermute | solution.py:314
  48.1 5.9 %collective-permute-start.9 = (bf16[2,64,512]{2,1,0:T(8,128)(2,1)S(1)}, bf16[2,64,512]{2,1,0:T(8,128)(2,1)S(1)}, u32[]{:S(2)}, u32[]{:S(2)}) collective-permute-start(bf16[2,64,512]{2,1,0:T(8,128)(2,1)S(1)} %get-tuple-element.33), channel_id=1, source_target_pairs={{0,2},{1,3},{2,0},{3,1},{4,6},{5,7},{6,4},{7,5},{8,10},{9,11},{10,... | collective-permute-start | bytes 393224 | tf_op jit(solution)/shard_map/ppermute | solution.py:314
  54.6 2.8 %collective-permute-start.14 = (bf16[2,64,512]{2,1,0:T(8,128)(2,1)S(1)}, bf16[2,64,512]{2,1,0:T(8,128)(2,1)S(1)}, u32[]{:S(2)}, u32[]{:S(2)}) collective-permute-start(bf16[2,64,512]{2,1,0:T(8,128)(2,1)S(1)} %get-tuple-element.34), channel_id=1, source_target_pairs={{0,1},{1,0},{2,3},{3,2},{4,5},{5,4},{6,7},{7,6},{8,9},{9,8},{10,11... | collective-permute-start | bytes 393224 | tf_op jit(solution)/shard_map/ppermute | solution.py:310

commit v7 on v6

--- a/solution.py
+++ b/solution.py
@@ -153,7 +153,7 @@
             first_ref[0], first_ref[1] = times(pair(term), (greens[0, 0], greens[0, 1]))
 
 
-def far_kernel(straight, across_corner, near_map, far_map, out_ref):
+def far_kernel(across_corner, straight, near_map, far_map, out_ref):
     chip = lax.div(lax.axis_index("wire"), 2)
     for here, (begin, added, step) in {
         2: (straight, across_corner, near_map),
@@ -373,7 +373,7 @@
     if chips == 4:
         beside, straight, corner = [exchange(chip_send, offset) for offset in range(1, chips)]
         near_map, far_map = [later(chip_map, hops, 1) for hops in range(1, chips - 1)]
-        far = call(far_kernel, "far", [(wave, BF16)], [], [straight, corner, near_map, far_map])[0]
+        far = call(far_kernel, "far", [(wave, BF16)], [], [corner, straight, near_map, far_map])[0]
         kernel, kept = near_kernel, [(wave, BF16)] + kept
         arrived = [beside, far, near_map]
     elif chips < 3:

time: 58.9 us -> 58.6 us (level)
  starting transfers between devices: 25.4 us -> 24.6 us
    ppermute x10, starting transfers between devices: 21.2 us -> 20.4 us  [swap(): return lax.ppermute(value, ('energy', 'wire'), pairs)]
    ppermute x3, waiting for transfers between devices: 5.5 us -> 6.17 us  [exchange(): return lax.ppermute(value, 'wire', pairs)]
  transfers between devices with their start and end apart: 15 -> 15, of which waited for: 8 -> 6; matrix products, arithmetic and copies ran while one was open for 3% -> 3% of each run, Pallas kernels for 16% -> 17%
where the time goes in v7:
time: 58.6 us; the launch traced here: 58.4 us
  starting transfers between devices  24.6 us (42%)
  waiting for transfers between devices  18.7 us (32%)
  Pallas kernels  11.6 us (20%)
  between operations  2.1 us (4%)
  other arithmetic  1.49 us (3%)
    ppermute x10, starting transfers between devices, swap(): return lax.ppermute(value, ('energy', 'wire'), pairs)  20.4 us
    ppermute x10, waiting for transfers between devices, swap(): return lax.ppermute(value, ('energy', 'wire'), pairs)  12.5 us
    pallas_call x11, Pallas kernels, call(): pl.pallas_call(kernel, out_shape=shapes, in_specs=[SMEM] * len(scalars) +...  6.28 us
    ppermute x3, waiting for transfers between devices, exchange(): return lax.ppermute(value, 'wire', pairs)  6.17 us
    ppermute x3, starting transfers between devices, exchange(): return lax.ppermute(value, 'wire', pairs)  2.71 us
    pallas_call x1, Pallas kernels, shards(): pl.pallas_call(prepare_kernel, out_shape=[jax.ShapeDtypeStruct((2,) + blo...  2.69 us
    pallas_call x2, Pallas kernels, green_blocks(): pl.pallas_call(functools.partial(block_kernel, turn), out_shape=[jax.Shap...  2.58 us
    ppermute x2, starting transfers between devices, later(): return lax.ppermute(value, 'wire', pairs)  1.46 us
  transfers between devices with their start and end apart: 15, of which 6 were waited for; matrix products, arithmetic and copies ran while one was open for 3% of the time, Pallas kernels for 17%

profile of v7, /device:TPU:1, one launch (start us, length us, event | category | flops | bytes accessed | tf_op | source)
XLA Modules:
  0.0 58.4 jit_solution(3931835676482347763)
XLA Ops:
  0.6 0.1 collective-permute-start
  0.8 0.5 collective-permute-start.1
  1.2 2.4 %collective-permute-start.2 = (bf16[2,2,64,512]{3,2,1,0:T(8,128)(2,1)}, bf16[2,2,64,512]{3,2,1,0:T(8,128)(2,1)S(1)}, u32[]{:S(2)}, u32[]{:S(2)}) collective-permute-start(bf16[2,2,64,512]{3,2,1,0:T(8,128)(2,1)} %bitcast.14), channel_id=1, source_target_pairs={{0,8},{1,9},{2,10},{3,11},{4,12},{5,13},{6,14},{7,15},{8,0},{9,1},... | collective-permute-start | bytes 786440 | tf_op jit(solution)/shard_map/ppermute | solution.py:310
  3.6 2.3 %collective-permute-start.3 = (bf16[2,2,64,512]{3,2,1,0:T(8,128)(2,1)}, bf16[2,2,64,512]{3,2,1,0:T(8,128)(2,1)S(1)}, u32[]{:S(2)}, u32[]{:S(2)}) collective-permute-start(bf16[2,2,64,512]{3,2,1,0:T(8,128)(2,1)} %bitcast.15), channel_id=1, source_target_pairs={{0,16},{1,17},{2,18},{3,19},{4,20},{5,21},{6,22},{7,23},{8,24},{9,... | collective-permute-start | bytes 786440 | tf_op jit(solution)/shard_map/ppermute | solution.py:310
  7.2 0.7 %pad_maximum_fusion.real_valued = f32[18]{0:T(128)S(1)} fusion(f32[16]{0:T(128)} %param.18, f32[2]{0:T(128)} %param.19), kind=kLoop, calls=%fused_computation.1 | loop fusion | flops 18 | bytes 144 | tf_op jit(solution)/shard_map/concatenate | solution.py:324
  7.9 0.7 %pad_add_fusion.whole = s32[17]{0:T(128)S(1)} fusion(s32[1]{0:T(128)S(6)} %copy.19, s32[8]{0:T(128)} %param.15, s32[8]{0:T(128)} %param.14), kind=kLoop, calls=%fused_computation | loop fusion | flops 34 | bytes 136 | tf_op jit(solution)/shard_map/concatenate | solution.py:323
  8.7 0.0 copy-start
  8.7 0.0 collective-permute-done.prop_other
  8.7 0.0 collective-permute-done.1.green_other
  8.7 2.7 %prepare.1 = (bf16[2,2,512,512]{3,2,1,0:T(8,128)(2,1)S(1)}, bf16[2,2,512,512]{3,2,1,0:T(8,128)(2,1)S(1)}, bf16[2,512,512]{2,1,0:T(8,128)(2,1)S(1)}) custom-call(bf16[2,2,512,512]{3,2,1,0:T(8,128)(2,1)} %bitcast.20, bf16[2,2,512,512]{3,2,1,0:T(8,128)(2,1)S(1)} %collective-permute-done.prop_other, bf16[2,2,512,512]{3,2,1,0:T(8,128)(2,1)} %bitcast.22, ...), custom_call_target="tpu_custom_call" | custom-call | flops 2000000000 | bytes 1 | tf_op jit(solution)/shard_map/prepare/pallas_call | solution.py:335
  11.4 0.7 %collective-permute-start.12 = (bf16[2,512,512]{2,1,0:T(8,128)(2,1)S(1)}, bf16[2,512,512]{2,1,0:T(8,128)(2,1)S(1)}, u32[]{:S(2)}, u32[]{:S(2)}) collective-permute-start(bf16[2,512,512]{2,1,0:T(8,128)(2,1)S(1)} %get-tuple-element.22.chip_map), channel_id=1, source_target_pairs={{2,4},{3,5},{4,6},{5,7},{10,12},{11,13},{12,14},{13,15},{18,20},{1... | collective-permute-start | bytes 3145736 | tf_op jit(solution)/shard_map/ppermute | solution.py:320
  12.1 0.7 %collective-permute-start.13 = (bf16[2,512,512]{2,1,0:T(8,128)(2,1)S(1)}, bf16[2,512,512]{2,1,0:T(8,128)(2,1)S(1)}, u32[]{:S(2)}, u32[]{:S(2)}) collective-permute-start(bf16[2,512,512]{2,1,0:T(8,128)(2,1)S(1)} %get-tuple-element.22.chip_map), channel_id=1, source_target_pairs={{2,6},{3,7},{10,14},{11,15},{18,22},{19,23},{26,30},{27,31}} | collective-permute-start | bytes 3145736 | tf_op jit(solution)/shard_map/ppermute | solution.py:320
  12.9 2.7 %collective-permute-done.2.wave_ref = bf16[2,2,64,512]{3,2,1,0:T(8,128)(2,1)S(1)} collective-permute-done((bf16[2,2,64,512]{3,2,1,0:T(8,128)(2,1)}, bf16[2,2,64,512]{3,2,1,0:T(8,128)(2,1)S(1)}, u32[]{:S(2)}, u32[]{:S(2)}) %collective-permute-start.2) | collective-permute-done | bytes 262176 | tf_op jit(solution)/shard_map/ppermute | solution.py:310
  15.6 0.0 collective-permute-done.3.wave_ref
  15.6 2.3 %collective-permute-start.4 = (bf16[2,2,64,512]{3,2,1,0:T(8,128)(2,1)S(1)}, bf16[2,2,64,512]{3,2,1,0:T(8,128)(2,1)S(1)}, u32[]{:S(2)}, u32[]{:S(2)}) collective-permute-start(bf16[2,2,64,512]{3,2,1,0:T(8,128)(2,1)S(1)} %collective-permute-done.3.wave_ref), channel_id=1, source_target_pairs={{0,8},{1,9},{2,10},{3,11},{4,12},{5,13},{6,14},{7,15},{8,0},{9,1},... | collective-permute-start | bytes 786440 | tf_op jit(solution)/shard_map/ppermute | solution.py:310
  17.9 0.0 copy-done
  17.9 0.6 %product.5 = bf16[2,2,64,512]{3,2,1,0:T(8,128)(2,1)S(1)} custom-call(s32[17]{0:T(128)S(1)} %pad_add_fusion.whole, f32[18]{0:T(128)S(1)} %pad_maximum_fusion.real_valued, bf16[2,2,64,512]{3,2,1,0:T(8,128)(2,1)S(1)} %collective-permute-done.3.wave_ref, bf16[2,2,512,512]{3,2,1,0:T(8,128)(2,1)S(1)} %bitcast.10), custom_call_target="tpu_custom_call" | custom-call | flops 2000000000 | bytes 1 | tf_op jit(solution)/shard_map/product/pallas_call | solution.py:19
  18.6 2.8 %collective-permute-start.6 = (bf16[2,2,64,512]{3,2,1,0:T(8,128)(2,1)S(1)}, bf16[2,2,64,512]{3,2,1,0:T(8,128)(2,1)S(1)}, u32[]{:S(2)}, u32[]{:S(2)}) collective-permute-start(bf16[2,2,64,512]{3,2,1,0:T(8,128)(2,1)S(1)} %product.5), channel_id=1, source_target_pairs={{0,16},{1,17},{2,18},{3,19},{4,20},{5,21},{6,22},{7,23},{8,24},{9,... | collective-permute-start | bytes 786440 | tf_op jit(solution)/shard_map/ppermute | solution.py:310
  21.3 0.9 %product.4 = bf16[2,2,64,512]{3,2,1,0:T(8,128)(2,1)S(1)} custom-call(s32[17]{0:T(128)S(1)} %pad_add_fusion.whole, f32[18]{0:T(128)S(1)} %pad_maximum_fusion.real_valued, bf16[2,2,64,512]{3,2,1,0:T(8,128)(2,1)S(1)} %collective-permute-done.2.wave_ref, bf16[2,2,512,512]{3,2,1,0:T(8,128)(2,1)S(1)} %bitcast.11), custom_call_target="tpu_custom_call" | custom-call | flops 2000000000 | bytes 1 | tf_op jit(solution)/shard_map/product/pallas_call | solution.py:19
  22.3 0.0 copy-start.1
  22.3 0.1 collective-permute-start.5
  22.3 0.0 collective-permute-done.4.wave_ref
  22.4 0.9 %product.3 = bf16[2,2,64,512]{3,2,1,0:T(8,128)(2,1)S(1)} custom-call(s32[17]{0:T(128)S(1)} %pad_add_fusion.whole, f32[18]{0:T(128)S(1)} %pad_maximum_fusion.real_valued, bf16[2,2,64,512]{3,2,1,0:T(8,128)(2,1)S(1)} %collective-permute-done.4.wave_ref, bf16[2,2,512,512]{3,2,1,0:T(8,128)(2,1)S(1)} %bitcast.12), custom_call_target="tpu_custom_call" | custom-call | flops 2000000000 | bytes 1 | tf_op jit(solution)/shard_map/product/pallas_call | solution.py:19
  23.3 7.1 %collective-permute-start.7 = (bf16[2,2,64,512]{3,2,1,0:T(8,128)(2,1)S(1)}, bf16[2,2,64,512]{3,2,1,0:T(8,128)(2,1)S(1)}, u32[]{:S(2)}, u32[]{:S(2)}) collective-permute-start(bf16[2,2,64,512]{3,2,1,0:T(8,128)(2,1)S(1)} %product.3), channel_id=1, source_target_pairs={{0,24},{1,25},{2,26},{3,27},{4,28},{5,29},{6,30},{7,31},{8,16},{9,... | collective-permute-start | bytes 786440 | tf_op jit(solution)/shard_map/ppermute | solution.py:310
  30.4 0.0 copy-done.1
  30.4 1.0 %own.1.base = f32[2,2,64,512]{3,2,1,0:T(8,128)S(1)} custom-call(s32[17]{0:T(128)S(1)} %pad_add_fusion.whole, f32[18]{0:T(128)S(1)} %pad_maximum_fusion.real_valued, bf16[2,2,64,512]{3,2,1,0:T(8,128)(2,1)S(1)} %bitcast.16, bf16[2,2,512,512]{3,2,1,0:T(8,128)(2,1)S(1)} %bitcast.13), custom_call_target="tpu_custom_call" | custom-call | flops 2000000000 | bytes 1 | tf_op jit(solution)/shard_map/own/pallas_call | solution.py:19
  31.3 1.3 %fold.1.folded = bf16[2,512,512]{2,1,0:T(8,128)(2,1)S(1)} custom-call(bf16[2,2,512,512]{3,2,1,0:T(8,128)(2,1)S(1)} %get-tuple-element.30.steps, bf16[2,2,512,512]{3,2,1,0:T(8,128)(2,1)S(1)} %get-tuple-element.31.greens), custom_call_target="tpu_custom_call" | custom-call | flops 2000000000 | bytes 1 | tf_op jit(solution)/shard_map/fold/pallas_call | solution.py:19
  32.6 0.0 collective-permute-done.6.refs_1_
  32.6 0.9 %collective-permute-done.5.refs_0_ = bf16[2,2,64,512]{3,2,1,0:T(8,128)(2,1)S(1)} collective-permute-done((bf16[2,2,64,512]{3,2,1,0:T(8,128)(2,1)S(1)}, bf16[2,2,64,512]{3,2,1,0:T(8,128)(2,1)S(1)}, u32[]{:S(2)}, u32[]{:S(2)}) %collective-permute-start.5) | collective-permute-done | bytes 262176 | tf_op jit(solution)/shard_map/ppermute | solution.py:310
  33.5 8.3 %collective-permute-done.7.refs_2_ = bf16[2,2,64,512]{3,2,1,0:T(8,128)(2,1)S(1)} collective-permute-done((bf16[2,2,64,512]{3,2,1,0:T(8,128)(2,1)S(1)}, bf16[2,2,64,512]{3,2,1,0:T(8,128)(2,1)S(1)}, u32[]{:S(2)}, u32[]{:S(2)}) %collective-permute-start.7) | collective-permute-done | bytes 262176 | tf_op jit(solution)/shard_map/ppermute | solution.py:310
  41.7 0.1 term.1
  41.8 2.3 %collective-permute-start.8 = (bf16[2,64,512]{2,1,0:T(8,128)(2,1)S(1)}, bf16[2,64,512]{2,1,0:T(8,128)(2,1)S(1)}, u32[]{:S(2)}, u32[]{:S(2)}) collective-permute-start(bf16[2,64,512]{2,1,0:T(8,128)(2,1)S(1)} %get-tuple-element.29), channel_id=1, source_target_pairs={{0,1},{1,0},{2,3},{3,2},{4,5},{5,4},{6,7},{7,6},{8,9},{9,8},{10,11... | collective-permute-start | bytes 393224 | tf_op jit(solution)/shard_map/ppermute | solution.py:310
  44.2 0.3 own_part.1.part
  44.5 0.7 %collective-permute-done.8.other = bf16[2,64,512]{2,1,0:T(8,128)(2,1)S(1)} collective-permute-done((bf16[2,64,512]{2,1,0:T(8,128)(2,1)S(1)}, bf16[2,64,512]{2,1,0:T(8,128)(2,1)S(1)}, u32[]{:S(2)}, u32[]{:S(2)}) %collective-permute-start.8) | collective-permute-done | bytes 131104 | tf_op jit(solution)/shard_map/ppermute | solution.py:310
  45.2 0.3 chip_wave.1
  45.5 2.2 %collective-permute-start.10 = (bf16[2,64,512]{2,1,0:T(8,128)(2,1)S(1)}, bf16[2,64,512]{2,1,0:T(8,128)(2,1)S(1)}, u32[]{:S(2)}, u32[]{:S(2)}) collective-permute-start(bf16[2,64,512]{2,1,0:T(8,128)(2,1)S(1)} %get-tuple-element.33), channel_id=1, source_target_pairs={{0,6},{1,7},{2,4},{3,5},{4,2},{5,3},{6,0},{7,1},{8,14},{9,15},{10,... | collective-permute-start | bytes 393224 | tf_op jit(solution)/shard_map/ppermute | solution.py:314
  47.7 0.4 collective-permute-start.11
  48.1 0.1 collective-permute-start.9
  48.2 0.3 first.1
  48.5 2.7 %collective-permute-done.10.across_corner = bf16[2,64,512]{2,1,0:T(8,128)(2,1)S(1)} collective-permute-done((bf16[2,64,512]{2,1,0:T(8,128)(2,1)S(1)}, bf16[2,64,512]{2,1,0:T(8,128)(2,1)S(1)}, u32[]{:S(2)}, u32[]{:S(2)}) %collective-permute-start.10) | collective-permute-done | bytes 131104 | tf_op jit(solution)/shard_map/ppermute | solution.py:314
  51.2 3.5 %collective-permute-done.11.straight = bf16[2,64,512]{2,1,0:T(8,128)(2,1)S(1)} collective-permute-done((bf16[2,64,512]{2,1,0:T(8,128)(2,1)S(1)}, bf16[2,64,512]{2,1,0:T(8,128)(2,1)S(1)}, u32[]{:S(2)}, u32[]{:S(2)}) %collective-permute-start.11) | collective-permute-done | bytes 131104 | tf_op jit(solution)/shard_map/ppermute | solution.py:314
  54.7 0.0 collective-permute-done.12.near_map
  54.7 0.0 collective-permute-done.13.far_map
  54.7 0.0 collective-permute-done.9.beside
  54.7 0.5 chain.1
  55.2 0.6 collective-permute-start.14
  55.8 1.3 %green_blocks.2 = (bf16[2,2,64,512]{3,2,1,0:T(8,128)(2,1)}, bf16[2,2,512,512]{3,2,1,0:T(8,128)(2,1)}) custom-call(s32[1]{0:T(128)S(6)} %copy.18.counts, bf16[2,2,64,512]{3,2,1,0:T(8,128)(2,1)S(1)} %bitcast.17, bf16[2,64,512]{2,1,0:T(8,128)(2,1)S(1)} %get-tuple-element.35.chained), custom_call_target="tpu_custom_call" | custom-call | flops 2000000000 | bytes 1 | tf_op jit(solution)/shard_map/green_blocks/pallas_call | solution.py:269
  57.1 0.0 collective-permute-done.14.chained
  57.1 1.3 %green_blocks.3 = (bf16[2,2,64,512]{3,2,1,0:T(8,128)(2,1)}, bf16[2,2,512,512]{3,2,1,0:T(8,128)(2,1)}) custom-call(s32[1]{0:T(128)S(6)} %copy.18.counts, bf16[2,2,64,512]{3,2,1,0:T(8,128)(2,1)S(1)} %bitcast.18, bf16[2,64,512]{2,1,0:T(8,128)(2,1)S(1)} %collective-permute-done.14.chained, ...), custom_call_target="tpu_custom_call", output_to_operand_aliasing={{0}: (3, {}), {1}: (4, {})} | custom-call | flops 2000000000 | bytes 1 | tf_op jit(solution)/shard_map/green_blocks/pallas_call | solution.py:269
  (1 shorter events, 0.0 us)
Async XLA Ops:
  0.6 8.1 %collective-permute-start = (bf16[2,2,512,512]{3,2,1,0:T(8,128)(2,1)}, bf16[2,2,512,512]{3,2,1,0:T(8,128)(2,1)S(1)}, u32[]{:S(2)}, u32[]{:S(2)}) collective-permute-start(bf16[2,2,512,512]{3,2,1,0:T(8,128)(2,1)} %bitcast.19), channel_id=1, source_target_pairs={{0,1},{1,0},{2,3},{3,2},{4,5},{5,4},{6,7},{7,6},{8,9},{9,8},{10,11... | collective-permute-start | bytes 6291464 | tf_op jit(solution)/shard_map/ppermute | solution.py:310
  0.8 7.9 %collective-permute-start.1 = (bf16[2,2,512,512]{3,2,1,0:T(8,128)(2,1)}, bf16[2,2,512,512]{3,2,1,0:T(8,128)(2,1)S(1)}, u32[]{:S(2)}, u32[]{:S(2)}) collective-permute-start(bf16[2,2,512,512]{3,2,1,0:T(8,128)(2,1)} %bitcast.21), channel_id=1, source_target_pairs={{0,1},{1,0},{2,3},{3,2},{4,5},{5,4},{6,7},{7,6},{8,9},{9,8},{10,11... | collective-permute-start | bytes 6291464 | tf_op jit(solution)/shard_map/ppermute | solution.py:310
  1.2 14.4 %collective-permute-start.2 = (bf16[2,2,64,512]{3,2,1,0:T(8,128)(2,1)}, bf16[2,2,64,512]{3,2,1,0:T(8,128)(2,1)S(1)}, u32[]{:S(2)}, u32[]{:S(2)}) collective-permute-start(bf16[2,2,64,512]{3,2,1,0:T(8,128)(2,1)} %bitcast.14), channel_id=1, source_target_pairs={{0,8},{1,9},{2,10},{3,11},{4,12},{5,13},{6,14},{7,15},{8,0},{9,1},... | collective-permute-start | bytes 786440 | tf_op jit(solution)/shard_map/ppermute | solution.py:310
  3.6 12.0 %collective-permute-start.3 = (bf16[2,2,64,512]{3,2,1,0:T(8,128)(2,1)}, bf16[2,2,64,512]{3,2,1,0:T(8,128)(2,1)S(1)}, u32[]{:S(2)}, u32[]{:S(2)}) collective-permute-start(bf16[2,2,64,512]{3,2,1,0:T(8,128)(2,1)} %bitcast.15), channel_id=1, source_target_pairs={{0,16},{1,17},{2,18},{3,19},{4,20},{5,21},{6,22},{7,23},{8,24},{9,... | collective-permute-start | bytes 786440 | tf_op jit(solution)/shard_map/ppermute | solution.py:310
  8.7 9.2 %copy-start = (bf16[2,2,1,512,512]{4,3,2,1,0:T(8,128)(2,1)S(1)}, bf16[2,2,1,512,512]{4,3,2,1,0:T(8,128)(2,1)}, u32[]{:S(2)}) copy-start(bf16[2,2,1,512,512]{4,3,2,1,0:T(8,128)(2,1)} %param.10) | copy-start | bytes 6291460
  11.4 43.3 %collective-permute-start.12 = (bf16[2,512,512]{2,1,0:T(8,128)(2,1)S(1)}, bf16[2,512,512]{2,1,0:T(8,128)(2,1)S(1)}, u32[]{:S(2)}, u32[]{:S(2)}) collective-permute-start(bf16[2,512,512]{2,1,0:T(8,128)(2,1)S(1)} %get-tuple-element.22.chip_map), channel_id=1, source_target_pairs={{2,4},{3,5},{4,6},{5,7},{10,12},{11,13},{12,14},{13,15},{18,20},{1... | collective-permute-start | bytes 3145736 | tf_op jit(solution)/shard_map/ppermute | solution.py:320
  12.1 42.6 %collective-permute-start.13 = (bf16[2,512,512]{2,1,0:T(8,128)(2,1)S(1)}, bf16[2,512,512]{2,1,0:T(8,128)(2,1)S(1)}, u32[]{:S(2)}, u32[]{:S(2)}) collective-permute-start(bf16[2,512,512]{2,1,0:T(8,128)(2,1)S(1)} %get-tuple-element.22.chip_map), channel_id=1, source_target_pairs={{2,6},{3,7},{10,14},{11,15},{18,22},{19,23},{26,30},{27,31}} | collective-permute-start | bytes 3145736 | tf_op jit(solution)/shard_map/ppermute | solution.py:320
  15.6 6.8 %collective-permute-start.4 = (bf16[2,2,64,512]{3,2,1,0:T(8,128)(2,1)S(1)}, bf16[2,2,64,512]{3,2,1,0:T(8,128)(2,1)S(1)}, u32[]{:S(2)}, u32[]{:S(2)}) collective-permute-start(bf16[2,2,64,512]{3,2,1,0:T(8,128)(2,1)S(1)} %collective-permute-done.3.wave_ref), channel_id=1, source_target_pairs={{0,8},{1,9},{2,10},{3,11},{4,12},{5,13},{6,14},{7,15},{8,0},{9,1},... | collective-permute-start | bytes 786440 | tf_op jit(solution)/shard_map/ppermute | solution.py:310
  18.6 14.1 %collective-permute-start.6 = (bf16[2,2,64,512]{3,2,1,0:T(8,128)(2,1)S(1)}, bf16[2,2,64,512]{3,2,1,0:T(8,128)(2,1)S(1)}, u32[]{:S(2)}, u32[]{:S(2)}) collective-permute-start(bf16[2,2,64,512]{3,2,1,0:T(8,128)(2,1)S(1)} %product.5), channel_id=1, source_target_pairs={{0,16},{1,17},{2,18},{3,19},{4,20},{5,21},{6,22},{7,23},{8,24},{9,... | collective-permute-start | bytes 786440 | tf_op jit(solution)/shard_map/ppermute | solution.py:310
  22.3 8.1 %copy-start.1 = (bf16[2,2,1,64,512]{4,3,2,1,0:T(8,128)(2,1)S(1)}, bf16[2,2,1,64,512]{4,3,2,1,0:T(8,128)(2,1)}, u32[]{:S(2)}) copy-start(bf16[2,2,1,64,512]{4,3,2,1,0:T(8,128)(2,1)} %param.13) | copy-start | bytes 786436
  22.3 11.2 %collective-permute-start.5 = (bf16[2,2,64,512]{3,2,1,0:T(8,128)(2,1)S(1)}, bf16[2,2,64,512]{3,2,1,0:T(8,128)(2,1)S(1)}, u32[]{:S(2)}, u32[]{:S(2)}) collective-permute-start(bf16[2,2,64,512]{3,2,1,0:T(8,128)(2,1)S(1)} %product.4), channel_id=1, source_target_pairs={{0,8},{1,9},{2,10},{3,11},{4,12},{5,13},{6,14},{7,15},{8,0},{9,1},... | collective-permute-start | bytes 786440 | tf_op jit(solution)/shard_map/ppermute | solution.py:310
  23.3 18.4 %collective-permute-start.7 = (bf16[2,2,64,512]{3,2,1,0:T(8,128)(2,1)S(1)}, bf16[2,2,64,512]{3,2,1,0:T(8,128)(2,1)S(1)}, u32[]{:S(2)}, u32[]{:S(2)}) collective-permute-start(bf16[2,2,64,512]{3,2,1,0:T(8,128)(2,1)S(1)} %product.3), channel_id=1, source_target_pairs={{0,24},{1,25},{2,26},{3,27},{4,28},{5,29},{6,30},{7,31},{8,16},{9,... | collective-permute-start | bytes 786440 | tf_op jit(solution)/shard_map/ppermute | solution.py:310
  41.8 3.3 %collective-permute-start.8 = (bf16[2,64,512]{2,1,0:T(8,128)(2,1)S(1)}, bf16[2,64,512]{2,1,0:T(8,128)(2,1)S(1)}, u32[]{:S(2)}, u32[]{:S(2)}) collective-permute-start(bf16[2,64,512]{2,1,0:T(8,128)(2,1)S(1)} %get-tuple-element.29), channel_id=1, source_target_pairs={{0,1},{1,0},{2,3},{3,2},{4,5},{5,4},{6,7},{7,6},{8,9},{9,8},{10,11... | collective-permute-start | bytes 393224 | tf_op jit(solution)/shard_map/ppermute | solution.py:310
  45.5 5.7 %collective-permute-start.10 = (bf16[2,64,512]{2,1,0:T(8,128)(2,1)S(1)}, bf16[2,64,512]{2,1,0:T(8,128)(2,1)S(1)}, u32[]{:S(2)}, u32[]{:S(2)}) collective-permute-start(bf16[2,64,512]{2,1,0:T(8,128)(2,1)S(1)} %get-tuple-element.33), channel_id=1, source_target_pairs={{0,6},{1,7},{2,4},{3,5},{4,2},{5,3},{6,0},{7,1},{8,14},{9,15},{10,... | collective-permute-start | bytes 393224 | tf_op jit(solution)/shard_map/ppermute | solution.py:314
  47.7 7.0 %collective-permute-start.11 = (bf16[2,64,512]{2,1,0:T(8,128)(2,1)S(1)}, bf16[2,64,512]{2,1,0:T(8,128)(2,1)S(1)}, u32[]{:S(2)}, u32[]{:S(2)}) collective-permute-start(bf16[2,64,512]{2,1,0:T(8,128)(2,1)S(1)} %get-tuple-element.33), channel_id=1, source_target_pairs={{0,4},{1,5},{2,6},{3,7},{4,0},{5,1},{6,2},{7,3},{8,12},{9,13},{10,... | collective-permute-start | bytes 393224 | tf_op jit(solution)/shard_map/ppermute | solution.py:314
  48.1 6.6 %collective-permute-start.9 = (bf16[2,64,512]{2,1,0:T(8,128)(2,1)S(1)}, bf16[2,64,512]{2,1,0:T(8,128)(2,1)S(1)}, u32[]{:S(2)}, u32[]{:S(2)}) collective-permute-start(bf16[2,64,512]{2,1,0:T(8,128)(2,1)S(1)} %get-tuple-element.33), channel_id=1, source_target_pairs={{0,2},{1,3},{2,0},{3,1},{4,6},{5,7},{6,4},{7,5},{8,10},{9,11},{10,... | collective-permute-start | bytes 393224 | tf_op jit(solution)/shard_map/ppermute | solution.py:314
  55.2 1.9 %collective-permute-start.14 = (bf16[2,64,512]{2,1,0:T(8,128)(2,1)S(1)}, bf16[2,64,512]{2,1,0:T(8,128)(2,1)S(1)}, u32[]{:S(2)}, u32[]{:S(2)}) collective-permute-start(bf16[2,64,512]{2,1,0:T(8,128)(2,1)S(1)} %get-tuple-element.34), channel_id=1, source_target_pairs={{0,1},{1,0},{2,3},{3,2},{4,5},{5,4},{6,7},{7,6},{8,9},{9,8},{10,11... | collective-permute-start | bytes 393224 | tf_op jit(solution)/shard_map/ppermute | solution.py:310
